TPU v7x, 128 devices: a whole 4x4x4 slice. The times are simulated.
128 devices in a mesh: ctx: 16 (over z, x), tp: 8 (over y, core).
Axes of the slice: x: 4, y: 4, z: 4, core: 2. Of those that a mesh axis runs over, the one named last changes fastest.
Arguments:
- x_in: bfloat16 [8192, 8192], P('ctx', 'tp'), may hold values from -6 to 6
- bc_in: bfloat16 [8192, 256], P('ctx'), may hold values from -6 to 6
- z_in: bfloat16 [8192, 8192], P('ctx', 'tp'), may hold values from -6 to 6
- codes: int32 [8192, 64], P('ctx', 'tp'), may hold values from 0 to 63
- head_rate: float32 [64], P('tp'), may hold values from 0.25 to 1
- conv_x: float32 [4, 8192], P(None, 'tp'), may hold values from -3 to 3
- conv_bc: float32 [4, 256], replicated, may hold values from -3 to 3
- bias_x: float32 [8192], P('tp'), may hold values from -2 to 2
- bias_bc: float32 [256], replicated, may hold values from -2 to 2
- skip: float32 [64], P('tp'), may hold values from 0.5 to 1.5
- norm_gain: float32 [8192], P('tp'), may hold values from 0.5 to 1.5
- w_out: bfloat16 [8192, 8192], P('tp'), may hold values from -0.09375 to 0.09375
Outputs:
- mixed: bfloat16 [8192, 8192], P('ctx', 'tp')
All inputs are finite; a program needn't handle non-finite values.
Results may differ from a plain program's by a relative error of at most 0.019.
Values may be sent and summed in bfloat16 or wider, within the bound.
No kernel may reach another device: no remote copies, remote signals or barrier semaphores. Data moves between devices by JAX's collectives and lax.ppermute only.
A program may use at most 128 MiB of HBM per device.

v0:
```python
import math

import jax
import jax.numpy as jnp
from jax import lax
from jax.sharding import PartitionSpec as P


def shifted(value, axis, steps):
    count = lax.axis_size(axis)
    first, last = (max(0, -steps), min(count, count - steps))
    return lax.ppermute(value, axis, [(source, source + steps) for source in range(first, last)])


def carried_in(shard, axis, join, neutral):
    place = lax.axis_index(axis)
    gathered = jax.tree.map(
        lambda a, kind: lax.all_gather(a.astype(kind), axis), shard, (jnp.bfloat16, jnp.bfloat16)
    )
    state = jax.tree.map(lambda a, e: jnp.zeros_like(a) + jnp.asarray(e, a.dtype), shard, neutral)

    def one(lap, state):
        return join(
            state,
            jax.tree.map(
                lambda a, own: lax.dynamic_index_in_dim(a, lap, 0, False).astype(own.dtype),
                gathered,
                shard,
            ),
        )

    return lax.fori_loop(0, place, one, state)


def causal_conv(signal, rim_rows, weight, shift_bias):
    tok_count = signal.shape[0]
    extended = jnp.concatenate([rim_rows, signal], axis=0).astype(jnp.float32)
    total = shift_bias[None, :]
    for k in range(4):
        total = total + weight[k][None, :] * extended[k : k + tok_count]
    return jax.nn.silu(total).astype(jnp.bfloat16)


def body(
    x_in, bc_in, z_in, codes, head_rate, conv_x, conv_bc, bias_x, bias_bc, skip, norm_gain, w_out
):
    wide = lax.Precision.HIGH
    tok_rows = x_in.shape[0]
    head_count = skip.shape[0]
    head_width = x_in.shape[1] // head_count
    state_dim = bc_in.shape[1] // 2
    seq_total = tok_rows * lax.axis_size("ctx")
    rim_x, rim_bc = shifted((x_in[tok_rows - 3 :], bc_in[tok_rows - 3 :]), "ctx", 1)
    xc = causal_conv(x_in, rim_x, conv_x, bias_x).reshape(tok_rows, head_count, head_width)
    bcc = causal_conv(bc_in, rim_bc, conv_bc, bias_bc)
    in_maps = bcc[:, :state_dim]
    out_maps = bcc[:, state_dim:]
    log_decay = -12.288 / seq_total * head_rate[None, :] * codes.astype(jnp.float32) / 63.0
    local_cum = jnp.cumsum(log_decay, axis=0)
    block_len = math.gcd(tok_rows, 128)
    causal = jnp.tril(jnp.ones((block_len, block_len), dtype=bool))[:, :, None]
    running_state = jnp.zeros((head_count, state_dim, head_width), jnp.float32)
    block_start = jnp.zeros((head_count,), jnp.float32)
    outputs = []
    for index in range(tok_rows // block_len):
        lower = index * block_len
        x_block = xc[lower : lower + block_len]
        in_block = in_maps[lower : lower + block_len]
        out_block = out_maps[lower : lower + block_len]
        cum_block = local_cum[lower : lower + block_len]
        scores = jnp.dot(out_block, in_block.T, preferred_element_type=jnp.float32)
        log_gap = cum_block[:, None, :] - cum_block[None, :, :]
        weights = (
            jnp.where(causal, jnp.exp(jnp.where(causal, log_gap, 0.0)), 0.0) * scores[:, :, None]
        )
        weights = weights.astype(jnp.bfloat16)
        inside = jnp.einsum("tsh,shp->thp", weights, x_block, preferred_element_type=jnp.float32)
        carried = jnp.einsum(
            "tn,hnp->thp", out_block.astype(jnp.float32), running_state, precision=wide
        )
        carried = carried * jnp.exp(cum_block - block_start[None, :])[:, :, None]
        outputs.append(inside + carried)
        block_end = cum_block[-1]
        factors = jnp.exp(block_end[None, :] - cum_block)
        sent = (x_block.astype(jnp.float32) * factors[:, :, None]).astype(jnp.bfloat16)
        added = jnp.einsum("sn,shp->hnp", in_block, sent, preferred_element_type=jnp.float32)
        running_state = jnp.exp(block_end - block_start)[:, None, None] * running_state + added
        block_start = block_end
    scanned = jnp.concatenate(outputs, axis=0)
    decay_total = local_cum[-1]
    empty_state = jnp.zeros((head_count, state_dim, head_width), jnp.float32)

    def combine_pair(earlier, latter):
        return (earlier[0] + latter[0], jnp.exp(latter[0])[:, None, None] * earlier[1] + latter[1])

    identity = (jnp.zeros((head_count,), jnp.float32), empty_state)
    _, incoming = carried_in((decay_total, running_state), "ctx", combine_pair, identity)
    from_before = jnp.einsum("tn,hnp->thp", out_maps.astype(jnp.float32), incoming, precision=wide)
    from_before = from_before * jnp.exp(local_cum)[:, :, None]
    ssd_scale = 1.0 / math.sqrt(state_dim * seq_total)
    ssd = (scanned + from_before) * ssd_scale + skip[None, :, None] * xc.astype(jnp.float32)
    gated_out = ssd * jax.nn.silu(
        z_in.astype(jnp.float32).reshape(tok_rows, head_count, head_width)
    )
    mean_square = jnp.mean(gated_out * gated_out, axis=-1, keepdims=True)
    normed = (
        gated_out * lax.rsqrt(mean_square + 1e-05) * norm_gain.reshape(head_count, head_width)[None]
    )
    normed = normed.astype(jnp.bfloat16).reshape(tok_rows, head_count * head_width)
    partial_value = jnp.dot(normed, w_out, preferred_element_type=jnp.float32)
    summed = lax.psum_scatter(
        partial_value.astype(jnp.bfloat16), "tp", scatter_dimension=1, tiled=True
    )
    return summed


def solution(mesh):
    in_specs = (
        P("ctx", "tp"),
        P("ctx", None),
        P("ctx", "tp"),
        P("ctx", "tp"),
        P("tp"),
        P(None, "tp"),
        P(),
        P("tp"),
        P(),
        P("tp"),
        P("tp"),
        P("tp", None),
    )
    out_specs = P("ctx", "tp")
    return jax.shard_map(body, mesh=mesh, in_specs=in_specs, out_specs=out_specs, check_vma=False)
```

profile of v0, /device:TPU:0, one launch (start us, length us, event | category | flops | bytes accessed | tf_op | source)
XLA Modules:
  0.0 194.7 jit_solution(14121074269895709477)
XLA Ops:
  7.3 3.5 %collective-permute-start.1 = (bf16[3,256]{1,0:T(4,128)(2,1)S(1)}, bf16[3,256]{1,0:T(4,128)(2,1)S(1)}, u32[]{:S(2)}, u32[]{:S(2)}) collective-permute-start(bf16[3,256]{1,0:T(4,128)(2,1)S(1)} %slice.164), channel_id=1, source_target_pairs={{0,8},{8,16},{16,24},{24,32},{32,40},{40,48},{48,56},{56,64},{64,7... | collective-permute-start | bytes 4616 | tf_op jit(solution)/shard_map/ppermute | solution.py:12
  11.7 3.4 %collective-permute-start = (bf16[3,1024]{0,1:T(8,128)(2,1)S(1)}, bf16[3,1024]{0,1:T(8,128)(2,1)S(1)}, u32[]{:S(2)}, u32[]{:S(2)}) collective-permute-start(bf16[3,1024]{0,1:T(8,128)(2,1)S(1)} %copy.80), channel_id=1, source_target_pairs={{0,8},{8,16},{16,24},{24,32},{32,40},{40,48},{48,56},{56,64},{64,7... | collective-permute-start | bytes 18440 | tf_op jit(solution)/shard_map/ppermute | solution.py:12
  16.6 1.1 reduce-window.6
  19.7 0.9 fusion.84
  21.2 1.5 copy.81
  23.9 2.7 %multiply_convert_fusion.1 = bf16[512,1024]{0,1:T(8,128)(2,1)S(1)} fusion(f32[515,1024]{0,1:T(8,128)S(1)} %maximum_convert_fusion, f32[1024]{0:T(1024)S(1)} %bitcast.128, f32[1024]{0:T(1024)S(1)} %bitcast.129, f32[1024]{0:T(1024)S(1)} %bitcast.127, f32[1024]{0:T(1024)S(1)} %bitcast.126, f32[1024]{0:T(1024)S(1)} %copy-done.16), kind=kLoop, calls=%fused_computation.17 | loop fusion | flops 6815744 | bytes 9457664 | tf_op jit(solution)/shard_map/convert_element_type | solution.py:41
  28.0 0.9 fusion.15
  28.9 1.8 copy.90
  30.9 21.5 %all-gather.1 = bf16[16,1,8]{2,1,0:T(2,128)(2,1)S(1)} all-gather(bf16[1,1,8]{2,1,0:T(2,128)(2,1)S(1)} %bitcast.136), channel_id=1, replica_groups=mesh['ctx'=16,'tp'=8] {'ctx'}, dimensions={0}, use_global_device_ids=true | all-gather | bytes 272 | tf_op jit(solution)/shard_map/all_gather | solution.py:18
  53.1 2.3 %copy.95 = bf16[512,1024]{0,1:T(8,128)(2,1)} copy(bf16[512,1024]{1,0:T(8,128)(2,1)} %param.16) | data formatting | bytes 2097152 | tf_op args[2]
  55.4 2.6 %copy.97 = f32[512,8,128]{2,0,1:T(8,128)} copy(bf16[512,8,128]{0,2,1:T(8,128)(2,1)} %bitcast.114) | data formatting | bytes 3145728 | tf_op jit(solution)/shard_map/reshape | solution.py:103
  59.8 1.7 convolution_multiply_fusion.3
  61.5 1.6 copy.94
  63.2 1.1 convolution_multiply_fusion.1
  64.3 1.0 convolution_multiply_fusion
  65.7 1.2 fusion.13
  66.9 1.1 fusion.14
  68.0 1.2 fusion.12
  69.2 1.1 fusion.11
  70.3 14.3 %all-gather.4.cloned.1.call-done = bf16[128,128,128]{2,1,0:T(8,128)(2,1)} async-done(((bf16[8,128,128]{2,1,0:T(8,128)(2,1)}), bf16[128,128,128]{2,1,0:T(8,128)(2,1)}) %all-gather.4.cloned.1.call-update) | async-done | bytes 4194320 | tf_op jit(solution)/shard_map/all_gather | solution.py:18
  85.7 1.9 copy.93
  87.7 3.8 %multiply_reduce_fusion = (f32[512,8]{0,1:T(8,128)S(1)}, f32[512,8,128]{2,0,1:T(8,128)S(1)}) fusion(f32[512,8,128]{2,0,1:T(8,128)} %copy.97, f32[512,8,128]{2,0,1:T(8,128)} %copy.94, f32[8]{0:T(128)S(1)} %copy-done.19, f32[512,8,128]{2,0,1:T(8,128)} %copy.93, f32[512,8]{0,1:T(8,128)S(1)} %copy-done.10, f32[128,8,128]{2,0,1:T(8,128)S(1)} %copy-done.6, ...), kind=kLoop, calls=%fused_computation.16 | loop fusion | flops 7860224 | bytes 10518560 | tf_op jit(solution)/shard_map/reduce_sum | solution.py:105
  92.7 17.0 %convolution_convert_fusion = bf16[512,8192]{1,0:T(8,128)(2,1)} fusion(bf16[512,1024]{0,1:T(8,128)(2,1)S(1)} %bitcast.124, bf16[1024,8192]{1,0:T(8,128)(2,1)} %param.25), kind=kOutput, calls=%fused_computation.2 | convolution fusion | flops 8594128896 | bytes 26214400 | tf_op jit(solution)/shard_map/dot_general | solution.py:110
  109.7 78.1 %reduce-scatter.2.cloned.1.call-done = bf16[512,1024]{1,0:T(8,128)(2,1)} async-done(((bf16[512,8192]{1,0:T(8,128)(2,1)}), bf16[512,1024]{1,0:T(8,128)(2,1)}) %reduce-scatter.2.cloned.1.call-update) | async-done | bytes 1048592 | tf_op jit(solution)/shard_map/reduce_scatter | solution.py:111
  (81 shorter events, 13.7 us)
Async XLA Ops:
  6.5 16.2 %copy-start.7 = (bf16[512,256]{1,0:T(8,128)(2,1)S(1)}, bf16[512,256]{1,0:T(8,128)(2,1)}, u32[]{:S(2)}) copy-start(bf16[512,256]{1,0:T(8,128)(2,1)} %param.15) | copy-start | bytes 786436
  6.5 16.3 %copy-start.18 = (f32[256]{0:T(256)S(1)}, f32[256]{0:T(256)}, u32[]{:S(2)}) copy-start(f32[256]{0:T(256)} %param.22) | copy-start | bytes 3076
  6.5 78.0 %all-gather.4.cloned.1.call-start = ((), (), s32[]{:S(2)}) async-start(), calls=%async_computation.2 | async-start | bytes 4456448 | tf_op jit(solution)/shard_map/all_gather | solution.py:18
  7.3 15.4 %collective-permute-start.1 = (bf16[3,256]{1,0:T(4,128)(2,1)S(1)}, bf16[3,256]{1,0:T(4,128)(2,1)S(1)}, u32[]{:S(2)}, u32[]{:S(2)}) collective-permute-start(bf16[3,256]{1,0:T(4,128)(2,1)S(1)} %slice.164), channel_id=1, source_target_pairs={{0,8},{8,16},{16,24},{24,32},{32,40},{40,48},{48,56},{56,64},{64,7... | collective-permute-start | bytes 4616 | tf_op jit(solution)/shard_map/ppermute | solution.py:12
  11.7 11.5 %collective-permute-start = (bf16[3,1024]{0,1:T(8,128)(2,1)S(1)}, bf16[3,1024]{0,1:T(8,128)(2,1)S(1)}, u32[]{:S(2)}, u32[]{:S(2)}) collective-permute-start(bf16[3,1024]{0,1:T(8,128)(2,1)S(1)} %copy.80), channel_id=1, source_target_pairs={{0,8},{8,16},{16,24},{24,32},{32,40},{40,48},{48,56},{56,64},{64,7... | collective-permute-start | bytes 18440 | tf_op jit(solution)/shard_map/ppermute | solution.py:12
  23.2 0.7 copy-start.16
  26.8 0.7 copy-start
  26.8 1.1 copy-start.2
  30.7 157.2 %reduce-scatter.2.cloned.1.call-start = ((), (), s32[]{:S(2)}) async-start(), calls=%async_computation.1 | async-start | bytes 9437184 | tf_op jit(solution)/shard_map/reduce_scatter | solution.py:111
  63.2 2.1 %copy-start.15 = (f32[128,8]{0,1:T(8,128)S(1)}, f32[128,8]{0,1:T(8,128)}, u32[]{:S(2)}) copy-start(f32[128,8]{0,1:T(8,128)} %get-tuple-element.92) | copy-start | bytes 12292
  63.2 2.4 %copy-start.9 = (f32[128,128]{1,0:T(8,128)S(1)}, f32[128,128]{1,0:T(8,128)}, u32[]{:S(2)}) copy-start(f32[128,128]{1,0:T(8,128)} %fusion.61) | copy-start | bytes 196612
  63.2 2.5 %copy-start.14 = (f32[128,8]{0,1:T(8,128)S(1)}, f32[128,8]{0,1:T(8,128)}, u32[]{:S(2)}) copy-start(f32[128,8]{0,1:T(8,128)} %get-tuple-element.110) | copy-start | bytes 12292
  63.2 3.7 %copy-start.3 = (bf16[128,1024]{0,1:T(8,128)(2,1)S(1)}, bf16[128,1024]{0,1:T(8,128)(2,1)}, u32[]{:S(2)}) copy-start(bf16[128,1024]{0,1:T(8,128)(2,1)} %copy-done.2) | copy-start | bytes 786436
  63.2 3.7 %copy-start.8 = (f32[128,128]{1,0:T(8,128)S(1)}, f32[128,128]{1,0:T(8,128)}, u32[]{:S(2)}) copy-start(f32[128,128]{1,0:T(8,128)} %fusion.56) | copy-start | bytes 196612
  63.2 3.7 %copy-start.13 = (f32[128,8]{0,1:T(8,128)S(1)}, f32[128,8]{0,1:T(8,128)}, u32[]{:S(2)}) copy-start(f32[128,8]{0,1:T(8,128)} %get-tuple-element.109) | copy-start | bytes 12292
  65.3 2.7 %copy-start.12 = (f32[128,8]{0,1:T(8,128)S(1)}, f32[128,8]{0,1:T(8,128)}, u32[]{:S(2)}) copy-start(f32[128,8]{0,1:T(8,128)} %get-tuple-element.101) | copy-start | bytes 12292
  65.6 3.5 %copy-start.1 = (bf16[128,1024]{0,1:T(8,128)(2,1)S(1)}, bf16[128,1024]{0,1:T(8,128)(2,1)}, u32[]{:S(2)}) copy-start(bf16[128,1024]{0,1:T(8,128)(2,1)} %copy-done) | copy-start | bytes 786436
  65.7 3.5 %copy-start.4 = (f32[128,8,128]{2,0,1:T(8,128)S(1)}, f32[128,8,128]{2,0,1:T(8,128)}, u32[]{:S(2)}) copy-start(f32[128,8,128]{2,0,1:T(8,128)} %convolution_multiply_fusion.3) | copy-start | bytes 1572868
  65.7 3.5 %copy-start.11 = (f32[128,8]{0,1:T(8,128)S(1)}, f32[128,8]{0,1:T(8,128)}, u32[]{:S(2)}) copy-start(f32[128,8]{0,1:T(8,128)} %get-tuple-element.103) | copy-start | bytes 12292
  85.7 1.9 copy-start.5
  85.7 1.9 copy-start.6
  85.7 1.9 copy-start.10
  85.7 1.9 copy-start.19
  87.6 3.8 %copy-start.17 = (f32[1024]{0:T(1024)S(1)}, f32[1024]{0:T(1024)}, u32[]{:S(2)}) copy-start(f32[1024]{0:T(1024)} %param.24) | copy-start | bytes 12292
Sparse Core Ops, SparseCore 0:
  30.8 53.6 all-gather.3
  109.9 77.9 reduce-scatter.1
where the time goes:
time: 196 us; the launch traced here: 195 us
  waiting for transfers between devices  92.4 us (47%)
  matrix products  29.8 us (15%)
  blocking collectives  21.5 us (11%)
  local copies, waits for them, and re-layouts  17.8 us (9%)
  between operations  13.8 us (7%)
  other arithmetic  12.2 us (6%)
  starting transfers between devices  6.93 us (4%)
    reduce_scatter x1, waiting for transfers between devices, body(): lax.psum_scatter(partial_value.astype(jnp.bfloat16), 'tp', scatter_dimens...  78.1 us
    all_gather x1, blocking collectives, carried_in(): lax.all_gather(a.astype(kind), axis)  21.5 us
    dot_general x1, matrix products, body(): partial_value = jnp.dot(normed, w_out, preferred_element_type=jnp.float32)  17 us
    all_gather x1, waiting for transfers between devices, carried_in(): lax.all_gather(a.astype(kind), axis)  14.3 us
    ppermute x2, starting transfers between devices, shifted(): lax.ppermute(value, axis, [(source, source + steps) for source in range(f...  6.88 us
    dot_general x4, matrix products, body(): jnp.einsum('tsh,shp->thp', weights, x_block, preferred_element_type=jnp.f...  4.6 us
    unnamed x42, local copies, waits for them, and re-layouts  4.44 us
    dot_general x4, matrix products, body(): jnp.einsum('tn,hnp->thp', out_block.astype(jnp.float32), running_state, p...  4.07 us
  transfers between devices with their start and end apart: 4, of which 2 were waited for; matrix products, arithmetic and copies ran while one was open for 14% of the time, Pallas kernels for 0%

commit v1 on v0

v1 whole, which is shorter than its diff:
```python
import functools

import jax
import jax.numpy as jnp
from jax import lax
from jax.experimental import pallas as pl
from jax.experimental.pallas import tpu as pltpu
from jax.sharding import PartitionSpec as P

BF = jnp.bfloat16
F32 = jnp.float32
TOK = 512
WID = 1024
HEADS = 8
HW = 128
ST = 128
CTX = 16
CB = 256
NB = WID // CB
HB = CB // HW
SEQ = TOK * CTX
DECAY = 12.288 / SEQ / 63.0
SCALE = 1.0 / (ST * SEQ) ** 0.5
ROWS = 64


def silu(v):
    half = 0.5 * v
    return half + half * jnp.tanh(half)


def mm(a, b):
    return jnp.dot(a, b, preferred_element_type=F32)


def lanes(ref, first, count, factor):
    rows = [jnp.full((1, HW), ref[first + k] * factor, F32) for k in range(count)]
    return jnp.concatenate(rows, axis=1)


def fill_tri(tri):
    for r in range(0, TOK, HW):
        row = lax.broadcasted_iota(jnp.int32, (HW, TOK), 0) + r
        col = lax.broadcasted_iota(jnp.int32, (HW, TOK), 1)
        tri[r : r + HW, :] = jnp.where(row >= col, 1.0, 0.0).astype(BF)


def code_sums(codes_ref, tri, block):
    head = lax.broadcasted_iota(jnp.int32, (HEADS, CB), 0)
    lane = lax.broadcasted_iota(jnp.int32, (HEADS, CB), 1) // HW + HB * block
    spread = jnp.where(head == lane, 1.0, 0.0).astype(BF)
    wide = mm(codes_ref[...].astype(F32).astype(BF), spread).astype(BF)
    return mm(tri[...], wide)


def conv_rows(xe, w_ref, bias_ref, r):
    total = bias_ref[...]
    for k in range(4):
        total = total + w_ref[k : k + 1, :] * xe[5 + k + r : 5 + k + r + ROWS, :]
    return silu(total)


def scan_in_body(
    rate_ref, x_ref, rim_ref, bc_ref, rimbc_ref, codes_ref, cx_ref, bx_ref, cbc_ref, bbc_ref,
    xc_ref, xt_ref, b_ref, c_ref, msg_ref, xe, tri, bt, sums,
):
    block = pl.program_id(0)

    @pl.when(block == 0)
    def _():
        fill_tri(tri)
        xe[0:8, :] = rimbc_ref[...].astype(F32)
        xe[8 : 8 + TOK, :] = bc_ref[...].astype(F32)
        for r in range(0, TOK, ROWS):
            out = conv_rows(xe, cbc_ref, bbc_ref, r)
            b_ref[r : r + ROWS, :] = out[:, :ST].astype(BF)
            c_ref[r : r + ROWS, :] = out[:, ST:].astype(BF)
        bt[...] = b_ref[...].astype(F32).T.astype(BF)

    xe[0:8, :] = rim_ref[...].astype(F32)
    xe[8 : 8 + TOK, :] = x_ref[...].astype(F32)
    sums[...] = code_sums(codes_ref, tri, block)
    rate = lanes(rate_ref, block * HB, HB, DECAY)
    for r in range(0, TOK, ROWS):
        xc = conv_rows(xe, cx_ref, bx_ref, r).astype(BF)
        xc_ref[r : r + ROWS, :] = xc
        xt_ref[r : r + ROWS, :] = (xc.astype(F32) * jnp.exp(rate * sums[r : r + ROWS, :])).astype(BF)
    state = mm(bt[...], xt_ref[...])
    total = sums[TOK - 1 : TOK, :]
    high = jnp.floor(total * (1.0 / 256.0))
    low = total - 256.0 * high
    row = lax.broadcasted_iota(jnp.int32, (8, CB), 0)
    extra = jnp.where(row == 0, high, jnp.where(row == 1, low, 0.0))
    for j in range(CTX):
        part = jnp.concatenate([state[8 * j : 8 * j + 8, :], extra], axis=0)
        msg_ref[j] = part.astype(BF)


def local_body(
    rate_ref, skip_ref, xt_ref, xc_ref, z_ref, codes_ref, b_ref, c_ref, a1_ref, a2_ref, tri, gram, sums, prod,
):
    block = pl.program_id(0)

    @pl.when(block == 0)
    def _():
        fill_tri(tri)
        for r in range(0, TOK, HW):
            part = lax.dot_general(
                c_ref[r : r + HW, :], b_ref[...], (((1,), (1,)), ((), ())), preferred_element_type=F32
            )
            row = lax.broadcasted_iota(jnp.int32, (HW, TOK), 0) + r
            col = lax.broadcasted_iota(jnp.int32, (HW, TOK), 1)
            gram[r : r + HW, :] = jnp.where(row >= col, part, 0.0).astype(BF)

    sums[...] = code_sums(codes_ref, tri, block)
    prod[...] = mm(gram[...], xt_ref[...])
    rate = lanes(rate_ref, block * HB, HB, -DECAY)
    skip = lanes(skip_ref, block * HB, HB, 1.0)
    for r in range(0, TOK, ROWS):
        gate = silu(z_ref[r : r + ROWS, :].astype(F32))
        fade = SCALE * jnp.exp(rate * sums[r : r + ROWS, :])
        xc = xc_ref[r : r + ROWS, :].astype(F32)
        a1_ref[r : r + ROWS, :] = (prod[r : r + ROWS, :] * fade + skip * xc) * gate
        a2_ref[r : r + ROWS, :] = fade * gate


def prefix_body(rate_ref, r_ref, q_ref):
    rate = lanes(rate_ref, 0, HEADS, -DECAY)
    state = jnp.zeros((8, WID), F32)
    for c in range(CTX):
        q_ref[c] = state.astype(BF)
        got = r_ref[c].astype(F32)
        total = 256.0 * got[8:9, :] + got[9:10, :]
        state = jnp.exp(rate * total) * (state + got[0:8, :])


def norm_body(q_ref, a1_ref, a2_ref, c_ref, gain_ref, n_ref, prod):
    state = q_ref[...].astype(F32).reshape(ST, CB).astype(BF)
    prod[...] = mm(c_ref[...], state)
    for r in range(0, TOK, ROWS):
        for h in range(0, CB, HW):
            rs, hs = slice(r, r + ROWS), slice(h, h + HW)
            gated = a1_ref[rs, hs] + a2_ref[rs, hs] * prod[rs, hs]
            power = jnp.mean(gated * gated, axis=-1, keepdims=True)
            n_ref[rs, hs] = (gated * lax.rsqrt(power + 1e-05) * gain_ref[:, hs]).astype(BF)


def pick_body(index_ref, w_ref, gate_ref, o_ref):
    o_ref[0] = w_ref[...]


def proj_body(adds, index_ref, own_ref, sib_ref, w_ref, ws_ref, *refs):
    step = pl.program_id(0)
    outs = refs[-2:]
    value = mm(own_ref[...], w_ref[...]) + mm(sib_ref[...], ws_ref[0])
    for k in range(2):

        @pl.when(step == k)
        def _():
            total = value
            for a in range(adds):
                total = total + refs[2 * a + k][...].astype(F32)
            outs[k][...] = total.astype(outs[k].dtype)


def final_body(m0_ref, m1_ref, a_ref, b_ref, o_ref):
    half = m0_ref.shape[1]
    o_ref[:, :half] = (m0_ref[...] + a_ref[...].astype(F32)).astype(BF)
    o_ref[:, half:] = (m1_ref[...] + b_ref[...].astype(F32)).astype(BF)


def params(**kw):
    return pltpu.CompilerParams(dimension_semantics=("arbitrary",), vmem_limit_bytes=48 << 20, **kw)


SMEM = pl.BlockSpec(memory_space=pltpu.SMEM)


def whole(*shape):
    return pl.BlockSpec(shape, lambda i: (0,) * len(shape))


def cols(rows):
    return pl.BlockSpec((rows, CB), lambda i: (0, i))


def project(index, own, sib, w, ws, addends, kind):
    half = WID // 2
    flat = [a for pair in addends for a in pair]
    const = pl.BlockSpec((TOK, half), lambda i, ix: (0, 0))
    full = pl.BlockSpec((TOK, WID), lambda i, ix: (0, 0))
    return pl.pallas_call(
        functools.partial(proj_body, len(addends)),
        out_shape=[jax.ShapeDtypeStruct((TOK, half), kind)] * 2,
        grid_spec=pltpu.PrefetchScalarGridSpec(
            num_scalar_prefetch=1,
            grid=(2,),
            in_specs=[
                full,
                full,
                pl.BlockSpec((WID, half), lambda i, ix: (0, ix[i])),
                pl.BlockSpec((1, WID, half), lambda i, ix: (ix[2 + i], 0, ix[4 + i])),
            ]
            + [const] * len(flat),
            out_specs=[const, const],
        ),
        compiler_params=params(),
        name="project",
    )(index, own, sib, w, ws, *flat)


def body(
    x_in, bc_in, z_in, codes, head_rate, conv_x, conv_bc, bias_x, bias_bc, skip, norm_gain, w_out
):
    place = lax.axis_index("tp")
    row, core = place // 2, place % 2
    rim = jnp.concatenate([x_in[TOK - 8 :], bc_in[TOK - 8 :]], axis=1)
    rim = lax.ppermute(rim, "ctx", [(s, s + 1) for s in range(CTX - 1)])

    sd = jax.ShapeDtypeStruct
    xc, xt, b_map, c_map, msg = pl.pallas_call(
        scan_in_body,
        grid=(NB,),
        in_specs=[
            SMEM, cols(TOK), cols(8), whole(TOK, 2 * ST),
            pl.BlockSpec((8, CB), lambda i: (0, NB)), whole(TOK, HEADS), cols(4), cols(1),
            whole(4, 2 * ST), whole(1, 2 * ST),
        ],
        out_specs=[
            cols(TOK), cols(TOK), whole(TOK, ST), whole(TOK, ST),
            pl.BlockSpec((CTX, 16, CB), lambda i: (0, 0, i)),
        ],
        out_shape=[
            sd((TOK, WID), BF), sd((TOK, WID), BF), sd((TOK, ST), BF), sd((TOK, ST), BF),
            sd((CTX, 16, WID), BF),
        ],
        scratch_shapes=[
            pltpu.VMEM((TOK + 8, CB), F32), pltpu.VMEM((TOK, TOK), BF), pltpu.VMEM((ST, TOK), BF),
            pltpu.VMEM((TOK, CB), F32),
        ],
        compiler_params=params(),
        name="scan_in",
    )(
        head_rate, x_in, rim, bc_in, rim, codes, conv_x, bias_x[None, :], conv_bc, bias_bc[None, :]
    )

    got = lax.all_to_all(msg, "ctx", 0, 0, tiled=True)

    order = jnp.stack([2 * r + 1 - core for r in range(4)]).astype(jnp.int32)
    picked = pl.pallas_call(
        pick_body,
        out_shape=sd((4, WID, WID), BF),
        grid_spec=pltpu.PrefetchScalarGridSpec(
            num_scalar_prefetch=1,
            grid=(4,),
            in_specs=[
                pl.BlockSpec((WID, WID), lambda i, ix: (0, ix[i])),
                pl.BlockSpec(memory_space=pl.ANY),
            ],
            out_specs=pl.BlockSpec((1, WID, WID), lambda i, ix: (i, 0, 0)),
        ),
        compiler_params=params(),
        name="pick",
    )(order, w_out, c_map)
    swap = [(s, s ^ 1) for s in range(8)]
    w_sib = lax.ppermute(picked, "tp", swap)

    a1, a2 = pl.pallas_call(
        local_body,
        grid=(NB,),
        in_specs=[
            SMEM, SMEM, cols(TOK), cols(TOK), cols(TOK), whole(TOK, HEADS), whole(TOK, ST),
            whole(TOK, ST),
        ],
        out_specs=[cols(TOK), cols(TOK)],
        out_shape=[sd((TOK, WID), F32)] * 2,
        scratch_shapes=[
            pltpu.VMEM((TOK, TOK), BF), pltpu.VMEM((TOK, TOK), BF), pltpu.VMEM((TOK, CB), F32),
            pltpu.VMEM((TOK, CB), F32),
        ],
        compiler_params=params(),
        name="local",
    )(head_rate, skip, xt, xc, z_in, codes, b_map, c_map)

    prefix = pl.pallas_call(
        prefix_body,
        in_specs=[SMEM, pl.BlockSpec(memory_space=pltpu.VMEM)],
        out_specs=pl.BlockSpec(memory_space=pltpu.VMEM),
        out_shape=sd((CTX, 8, WID), BF),
        compiler_params=pltpu.CompilerParams(vmem_limit_bytes=48 << 20),
        name="prefix",
    )(head_rate, got)
    incoming = lax.all_to_all(prefix, "ctx", 0, 0, tiled=True)

    normed = pl.pallas_call(
        norm_body,
        grid=(NB,),
        in_specs=[
            pl.BlockSpec((CTX, 8, CB), lambda i: (0, 0, i)), cols(TOK), cols(TOK), whole(TOK, ST),
            cols(1),
        ],
        out_specs=cols(TOK),
        out_shape=sd((TOK, WID), BF),
        scratch_shapes=[pltpu.VMEM((TOK, CB), F32)],
        compiler_params=params(),
        name="norm",
    )(incoming, a1, a2, c_map, norm_gain[None, :])
    sibling = lax.ppermute(normed, "tp", swap)

    up = [(s, (s + 2) % 8) for s in range(8)]
    down = [(s, (s + 6) % 8) for s in range(8)]

    def target(far0, half0, far1, half1):
        d0, d1 = (row + far0) % 4, (row + far1) % 4
        return jnp.stack(
            [(2 * d0 + core) * 2 + half0, (2 * d1 + core) * 2 + half1, d0, d1,
             jnp.int32(half0), jnp.int32(half1)]
        ).astype(jnp.int32)

    def run(index, addends, kind):
        return project(index, normed, sibling, w_out, w_sib, addends, kind)

    far_l, far_r = run(target(2, 0, 2, 1), [], BF)
    far_l = lax.ppermute(far_l, "tp", up)
    far_r = lax.ppermute(far_r, "tp", down)
    above_r, below_l = run(target(1, 1, 3, 0), [], BF)
    above_r = lax.ppermute(above_r, "tp", up)
    below_l = lax.ppermute(below_l, "tp", down)
    above_l, below_r = run(target(1, 0, 3, 1), [(far_l, far_r)], BF)
    above_l = lax.ppermute(above_l, "tp", up)
    below_r = lax.ppermute(below_r, "tp", down)
    here_l, here_r = run(target(0, 0, 0, 1), [(below_l, above_r)], F32)
    return pl.pallas_call(
        final_body,
        in_specs=[pl.BlockSpec(memory_space=pltpu.VMEM)] * 4,
        out_specs=pl.BlockSpec(memory_space=pltpu.VMEM),
        out_shape=sd((TOK, WID), BF),
        compiler_params=pltpu.CompilerParams(vmem_limit_bytes=48 << 20),
        name="final",
    )(here_l, here_r, above_l, below_r)


def solution(mesh):
    in_specs = (
        P("ctx", "tp"),
        P("ctx", None),
        P("ctx", "tp"),
        P("ctx", "tp"),
        P("tp"),
        P(None, "tp"),
        P(),
        P("tp"),
        P(),
        P("tp"),
        P("tp"),
        P("tp", None),
    )
    out_specs = P("ctx", "tp")
    return jax.shard_map(body, mesh=mesh, in_specs=in_specs, out_specs=out_specs, check_vma=False)
```

time: 196 us -> 113 us (0.58)
  waiting for transfers between devices: 92.4 us -> 15.5 us
  Pallas kernels: 0 us -> 46.3 us
  matrix products: 29.8 us -> 0 us
  between operations: 13.8 us -> 0.21 us
  other arithmetic: 12.2 us -> 0.08 us
  starting transfers between devices: 6.93 us -> 15.6 us
  local copies, waits for them, and re-layouts: 17.8 us -> 13.5 us
    reduce_scatter x1 -> x0, waiting for transfers between devices: 78.1 us -> none  [body(): lax.psum_scatter(partial_value.astype(jnp.bfloat16), 'tp', scatter_dimens...]
    pallas_call x0 -> x10, Pallas kernels: none -> 46.3 us  [the longest x4 22.5 us: project(): pl.pallas_call(functools.partial(proj_body, len(addends)), out_shape=[jax...]
    dot_general x17 -> x0, matrix products: 29.1 us -> none  [the longest x1 17 us: body(): partial_value = jnp.dot(normed, w_out, preferred_element_type=jnp.float32)]
    all_gather x1 -> x0, blocking collectives: 21.5 us -> none  [carried_in(): lax.all_gather(a.astype(kind), axis)]
    all_to_all x0 -> x1, blocking collectives: none -> 20.7 us  [body(): got = lax.all_to_all(msg, 'ctx', 0, 0, tiled=True)]
    ppermute x2 -> x9, waiting for transfers between devices: 0.01 us -> 15.5 us  [the longest x1 5.03 us: body(): far_l = lax.ppermute(far_l, 'tp', up)]
    all_gather x1 -> x0, waiting for transfers between devices: 14.3 us -> none  [carried_in(): lax.all_gather(a.astype(kind), axis)]
    unnamed x42 -> x33, local copies, waits for them, and re-layouts: 4.44 us -> 11.7 us
  transfers between devices with their start and end apart: 4 -> 10, of which waited for: 2 -> 6; matrix products, arithmetic and copies ran while one was open for 14% -> 1% of each run, Pallas kernels for 0% -> 22%
where the time goes in v1:
time: 113 us; the launch traced here: 112 us
  Pallas kernels  46.3 us (41%)
  blocking collectives  20.7 us (18%)
  starting transfers between devices  15.6 us (14%)
  waiting for transfers between devices  15.5 us (14%)
  local copies, waits for them, and re-layouts  13.5 us (12%)
    pallas_call x4, Pallas kernels, project(): pl.pallas_call(functools.partial(proj_body, len(addends)), out_shape=[jax...  22.5 us
    all_to_all x1, blocking collectives, body(): got = lax.all_to_all(msg, 'ctx', 0, 0, tiled=True)  20.7 us
    unnamed x33, local copies, waits for them, and re-layouts  11.7 us
    pallas_call x1, Pallas kernels, body(): pl.pallas_call(pick_body, out_shape=sd((4, WID, WID), BF), grid_spec=pltp...  7.77 us
    pallas_call x1, Pallas kernels, body(): pl.pallas_call(scan_in_body, grid=(NB,), in_specs=[SMEM, cols(TOK), cols(...  6.53 us
    ppermute x1, waiting for transfers between devices, body(): far_l = lax.ppermute(far_l, 'tp', up)  5.03 us
    pallas_call x1, Pallas kernels, body(): pl.pallas_call(local_body, grid=(NB,), in_specs=[SMEM, SMEM, cols(TOK), c...  4.97 us
    ppermute x1, waiting for transfers between devices, body(): above_l = lax.ppermute(above_l, 'tp', up)  4.83 us
  transfers between devices with their start and end apart: 10, of which 6 were waited for; matrix products, arithmetic and copies ran while one was open for 1% of the time, Pallas kernels for 22%

profile of v1, /device:TPU:0, one launch (start us, length us, event | category | flops | bytes accessed | tf_op | source)
XLA Modules:
  0.0 111.9 jit_solution(16038116445313470389)
XLA Ops:
  1.4 3.5 %collective-permute-start = (bf16[8,1280]{1,0:T(8,128)(2,1)S(1)}, bf16[8,1280]{1,0:T(8,128)(2,1)S(1)}, u32[]{:S(2)}, u32[]{:S(2)}) collective-permute-start(bf16[8,1280]{1,0:T(8,128)(2,1)S(1)} %pad_maximum_fusion), channel_id=1, source_target_pairs={{0,8},{8,16},{16,24},{24,32},{32,40},{40,48},{48,56},{56,64},{64,7... | collective-permute-start | bytes 61448 | tf_op jit(solution)/shard_map/ppermute | solution.py:218
  6.4 1.2 %copy-done.1 = bf16[512,1024]{1,0:T(8,128)(2,1)S(1)} copy-done((bf16[512,1024]{1,0:T(8,128)(2,1)S(1)}, bf16[512,1024]{1,0:T(8,128)(2,1)}, u32[]{:S(2)}) %copy-start.1) | copy-done | bytes 1048600
  12.0 6.5 %scan_in.1 = (bf16[512,1024]{1,0:T(8,128)(2,1)S(1)}, bf16[512,1024]{1,0:T(8,128)(2,1)S(1)}, bf16[512,128]{1,0:T(8,128)(2,1)S(1)}, bf16[512,128]{1,0:T(8,128)(2,1)S(1)}, bf16[16,16,1024]{2,1,0:T(8,128)(2,1)S(1)}) custom-call(f32[8]{0:T(128)S(1)} %copy-done.9, bf16[512,1024]{1,0:T(8,128)(2,1)S(1)} %copy-done.1, ...), custom_call_target="tpu_custom_call" | custom-call | tf_op jit(solution)/shard_map/scan_in/pallas_call | solution.py:221
  18.6 7.8 %pick.1 = bf16[4,1024,1024]{2,1,0:T(8,128)(2,1)} custom-call(s32[4]{0:T(128)S(1)} %pad_add_fusion.index_ref, bf16[1024,8192]{1,0:T(8,128)(2,1)} %w_ref.9, bf16[512,128]{1,0:T(8,128)(2,1)S(1)} %get-tuple-element.24.c_ref.gate_ref), custom_call_target="tpu_custom_call" | custom-call | tf_op jit(solution)/shard_map/pick/pallas_call | solution.py:250
  26.3 20.7 %all_to_all.10.r_ref = bf16[16,16,1024]{2,1,0:T(8,128)(2,1)S(1)} all-to-all(bf16[16,16,1024]{2,1,0:T(8,128)(2,1)S(1)} %get-tuple-element.20), channel_id=1, replica_groups=mesh['ctx'=16,'tp'=8] {'ctx'}, dimensions={0} | all-to-all | bytes 1048576 | tf_op jit(solution)/shard_map/all_to_all | solution.py:247
  47.0 1.4 %prefix.1 = bf16[16,8,1024]{2,1,0:T(8,128)(2,1)} custom-call(f32[8]{0:T(128)S(1)} %copy-done.9, bf16[16,16,1024]{2,1,0:T(8,128)(2,1)S(1)} %all_to_all.10.r_ref), custom_call_target="tpu_custom_call" | custom-call | tf_op jit(solution)/shard_map/prefix/pallas_call | solution.py:285
  48.5 3.5 %all-to-all-start.1 = ((bf16[16,8,1024]{2,1,0:T(8,128)(2,1)}), bf16[16,8,1024]{2,1,0:T(8,128)(2,1)S(1)}, u32[]{:S(2)}, u32[]{:S(2)}) async-start(bf16[16,8,1024]{2,1,0:T(8,128)(2,1)} %prefix.1), calls=%async_computation.1 | async-start | bytes 524288 | tf_op jit(solution)/shard_map/all_to_all | solution.py:293
  53.3 1.2 %copy-done.4 = bf16[512,1024]{1,0:T(8,128)(2,1)S(1)} copy-done((bf16[512,1024]{1,0:T(8,128)(2,1)S(1)}, bf16[512,1024]{1,0:T(8,128)(2,1)}, u32[]{:S(2)}) %copy-start.4) | copy-done | bytes 1048600
  55.7 5.0 %local.1 = (f32[512,1024]{1,0:T(8,128)S(1)}, f32[512,1024]{1,0:T(8,128)}) custom-call(f32[8]{0:T(128)S(1)} %copy-done.10, f32[8]{0:T(128)S(1)} %copy-done.15, bf16[512,1024]{1,0:T(8,128)(2,1)S(1)} %copy-done.6, bf16[512,1024]{1,0:T(8,128)(2,1)S(1)} %copy-done.4, bf16[512,1024]{1,0:T(8,128)(2,1)S(1)} %copy-done.2, s32[512,8]{1,0:T(8,128)S(1)} %copy.13.codes_ref, ...), custom_call_target="tpu_custom_call" | custom-call | tf_op jit(solution)/shard_map/local/pallas_call | solution.py:268
  60.7 1.6 %copy-done = f32[512,1024]{1,0:T(8,128)S(1)} copy-done((f32[512,1024]{1,0:T(8,128)S(1)}, f32[512,1024]{1,0:T(8,128)}, u32[]{:S(2)}) %copy-start) | copy-done | bytes 2097176
  62.3 2.0 %norm.1.own_ref = bf16[512,1024]{1,0:T(8,128)(2,1)S(1)} custom-call(bf16[16,8,1024]{2,1,0:T(8,128)(2,1)S(1)} %all-to-all-done.1.q_ref, f32[512,1024]{1,0:T(8,128)S(1)} %get-tuple-element.25.a1_ref, f32[512,1024]{1,0:T(8,128)S(1)} %copy-done, bf16[512,128]{1,0:T(8,128)(2,1)S(1)} %get-tuple-element.24.c_ref.gate_ref, f32[1,1024]{1,0:T(1,128)S(1)} %bitcast.20), custom_call_target="tpu_custom_call" | custom-call | tf_op jit(solution)/shard_map/norm/pallas_call | solution.py:295
  64.5 2.5 %collective-permute-done.1.sib_ref = bf16[512,1024]{1,0:T(8,128)(2,1)S(1)} collective-permute-done((bf16[512,1024]{1,0:T(8,128)(2,1)S(1)}, bf16[512,1024]{1,0:T(8,128)(2,1)S(1)}, u32[]{:S(2)}, u32[]{:S(2)}) %collective-permute-start.1) | collective-permute-done | bytes 1048608 | tf_op jit(solution)/shard_map/ppermute | solution.py:308
  67.0 5.8 %project.6 = (bf16[512,512]{1,0:T(8,128)(2,1)}, bf16[512,512]{1,0:T(8,128)(2,1)}) custom-call(s32[6]{0:T(128)S(1)} %stack.87.index_ref, bf16[512,1024]{1,0:T(8,128)(2,1)S(1)} %norm.1.own_ref, bf16[512,1024]{1,0:T(8,128)(2,1)S(1)} %collective-permute-done.1.sib_ref, bf16[1024,8192]{1,0:T(8,128)(2,1)} %w_ref.9, ...), custom_call_target="tpu_custom_call" | custom-call | tf_op jit(solution)/shard_map/project/pallas_call | solution.py:192
  72.8 1.6 %collective-permute-start.5 = (bf16[512,512]{1,0:T(8,128)(2,1)}, bf16[512,512]{1,0:T(8,128)(2,1)S(1)}, u32[]{:S(2)}, u32[]{:S(2)}) collective-permute-start(bf16[512,512]{1,0:T(8,128)(2,1)} %get-tuple-element.31), channel_id=1, source_target_pairs={{0,2},{1,3},{2,4},{3,5},{4,6},{5,7},{6,0},{7,1},{8,10},{9,11},{10,... | collective-permute-start | bytes 1572872 | tf_op jit(solution)/shard_map/ppermute | solution.py:324
  74.3 1.7 %collective-permute-start.6 = (bf16[512,512]{1,0:T(8,128)(2,1)}, bf16[512,512]{1,0:T(8,128)(2,1)S(1)}, u32[]{:S(2)}, u32[]{:S(2)}) collective-permute-start(bf16[512,512]{1,0:T(8,128)(2,1)} %get-tuple-element.32), channel_id=1, source_target_pairs={{0,6},{1,7},{2,0},{3,1},{4,2},{5,3},{6,4},{7,5},{8,14},{9,15},{10,... | collective-permute-start | bytes 1572872 | tf_op jit(solution)/shard_map/ppermute | solution.py:325
  76.2 5.7 %project.4 = (bf16[512,512]{1,0:T(8,128)(2,1)}, bf16[512,512]{1,0:T(8,128)(2,1)}) custom-call(s32[6]{0:T(128)S(1)} %stack.80.index_ref, bf16[512,1024]{1,0:T(8,128)(2,1)S(1)} %norm.1.own_ref, bf16[512,1024]{1,0:T(8,128)(2,1)S(1)} %collective-permute-done.1.sib_ref, bf16[1024,8192]{1,0:T(8,128)(2,1)} %w_ref.9, ...), custom_call_target="tpu_custom_call" | custom-call | tf_op jit(solution)/shard_map/project/pallas_call | solution.py:192
  81.9 1.8 %collective-permute-start.3 = (bf16[512,512]{1,0:T(8,128)(2,1)}, bf16[512,512]{1,0:T(8,128)(2,1)}, u32[]{:S(2)}, u32[]{:S(2)}) collective-permute-start(bf16[512,512]{1,0:T(8,128)(2,1)} %get-tuple-element.27), channel_id=1, source_target_pairs={{0,6},{1,7},{2,0},{3,1},{4,2},{5,3},{6,4},{7,5},{8,14},{9,15},{10,... | collective-permute-start | bytes 1572872 | tf_op jit(solution)/shard_map/ppermute | solution.py:328
  83.9 5.0 %collective-permute-done.5.refs_0_ = bf16[512,512]{1,0:T(8,128)(2,1)S(1)} collective-permute-done((bf16[512,512]{1,0:T(8,128)(2,1)}, bf16[512,512]{1,0:T(8,128)(2,1)S(1)}, u32[]{:S(2)}, u32[]{:S(2)}) %collective-permute-start.5) | collective-permute-done | bytes 524320 | tf_op jit(solution)/shard_map/ppermute | solution.py:324
  89.4 5.8 %project.7 = (bf16[512,512]{1,0:T(8,128)(2,1)}, bf16[512,512]{1,0:T(8,128)(2,1)}) custom-call(s32[6]{0:T(128)S(1)} %stack.83.index_ref, bf16[512,1024]{1,0:T(8,128)(2,1)S(1)} %norm.1.own_ref, bf16[512,1024]{1,0:T(8,128)(2,1)S(1)} %collective-permute-done.1.sib_ref, bf16[1024,8192]{1,0:T(8,128)(2,1)} %w_ref.9, ...), custom_call_target="tpu_custom_call" | custom-call | tf_op jit(solution)/shard_map/project/pallas_call | solution.py:192
  95.2 1.6 %collective-permute-start.7 = (bf16[512,512]{1,0:T(8,128)(2,1)}, bf16[512,512]{1,0:T(8,128)(2,1)S(1)}, u32[]{:S(2)}, u32[]{:S(2)}) collective-permute-start(bf16[512,512]{1,0:T(8,128)(2,1)} %get-tuple-element.33), channel_id=1, source_target_pairs={{0,2},{1,3},{2,4},{3,5},{4,6},{5,7},{6,0},{7,1},{8,10},{9,11},{10,... | collective-permute-start | bytes 1572872 | tf_op jit(solution)/shard_map/ppermute | solution.py:330
  96.8 1.7 %collective-permute-start.8 = (bf16[512,512]{1,0:T(8,128)(2,1)}, bf16[512,512]{1,0:T(8,128)(2,1)S(1)}, u32[]{:S(2)}, u32[]{:S(2)}) collective-permute-start(bf16[512,512]{1,0:T(8,128)(2,1)} %get-tuple-element.34), channel_id=1, source_target_pairs={{0,6},{1,7},{2,0},{3,1},{4,2},{5,3},{6,4},{7,5},{8,14},{9,15},{10,... | collective-permute-start | bytes 1572872 | tf_op jit(solution)/shard_map/ppermute | solution.py:331
  98.5 2.2 %collective-permute-done.3.refs_0_ = bf16[512,512]{1,0:T(8,128)(2,1)} collective-permute-done((bf16[512,512]{1,0:T(8,128)(2,1)}, bf16[512,512]{1,0:T(8,128)(2,1)}, u32[]{:S(2)}, u32[]{:S(2)}) %collective-permute-start.3) | collective-permute-done | bytes 524320 | tf_op jit(solution)/shard_map/ppermute | solution.py:328
  100.7 5.1 %project.5 = (f32[512,512]{1,0:T(8,128)S(1)}, f32[512,512]{1,0:T(8,128)S(1)}) custom-call(s32[6]{0:T(128)S(1)} %stack.70.index_ref, bf16[512,1024]{1,0:T(8,128)(2,1)S(1)} %norm.1.own_ref, bf16[512,1024]{1,0:T(8,128)(2,1)S(1)} %collective-permute-done.1.sib_ref, bf16[1024,8192]{1,0:T(8,128)(2,1)} %w_ref.9, ...), custom_call_target="tpu_custom_call" | custom-call | tf_op jit(solution)/shard_map/project/pallas_call | solution.py:192
  105.8 4.8 %collective-permute-done.7.a_ref = bf16[512,512]{1,0:T(8,128)(2,1)S(1)} collective-permute-done((bf16[512,512]{1,0:T(8,128)(2,1)}, bf16[512,512]{1,0:T(8,128)(2,1)S(1)}, u32[]{:S(2)}, u32[]{:S(2)}) %collective-permute-start.7) | collective-permute-done | bytes 524320 | tf_op jit(solution)/shard_map/ppermute | solution.py:330
  (48 shorter events, 11.9 us)
Async XLA Ops:
  1.4 4.9 %collective-permute-start = (bf16[8,1280]{1,0:T(8,128)(2,1)S(1)}, bf16[8,1280]{1,0:T(8,128)(2,1)S(1)}, u32[]{:S(2)}, u32[]{:S(2)}) collective-permute-start(bf16[8,1280]{1,0:T(8,128)(2,1)S(1)} %pad_maximum_fusion), channel_id=1, source_target_pairs={{0,8},{8,16},{16,24},{24,32},{32,40},{40,48},{48,56},{56,64},{64,7... | collective-permute-start | bytes 61448 | tf_op jit(solution)/shard_map/ppermute | solution.py:218
  6.4 1.2 %copy-start.1 = (bf16[512,1024]{1,0:T(8,128)(2,1)S(1)}, bf16[512,1024]{1,0:T(8,128)(2,1)}, u32[]{:S(2)}) copy-start(bf16[512,1024]{1,0:T(8,128)(2,1)} %x_ref.1) | copy-start | bytes 3145732
  7.6 0.9 copy-start.7
  8.5 0.7 copy-start.8
  9.9 0.7 copy-start.11
  10.6 0.7 copy-start.12
  18.5 7.8 %copy-start.3 = (bf16[512,1024]{1,0:T(8,128)(2,1)}, bf16[512,1024]{1,0:T(8,128)(2,1)S(1)}, u32[]{:S(2)}) copy-start(bf16[512,1024]{1,0:T(8,128)(2,1)S(1)} %get-tuple-element.22.xc_ref) | copy-start | bytes 3145732
  18.5 7.8 %copy-start.5 = (bf16[512,1024]{1,0:T(8,128)(2,1)}, bf16[512,1024]{1,0:T(8,128)(2,1)S(1)}, u32[]{:S(2)}) copy-start(bf16[512,1024]{1,0:T(8,128)(2,1)S(1)} %get-tuple-element.21.xt_ref) | copy-start | bytes 3145732
  18.5 33.5 %copy-start.10 = (f32[8]{0:T(128)S(1)}, f32[8]{0:T(128)}, u32[]{:S(2)}) copy-start(f32[8]{0:T(128)} %rate_ref.5) | copy-start | bytes 100
  18.5 33.5 %copy-start.15 = (f32[8]{0:T(128)S(1)}, f32[8]{0:T(128)}, u32[]{:S(2)}) copy-start(f32[8]{0:T(128)} %skip_ref.1) | copy-start | bytes 100
  18.5 42.1 %copy-start.13 = (f32[1024]{0:T(1024)S(1)}, f32[1024]{0:T(1024)}, u32[]{:S(2)}) copy-start(f32[1024]{0:T(1024)} %param.22) | copy-start | bytes 12292
  26.3 40.7 %collective-permute-start.2 = (bf16[4,1024,1024]{2,1,0:T(8,128)(2,1)}, bf16[4,1024,1024]{2,1,0:T(8,128)(2,1)}, u32[]{:S(2)}, u32[]{:S(2)}) collective-permute-start(bf16[4,1024,1024]{2,1,0:T(8,128)(2,1)} %pick.1), channel_id=1, source_target_pairs={{0,1},{1,0},{2,3},{3,2},{4,5},{5,4},{6,7},{7,6},{8,9},{9,8},{10,11... | collective-permute-start | bytes 25165832 | tf_op jit(solution)/shard_map/ppermute | solution.py:266
  48.5 12.2 %all-to-all-start.1 = ((bf16[16,8,1024]{2,1,0:T(8,128)(2,1)}), bf16[16,8,1024]{2,1,0:T(8,128)(2,1)S(1)}, u32[]{:S(2)}, u32[]{:S(2)}) async-start(bf16[16,8,1024]{2,1,0:T(8,128)(2,1)} %prefix.1), calls=%async_computation.1 | async-start | bytes 524288 | tf_op jit(solution)/shard_map/all_to_all | solution.py:293
  52.0 1.2 %copy-start.2 = (bf16[512,1024]{1,0:T(8,128)(2,1)S(1)}, bf16[512,1024]{1,0:T(8,128)(2,1)}, u32[]{:S(2)}) copy-start(bf16[512,1024]{1,0:T(8,128)(2,1)} %z_ref.1) | copy-start | bytes 3145732
  53.3 1.2 %copy-start.4 = (bf16[512,1024]{1,0:T(8,128)(2,1)S(1)}, bf16[512,1024]{1,0:T(8,128)(2,1)}, u32[]{:S(2)}) copy-start(bf16[512,1024]{1,0:T(8,128)(2,1)} %copy-done.3) | copy-start | bytes 3145732
  54.5 1.2 %copy-start.6 = (bf16[512,1024]{1,0:T(8,128)(2,1)S(1)}, bf16[512,1024]{1,0:T(8,128)(2,1)}, u32[]{:S(2)}) copy-start(bf16[512,1024]{1,0:T(8,128)(2,1)} %copy-done.5) | copy-start | bytes 3145732
  60.7 1.6 %copy-start = (f32[512,1024]{1,0:T(8,128)S(1)}, f32[512,1024]{1,0:T(8,128)}, u32[]{:S(2)}) copy-start(f32[512,1024]{1,0:T(8,128)} %get-tuple-element.26.a2_ref) | copy-start | bytes 6291460
  64.3 2.7 %collective-permute-start.1 = (bf16[512,1024]{1,0:T(8,128)(2,1)S(1)}, bf16[512,1024]{1,0:T(8,128)(2,1)S(1)}, u32[]{:S(2)}, u32[]{:S(2)}) collective-permute-start(bf16[512,1024]{1,0:T(8,128)(2,1)S(1)} %norm.1.own_ref), channel_id=1, source_target_pairs={{0,1},{1,0},{2,3},{3,2},{4,5},{5,4},{6,7},{7,6},{8,9},{9,8},{10,11... | collective-permute-start | bytes 3145736 | tf_op jit(solution)/shard_map/ppermute | solution.py:308
  72.8 16.2 %collective-permute-start.5 = (bf16[512,512]{1,0:T(8,128)(2,1)}, bf16[512,512]{1,0:T(8,128)(2,1)S(1)}, u32[]{:S(2)}, u32[]{:S(2)}) collective-permute-start(bf16[512,512]{1,0:T(8,128)(2,1)} %get-tuple-element.31), channel_id=1, source_target_pairs={{0,2},{1,3},{2,4},{3,5},{4,6},{5,7},{6,0},{7,1},{8,10},{9,11},{10,... | collective-permute-start | bytes 1572872 | tf_op jit(solution)/shard_map/ppermute | solution.py:324
  74.3 15.0 %collective-permute-start.6 = (bf16[512,512]{1,0:T(8,128)(2,1)}, bf16[512,512]{1,0:T(8,128)(2,1)S(1)}, u32[]{:S(2)}, u32[]{:S(2)}) collective-permute-start(bf16[512,512]{1,0:T(8,128)(2,1)} %get-tuple-element.32), channel_id=1, source_target_pairs={{0,6},{1,7},{2,0},{3,1},{4,2},{5,3},{6,4},{7,5},{8,14},{9,15},{10,... | collective-permute-start | bytes 1572872 | tf_op jit(solution)/shard_map/ppermute | solution.py:325
  81.9 18.8 %collective-permute-start.3 = (bf16[512,512]{1,0:T(8,128)(2,1)}, bf16[512,512]{1,0:T(8,128)(2,1)}, u32[]{:S(2)}, u32[]{:S(2)}) collective-permute-start(bf16[512,512]{1,0:T(8,128)(2,1)} %get-tuple-element.27), channel_id=1, source_target_pairs={{0,6},{1,7},{2,0},{3,1},{4,2},{5,3},{6,4},{7,5},{8,14},{9,15},{10,... | collective-permute-start | bytes 1572872 | tf_op jit(solution)/shard_map/ppermute | solution.py:328
  83.7 17.0 %collective-permute-start.4 = (bf16[512,512]{1,0:T(8,128)(2,1)}, bf16[512,512]{1,0:T(8,128)(2,1)}, u32[]{:S(2)}, u32[]{:S(2)}) collective-permute-start(bf16[512,512]{1,0:T(8,128)(2,1)} %get-tuple-element.28), channel_id=1, source_target_pairs={{0,2},{1,3},{2,4},{3,5},{4,6},{5,7},{6,0},{7,1},{8,10},{9,11},{10,... | collective-permute-start | bytes 1572872 | tf_op jit(solution)/shard_map/ppermute | solution.py:327
  95.2 15.5 %collective-permute-start.7 = (bf16[512,512]{1,0:T(8,128)(2,1)}, bf16[512,512]{1,0:T(8,128)(2,1)S(1)}, u32[]{:S(2)}, u32[]{:S(2)}) collective-permute-start(bf16[512,512]{1,0:T(8,128)(2,1)} %get-tuple-element.33), channel_id=1, source_target_pairs={{0,2},{1,3},{2,4},{3,5},{4,6},{5,7},{6,0},{7,1},{8,10},{9,11},{10,... | collective-permute-start | bytes 1572872 | tf_op jit(solution)/shard_map/ppermute | solution.py:330
  96.8 13.9 %collective-permute-start.8 = (bf16[512,512]{1,0:T(8,128)(2,1)}, bf16[512,512]{1,0:T(8,128)(2,1)S(1)}, u32[]{:S(2)}, u32[]{:S(2)}) collective-permute-start(bf16[512,512]{1,0:T(8,128)(2,1)} %get-tuple-element.34), channel_id=1, source_target_pairs={{0,6},{1,7},{2,0},{3,1},{4,2},{5,3},{6,4},{7,5},{8,14},{9,15},{10,... | collective-permute-start | bytes 1572872 | tf_op jit(solution)/shard_map/ppermute | solution.py:331
  (2 other events, 1.3 us)

commit v2 on v1

v2 whole, which is shorter than its diff:
```python
import functools

import jax
import jax.numpy as jnp
from jax import lax
from jax.experimental import pallas as pl
from jax.experimental.pallas import tpu as pltpu
from jax.sharding import PartitionSpec as P

BF = jnp.bfloat16
F32 = jnp.float32
TOK = 512
HT = TOK // 2
WID = 1024
HALF = WID // 2
HEADS = 8
HW = 128
ST = 128
CTX = 16
CB = 256
NB = WID // CB
HB = CB // HW
SEQ = TOK * CTX
DECAY = 12.288 / SEQ / 63.0
SCALE = 1.0 / (ST * SEQ) ** 0.5
ROWS = 64
SD = jax.ShapeDtypeStruct


def silu(v):
    half = 0.5 * v
    return half + half * jnp.tanh(half)


def mm(a, b):
    return jnp.dot(a, b, preferred_element_type=F32)


def lanes(ref, first, count, factor):
    rows = [jnp.full((1, HW), ref[first + k] * factor, F32) for k in range(count)]
    return jnp.concatenate(rows, axis=1)


def fill_tri(tri, first, count):
    for r in range(0, count, HW):
        row = lax.broadcasted_iota(jnp.int32, (HW, TOK), 0) + (r + first)
        col = lax.broadcasted_iota(jnp.int32, (HW, TOK), 1)
        tri[r : r + HW, :] = jnp.where(row >= col, 1.0, 0.0).astype(BF)


def fill_codes(codes_ref, codes):
    padded = jnp.concatenate([codes_ref[...].astype(F32), jnp.zeros((HW - HEADS, TOK), F32)], axis=0)
    codes[...] = padded.T.astype(BF)


def code_sums(codes, tri, block):
    head = lax.broadcasted_iota(jnp.int32, (HW, CB), 0)
    lane = lax.broadcasted_iota(jnp.int32, (HW, CB), 1) // HW + HB * block
    spread = jnp.where(head == lane, 1.0, 0.0).astype(BF)
    return mm(tri[...], mm(codes[...], spread).astype(BF))


def conv_rows(xe, w_ref, bias_ref, r):
    total = bias_ref[...]
    for k in range(4):
        total = total + w_ref[k : k + 1, :] * xe[5 + k + r : 5 + k + r + ROWS, :]
    return silu(total)


def rim_body(x_ref, bc_ref, o_ref):
    o_ref[:, :WID] = x_ref[...]
    o_ref[:, WID:] = bc_ref[...]


def scan_in_body(
    last, rate_ref, x_ref, rim_ref, bc_ref, rimbc_ref, codes_ref, cx_ref, bx_ref, cbc_ref, bbc_ref, *refs
):
    if last:
        xc_ref, xt_ref, b_ref, c_ref, state_ref, total_ref, xe, tri, bt, sums, codes = refs
    else:
        earlier_ref, whole_ref, xc_ref, xt_ref, b_ref, c_ref, msg_ref, xe, tri, bt, sums, codes = refs
    block = pl.program_id(0)

    @pl.when(block == 0)
    def _():
        fill_tri(tri, HT if last else 0, HT)
        fill_codes(codes_ref, codes)
        xe[0:8, :] = rimbc_ref[...].astype(F32)[-8:, :]
        xe[8 : 8 + HT, :] = bc_ref[...].astype(F32)
        for r in range(0, HT, ROWS):
            out = conv_rows(xe, cbc_ref, bbc_ref, r)
            b_ref[r : r + ROWS, :] = out[:, :ST].astype(BF)
            c_ref[r : r + ROWS, :] = out[:, ST:].astype(BF)
        bt[...] = b_ref[...].astype(F32).T.astype(BF)

    xe[0:8, :] = rim_ref[...].astype(F32)[-8:, :]
    xe[8 : 8 + HT, :] = x_ref[...].astype(F32)
    sums[...] = code_sums(codes, tri, block)
    rate = lanes(rate_ref, block * HB, HB, DECAY)
    for r in range(0, HT, ROWS):
        xc = conv_rows(xe, cx_ref, bx_ref, r).astype(BF)
        xc_ref[r : r + ROWS, :] = xc
        xt_ref[r : r + ROWS, :] = (xc.astype(F32) * jnp.exp(rate * sums[r : r + ROWS, :])).astype(BF)
    state = mm(bt[...], xt_ref[...])
    if last:
        state_ref[...] = state
        total_ref[...] = sums[HT - 8 : HT, :]
        return
    state = state + earlier_ref[...]
    total = whole_ref[7:8, :]
    high = jnp.floor(total * (1.0 / 256.0))
    low = total - 256.0 * high
    row = lax.broadcasted_iota(jnp.int32, (8, CB), 0)
    extra = jnp.where(row == 0, high, jnp.where(row == 1, low, 0.0))
    for j in range(CTX):
        part = jnp.concatenate([state[8 * j : 8 * j + 8, :], extra], axis=0)
        msg_ref[j] = part.astype(BF)


def local_body(
    rate_ref, skip_ref, xt0_ref, xt1_ref, xc0_ref, xc1_ref, z_ref, codes_ref, b0_ref, b1_ref, c0_ref, c1_ref,
    a1_ref, a2_ref, tri, gram, sums, prod, codes,
):
    block = pl.program_id(0)

    @pl.when(block == 0)
    def _():
        fill_tri(tri, 0, TOK)
        fill_codes(codes_ref, codes)
        for r in range(0, TOK, HW):
            c_ref = c0_ref if r < HT else c1_ref
            rows = c_ref[r % HT : r % HT + HW, :]
            row = lax.broadcasted_iota(jnp.int32, (HW, HT), 0) + r
            col = lax.broadcasted_iota(jnp.int32, (HW, HT), 1)
            for k, b_ref in enumerate((b0_ref, b1_ref)):
                part = lax.dot_general(
                    rows, b_ref[...], (((1,), (1,)), ((), ())), preferred_element_type=F32
                )
                gram[r : r + HW, k * HT : (k + 1) * HT] = jnp.where(
                    row >= col + k * HT, part, 0.0
                ).astype(BF)

    sums[...] = code_sums(codes, tri, block)
    prod[0:HT, :] = mm(gram[0:HT, 0:HT], xt0_ref[...])
    prod[HT:TOK, :] = mm(gram[HT:TOK, 0:HT], xt0_ref[...]) + mm(gram[HT:TOK, HT:TOK], xt1_ref[...])
    rate = lanes(rate_ref, block * HB, HB, -DECAY)
    skip = lanes(skip_ref, block * HB, HB, 1.0)
    for r in range(0, TOK, ROWS):
        gate = silu(z_ref[r : r + ROWS, :].astype(F32))
        fade = SCALE * jnp.exp(rate * sums[r : r + ROWS, :])
        xc_ref = xc0_ref if r < HT else xc1_ref
        xc = xc_ref[r % HT : r % HT + ROWS, :].astype(F32)
        a1_ref[r : r + ROWS, :] = (prod[r : r + ROWS, :] * fade + skip * xc) * gate
        a2_ref[r : r + ROWS, :] = fade * gate


def prefix_body(rate_ref, r_ref, after_ref, q_ref):
    rate = lanes(rate_ref, 0, HEADS, -DECAY)
    state = jnp.zeros((8, WID), F32)
    for c in range(CTX):
        q_ref[c] = state.astype(BF)
        got = r_ref[c].astype(F32)
        total = 256.0 * got[8:9, :] + got[9:10, :]
        state = jnp.exp(rate * total) * (state + got[0:8, :])


def norm_body(q_ref, a1_ref, a2_ref, c0_ref, c1_ref, gain_ref, n_ref, prod):
    state = q_ref[...].astype(F32).reshape(ST, CB).astype(BF)
    prod[0:HT, :] = mm(c0_ref[...], state)
    prod[HT:TOK, :] = mm(c1_ref[...], state)
    for r in range(0, TOK, ROWS):
        for h in range(0, CB, HW):
            rs, hs = slice(r, r + ROWS), slice(h, h + HW)
            gated = a1_ref[rs, hs] + a2_ref[rs, hs] * prod[rs, hs]
            power = jnp.mean(gated * gated, axis=-1, keepdims=True)
            n_ref[rs, hs] = (gated * lax.rsqrt(power + 1e-05) * gain_ref[:, hs]).astype(BF)


def partial_body(index_ref, n_ref, w_ref, after_ref, o_ref):
    o_ref[...] = mm(n_ref[...], w_ref[...]).astype(o_ref.dtype)


def summed_body(adds, index_ref, n_ref, w_ref, r_ref, after_ref, *refs):
    step = pl.program_id(0)
    outs = refs[-2:]
    for k in range(2):

        @pl.when(step == k)
        def _():
            total = mm(n_ref[...], w_ref[...]) + r_ref[...].astype(F32)
            for a in range(adds):
                total = total + refs[2 * a + k][...].astype(F32)
            outs[k][...] = total.astype(outs[k].dtype)


def final_body(m0_ref, m1_ref, a_ref, b_ref, o_ref):
    o_ref[:, :HALF] = (m0_ref[...] + a_ref[...].astype(F32)).astype(BF)
    o_ref[:, HALF:] = (m1_ref[...] + b_ref[...].astype(F32)).astype(BF)


def params(dims=1):
    return pltpu.CompilerParams(
        dimension_semantics=("arbitrary",) * dims if dims else None, vmem_limit_bytes=20 << 20
    )


SMEM = pl.BlockSpec(memory_space=pltpu.SMEM)
VMEM = pl.BlockSpec(memory_space=pltpu.VMEM)


def whole(*shape):
    return pl.BlockSpec(shape, lambda i: (0,) * len(shape))


def cols(rows, at=0):
    return pl.BlockSpec((rows, CB), lambda i: (at, i))


def in_hbm(a):
    return pltpu.with_memory_space_constraint(a, pltpu.HBM)


STEPS = ((2, 0), (2, 1), (1, 1), (3, 0), (1, 0), (3, 1), (0, 0), (0, 1))


def column_block(first, flip):
    def index(i, place_ref):
        place = place_ref[0]
        far, side = jnp.int32(0), jnp.int32(0)
        for k, (f, s) in enumerate(STEPS[first:]):
            far = jnp.where(i == k, f, far)
            side = jnp.where(i == k, s, side)
        core = (place & 1) ^ flip
        return 0, ((((place >> 1) + far) & 3) * 2 + core) * 2 + side

    return pl.BlockSpec((WID, HALF), index)


def whole2(*shape):
    return pl.BlockSpec(shape, lambda i, ix: (0,) * len(shape))


ANY = pl.BlockSpec(memory_space=pl.ANY)


def partial(place, normed, w, first, count, after):
    return pl.pallas_call(
        partial_body,
        out_shape=SD((TOK, count * HALF), BF),
        grid_spec=pltpu.PrefetchScalarGridSpec(
            num_scalar_prefetch=1,
            grid=(count,),
            in_specs=[whole2(TOK, WID), column_block(first, 1), ANY],
            out_specs=pl.BlockSpec((TOK, HALF), lambda i, ix: (0, i)),
        ),
        compiler_params=params(),
        name="partial",
    )(place, normed, w, after)


def summed(place, normed, w, first, got, at, addends, kind, after):
    flat = [a for pair in addends for a in pair]
    const = whole2(TOK, HALF)
    return pl.pallas_call(
        functools.partial(summed_body, len(addends)),
        out_shape=[SD((TOK, HALF), kind)] * 2,
        grid_spec=pltpu.PrefetchScalarGridSpec(
            num_scalar_prefetch=1,
            grid=(2,),
            in_specs=[
                whole2(TOK, WID),
                column_block(first, 0),
                pl.BlockSpec((TOK, HALF), lambda i, ix: (0, at + i)),
                ANY,
            ]
            + [const] * len(flat),
            out_specs=[const, const],
        ),
        compiler_params=params(),
        name="summed",
    )(place, normed, w, got, after, *flat)


def scan_in(last, rate, x_in, rim, bc_in, codes, conv_x, bias_x, conv_bc, bias_bc, *carry):
    at = 1 if last else 0
    if last:
        rims = [pl.BlockSpec((16, CB), lambda i: (15, i)), pl.BlockSpec((16, 2 * ST), lambda i: (15, 0))]
        rim_args = (x_in, bc_in)
        extra_out = [SD((ST, WID), F32), SD((8, WID), F32)]
        extra_spec = [cols(ST), cols(8)]
    else:
        rims = [cols(8), pl.BlockSpec((8, 2 * ST), lambda i: (0, NB))]
        rim_args = (rim, rim)
        extra_out = [SD((CTX, 16, WID), BF)]
        extra_spec = [pl.BlockSpec((CTX, 16, CB), lambda i: (0, 0, i))]
    return pl.pallas_call(
        functools.partial(scan_in_body, last),
        grid=(NB,),
        in_specs=[
            SMEM, cols(HT, at), rims[0], pl.BlockSpec((HT, 2 * ST), lambda i: (at, 0)), rims[1],
            whole(HEADS, TOK), cols(4), cols(1), whole(4, 2 * ST), whole(1, 2 * ST),
        ]
        + ([] if last else [cols(ST), cols(8)]),
        out_specs=[cols(HT), cols(HT), whole(HT, ST), whole(HT, ST)] + extra_spec,
        out_shape=[pltpu.HBM((HT, WID), BF), pltpu.HBM((HT, WID), BF), SD((HT, ST), BF), SD((HT, ST), BF)]
        + extra_out,
        scratch_shapes=[
            pltpu.VMEM((HT + 8, CB), F32), pltpu.VMEM((HT, TOK), BF), pltpu.VMEM((ST, HT), BF),
            pltpu.VMEM((HT, CB), F32), pltpu.VMEM((TOK, HW), BF),
        ],
        compiler_params=params(),
        name="scan_in",
    )(rate, x_in, rim_args[0], bc_in, rim_args[1], codes, conv_x, bias_x, conv_bc, bias_bc, *carry)


def body(
    x_in, bc_in, z_in, codes, head_rate, conv_x, conv_bc, bias_x, bias_bc, skip, norm_gain, w_out
):
    place = lax.axis_index("tp")
    where = jnp.full((1,), place, jnp.int32)
    x_in, bc_in, z_in, w_out = in_hbm(x_in), in_hbm(bc_in), in_hbm(z_in), in_hbm(w_out)
    codes, conv_x, conv_bc = in_hbm(codes.T), in_hbm(conv_x), in_hbm(conv_bc)
    head_rate, skip = in_hbm(head_rate), in_hbm(skip)
    bias_x, bias_bc, gain = in_hbm(bias_x[None, :]), in_hbm(bias_bc[None, :]), in_hbm(norm_gain[None, :])

    rim = pl.pallas_call(
        rim_body,
        grid=(1,),
        in_specs=[
            pl.BlockSpec((8, WID), lambda i: (TOK // 8 - 1, 0)),
            pl.BlockSpec((8, 2 * ST), lambda i: (TOK // 8 - 1, 0)),
        ],
        out_specs=whole(8, WID + 2 * ST),
        out_shape=SD((8, WID + 2 * ST), BF),
        compiler_params=params(),
        name="rim",
    )(x_in, bc_in)
    rim = lax.ppermute(rim, "ctx", [(s, s + 1) for s in range(CTX - 1)])

    shared = (codes, conv_x, bias_x, conv_bc, bias_bc)
    xc1, xt1, b1, c1, state1, total = scan_in(True, head_rate, x_in, None, bc_in, *shared)
    xc0, xt0, b0, c0, msg = scan_in(False, head_rate, x_in, rim, bc_in, *shared, state1, total)

    got = lax.all_to_all(msg, "ctx", 0, 0, tiled=True)

    a1, a2 = pl.pallas_call(
        local_body,
        grid=(NB,),
        in_specs=[
            SMEM, SMEM, cols(HT), cols(HT), cols(HT), cols(HT), cols(TOK), whole(HEADS, TOK),
            whole(HT, ST), whole(HT, ST), whole(HT, ST), whole(HT, ST),
        ],
        out_specs=[cols(TOK), cols(TOK)],
        out_shape=[pltpu.HBM((TOK, WID), F32)] * 2,
        scratch_shapes=[
            pltpu.VMEM((TOK, TOK), BF), pltpu.VMEM((TOK, TOK), BF), pltpu.VMEM((TOK, CB), F32),
            pltpu.VMEM((TOK, CB), F32), pltpu.VMEM((TOK, HW), BF),
        ],
        compiler_params=params(),
        cost_estimate=pl.CostEstimate(flops=2 << 30, transcendentals=1 << 20, bytes_accessed=8 << 20),
        name="local",
    )(head_rate, skip, *map(in_hbm, (xt0, xt1, xc0, xc1)), z_in, codes, b0, b1, c0, c1)
    a1, a2 = in_hbm(a1), in_hbm(a2)

    prefix = pl.pallas_call(
        prefix_body,
        in_specs=[SMEM, VMEM, ANY],
        out_specs=VMEM,
        out_shape=SD((CTX, 8, WID), BF),
        compiler_params=params(0),
        name="prefix",
    )(head_rate, got, a1)
    incoming = lax.all_to_all(prefix, "ctx", 0, 0, tiled=True)

    normed = pl.pallas_call(
        norm_body,
        grid=(NB,),
        in_specs=[
            pl.BlockSpec((CTX, 8, CB), lambda i: (0, 0, i)), cols(TOK), cols(TOK), whole(HT, ST),
            whole(HT, ST), cols(1),
        ],
        out_specs=cols(TOK),
        out_shape=SD((TOK, WID), BF),
        scratch_shapes=[pltpu.VMEM((TOK, CB), F32)],
        compiler_params=params(),
        name="norm",
    )(incoming, a1, a2, c0, c1, gain)

    swap = [(s, s ^ 1) for s in range(8)]
    up = [(s, (s + 2) % 8) for s in range(8)]
    down = [(s, (s + 6) % 8) for s in range(8)]
    args = (where, normed, w_out)
    s1 = partial(*args, 0, 2, where)
    r1 = lax.ppermute(s1, "tp", swap)
    s2 = partial(*args, 2, 2, s1)
    r2 = lax.ppermute(s2, "tp", swap)
    far_l, far_r = summed(*args, 0, r1, 0, [], BF, s2)
    got_l = lax.ppermute(far_l, "tp", up)
    got_r = lax.ppermute(far_r, "tp", down)
    above_r, below_l = summed(*args, 2, r2, 0, [], BF, far_l)
    from_r = lax.ppermute(above_r, "tp", up)
    from_l = lax.ppermute(below_l, "tp", down)
    r3 = lax.ppermute(partial(*args, 4, 4, above_r), "tp", swap)
    above_l, below_r = summed(*args, 4, r3, 0, [(got_l, got_r)], BF, where)
    last_l = lax.ppermute(above_l, "tp", up)
    last_r = lax.ppermute(below_r, "tp", down)
    here_l, here_r = summed(*args, 6, r3, 2, [(from_l, from_r)], F32, above_l)
    return pl.pallas_call(
        final_body,
        in_specs=[VMEM] * 4,
        out_specs=VMEM,
        out_shape=SD((TOK, WID), BF),
        compiler_params=params(0),
        name="final",
    )(here_l, here_r, last_l, last_r)


def solution(mesh):
    in_specs = (
        P("ctx", "tp"),
        P("ctx", None),
        P("ctx", "tp"),
        P("ctx", "tp"),
        P("tp"),
        P(None, "tp"),
        P(),
        P("tp"),
        P(),
        P("tp"),
        P("tp"),
        P("tp", None),
    )
    out_specs = P("ctx", "tp")
    return jax.shard_map(body, mesh=mesh, in_specs=in_specs, out_specs=out_specs, check_vma=False)
```

time: 113 us -> 112 us (level)
  waiting for transfers between devices: 15.5 us -> 40.3 us
  blocking collectives: 20.7 us -> 0 us
  local copies, waits for them, and re-layouts: 13.5 us -> 0 us
  starting transfers between devices: 15.6 us -> 23.8 us
    all_to_all x1 -> x0, blocking collectives: 20.7 us -> none  [body(): got = lax.all_to_all(msg, 'ctx', 0, 0, tiled=True)]
    ppermute x8 -> x9, waiting for transfers between devices: 15 us -> 26.7 us  [the longest x1 8.98 us: body(): got_r = lax.ppermute(far_r, 'tp', down)]
    unnamed x33 -> x0, local copies, waits for them, and re-layouts: 11.7 us -> none
    all_to_all x1, waiting for transfers between devices: 0.01 us -> 8.65 us  [body(): incoming = lax.all_to_all(prefix, 'ctx', 0, 0, tiled=True)]
    all_to_all x0 -> x1, starting transfers between devices: none -> 7.59 us  [body(): got = lax.all_to_all(msg, 'ctx', 0, 0, tiled=True)]
    all_to_all x0 -> x1, waiting for transfers between devices: none -> 4.95 us  [body(): got = lax.all_to_all(msg, 'ctx', 0, 0, tiled=True)]
    pallas_call x1, Pallas kernels: 1.96 us -> 3.74 us  [body(): pl.pallas_call(norm_body, grid=(NB,), in_specs=[pl.BlockSpec((CTX, 8, CB)...]
    pallas_call x9 -> x13, Pallas kernels: 44.3 us -> 42.7 us  [the longest x2 11.4 us: scan_in(): pl.pallas_call(functools.partial(scan_in_body, last), grid=(NB,), in_spec...]
  transfers between devices with their start and end apart: 10 -> 12, of which waited for: 6 -> 8; matrix products, arithmetic and copies ran while one was open for 1% -> 0% of each run, Pallas kernels for 22% -> 21%
where the time goes in v2:
time: 112 us; the launch traced here: 111 us
  Pallas kernels  46.4 us (41%)
  waiting for transfers between devices  40.3 us (36%)
  starting transfers between devices  23.8 us (21%)
    pallas_call x2, Pallas kernels, scan_in(): pl.pallas_call(functools.partial(scan_in_body, last), grid=(NB,), in_spec...  11.4 us
    pallas_call x4, Pallas kernels, summed(): pl.pallas_call(functools.partial(summed_body, len(addends)), out_shape=[S...  11.1 us
    pallas_call x3, Pallas kernels, partial(): pl.pallas_call(partial_body, out_shape=SD((TOK, count * HALF), BF), grid_...  10.5 us
    ppermute x1, waiting for transfers between devices, body(): got_r = lax.ppermute(far_r, 'tp', down)  8.98 us
    all_to_all x1, waiting for transfers between devices, body(): incoming = lax.all_to_all(prefix, 'ctx', 0, 0, tiled=True)  8.65 us
    all_to_all x1, starting transfers between devices, body(): got = lax.all_to_all(msg, 'ctx', 0, 0, tiled=True)  7.59 us
    pallas_call x1, Pallas kernels, body(): pl.pallas_call(local_body, grid=(NB,), in_specs=[SMEM, SMEM, cols(HT), co...  6.3 us
    all_to_all x1, waiting for transfers between devices, body(): got = lax.all_to_all(msg, 'ctx', 0, 0, tiled=True)  4.95 us
  transfers between devices with their start and end apart: 12, of which 8 were waited for; matrix products, arithmetic and copies ran while one was open for 0% of the time, Pallas kernels for 21%

profile of v2, /device:TPU:0, one launch (start us, length us, event | category | flops | bytes accessed | tf_op | source)
XLA Modules:
  0.0 110.6 jit_solution(11397201483147969351)
XLA Ops:
  0.7 3.5 %collective-permute-start = (bf16[8,1280]{1,0:T(8,128)(2,1)S(1)}, bf16[8,1280]{1,0:T(8,128)(2,1)S(1)}, u32[]{:S(2)}, u32[]{:S(2)}) collective-permute-start(bf16[8,1280]{1,0:T(8,128)(2,1)S(1)} %rim.1), channel_id=1, source_target_pairs={{0,8},{8,16},{16,24},{24,32},{32,40},{40,48},{48,56},{56,64},{64,7... | collective-permute-start | bytes 61448 | tf_op jit(solution)/shard_map/ppermute | solution.py:338
  4.2 5.6 %scan_in.2 = (bf16[256,1024]{1,0:T(8,128)(2,1)}, bf16[256,1024]{1,0:T(8,128)(2,1)}, bf16[256,128]{1,0:T(8,128)(2,1)S(1)}, bf16[256,128]{1,0:T(8,128)(2,1)S(1)}, ...) custom-call(f32[8]{0:T(128)} %rate_ref.7, bf16[512,1024]{1,0:T(8,128)(2,1)} %x_ref.5, bf16[512,1024]{1,0:T(8,128)(2,1)} %x_ref.5, ...), custom_call_target="tpu_custom_call" | custom-call | tf_op jit(solution)/shard_map/scan_in/pallas_call | solution.py:296
  9.8 5.8 %scan_in.3 = (bf16[256,1024]{1,0:T(8,128)(2,1)}, bf16[256,1024]{1,0:T(8,128)(2,1)}, bf16[256,128]{1,0:T(8,128)(2,1)S(1)}, bf16[256,128]{1,0:T(8,128)(2,1)S(1)}, bf16[16,16,1024]{2,1,0:T(8,128)(2,1)}) custom-call(f32[8]{0:T(128)} %rate_ref.7, bf16[512,1024]{1,0:T(8,128)(2,1)} %x_ref.5, bf16[8,1280]{1,0:T(8,128)(2,1)S(1)} %collective-permute-done.rim_ref.rimbc_ref, ...), custom_call_target="tpu_custom_call" | custom-call | tf_op jit(solution)/shard_map/scan_in/pallas_call | solution.py:296
  15.6 7.6 %all-to-all-start = ((bf16[16,16,1024]{2,1,0:T(8,128)(2,1)}), bf16[16,16,1024]{2,1,0:T(8,128)(2,1)S(1)}, u32[]{:S(2)}, u32[]{:S(2)}) async-start(bf16[16,16,1024]{2,1,0:T(8,128)(2,1)} %get-tuple-element.28), calls=%async_computation | async-start | bytes 1048576 | tf_op jit(solution)/shard_map/all_to_all | solution.py:344
  23.2 6.3 %local.1 = (f32[512,1024]{1,0:T(8,128)}, f32[512,1024]{1,0:T(8,128)}) custom-call(f32[8]{0:T(128)} %rate_ref.7, f32[8]{0:T(128)} %skip_ref.1, bf16[256,1024]{1,0:T(8,128)(2,1)} %get-tuple-element.29.xt0_ref, bf16[256,1024]{1,0:T(8,128)(2,1)} %get-tuple-element.30.xt1_ref, bf16[256,1024]{1,0:T(8,128)(2,1)} %get-tuple-element.31.xc0_ref, ...), custom_call_target="tpu_custom_call" | custom-call | flops 2147483648 | bytes 8388608 | tf_op jit(solution)/shard_map/local/pallas_call | solution.py:346
  29.5 5.0 %all-to-all-done.r_ref = bf16[16,16,1024]{2,1,0:T(8,128)(2,1)S(1)} async-done(((bf16[16,16,1024]{2,1,0:T(8,128)(2,1)}), bf16[16,16,1024]{2,1,0:T(8,128)(2,1)S(1)}, u32[]{:S(2)}, u32[]{:S(2)}) %all-to-all-start) | async-done | bytes 524320 | tf_op jit(solution)/shard_map/all_to_all | solution.py:344
  36.0 3.5 %all-to-all-start.1 = ((bf16[16,8,1024]{2,1,0:T(8,128)(2,1)}), bf16[16,8,1024]{2,1,0:T(8,128)(2,1)S(1)}, u32[]{:S(2)}, u32[]{:S(2)}) async-start(bf16[16,8,1024]{2,1,0:T(8,128)(2,1)} %prefix.1), calls=%async_computation.1 | async-start | bytes 524288 | tf_op jit(solution)/shard_map/all_to_all | solution.py:373
  39.6 8.7 %all-to-all-done.1.q_ref = bf16[16,8,1024]{2,1,0:T(8,128)(2,1)S(1)} async-done(((bf16[16,8,1024]{2,1,0:T(8,128)(2,1)}), bf16[16,8,1024]{2,1,0:T(8,128)(2,1)S(1)}, u32[]{:S(2)}, u32[]{:S(2)}) %all-to-all-start.1) | async-done | bytes 262176 | tf_op jit(solution)/shard_map/all_to_all | solution.py:373
  48.2 3.7 %norm.1.n_ref = bf16[512,1024]{1,0:T(8,128)(2,1)S(1)} custom-call(bf16[16,8,1024]{2,1,0:T(8,128)(2,1)S(1)} %all-to-all-done.1.q_ref, f32[512,1024]{1,0:T(8,128)} %get-tuple-element.37.after_ref.a1_ref, f32[512,1024]{1,0:T(8,128)} %get-tuple-element.38.a2_ref, bf16[256,128]{1,0:T(8,128)(2,1)S(1)} %get-tuple-element.35.c0_ref, ...), custom_call_target="tpu_custom_call" | custom-call | tf_op jit(solution)/shard_map/norm/pallas_call | solution.py:375
  52.0 2.8 %partial.3.after_ref = bf16[512,1024]{1,0:T(8,128)(2,1)S(1)} custom-call(s32[1]{0:T(128)} %bitcast.index_ref.after_ref, bf16[512,1024]{1,0:T(8,128)(2,1)S(1)} %norm.1.n_ref, bf16[1024,8192]{1,0:T(8,128)(2,1)} %w_ref.13, s32[1]{0:T(128)} %bitcast.index_ref.after_ref), custom_call_target="tpu_custom_call" | custom-call | tf_op jit(solution)/shard_map/partial/pallas_call | solution.py:247
  54.9 2.8 %partial.4.after_ref = bf16[512,1024]{1,0:T(8,128)(2,1)S(1)} custom-call(s32[1]{0:T(128)} %bitcast.index_ref.after_ref, bf16[512,1024]{1,0:T(8,128)(2,1)S(1)} %norm.1.n_ref, bf16[1024,8192]{1,0:T(8,128)(2,1)} %w_ref.13, bf16[512,1024]{1,0:T(8,128)(2,1)S(1)} %partial.3.after_ref), custom_call_target="tpu_custom_call" | custom-call | tf_op jit(solution)/shard_map/partial/pallas_call | solution.py:247
  58.2 2.8 %summed.4 = (bf16[512,512]{1,0:T(8,128)(2,1)S(1)}, bf16[512,512]{1,0:T(8,128)(2,1)S(1)}) custom-call(s32[1]{0:T(128)} %bitcast.index_ref.after_ref, bf16[512,1024]{1,0:T(8,128)(2,1)S(1)} %norm.1.n_ref, bf16[1024,8192]{1,0:T(8,128)(2,1)} %w_ref.13, bf16[512,1024]{1,0:T(8,128)(2,1)S(1)} %collective-permute-done.2.r_ref, bf16[512,1024]{1,0:T(8,128)(2,1)S(1)} %partial.4.after_ref), custom_call_target="tpu_custom_call" | custom-call | tf_op jit(solution)/shard_map/summed/pallas_call | solution.py:264
  61.0 2.8 %summed.5 = (bf16[512,512]{1,0:T(8,128)(2,1)S(1)}, bf16[512,512]{1,0:T(8,128)(2,1)S(1)}) custom-call(s32[1]{0:T(128)} %bitcast.index_ref.after_ref, bf16[512,1024]{1,0:T(8,128)(2,1)S(1)} %norm.1.n_ref, bf16[1024,8192]{1,0:T(8,128)(2,1)} %w_ref.13, bf16[512,1024]{1,0:T(8,128)(2,1)S(1)} %collective-permute-done.1.r_ref, ...), custom_call_target="tpu_custom_call" | custom-call | tf_op jit(solution)/shard_map/summed/pallas_call | solution.py:264
  63.8 4.8 %partial.5 = bf16[512,2048]{1,0:T(8,128)(2,1)S(1)} custom-call(s32[1]{0:T(128)} %bitcast.index_ref.after_ref, bf16[512,1024]{1,0:T(8,128)(2,1)S(1)} %norm.1.n_ref, bf16[1024,8192]{1,0:T(8,128)(2,1)} %w_ref.13, bf16[512,512]{1,0:T(8,128)(2,1)S(1)} %get-tuple-element.40.after_ref), custom_call_target="tpu_custom_call" | custom-call | tf_op jit(solution)/shard_map/partial/pallas_call | solution.py:247
  68.8 3.0 %collective-permute-start.5 = (bf16[512,512]{1,0:T(8,128)(2,1)S(1)}, bf16[512,512]{1,0:T(8,128)(2,1)S(1)}, u32[]{:S(2)}, u32[]{:S(2)}) collective-permute-start(bf16[512,512]{1,0:T(8,128)(2,1)S(1)} %get-tuple-element.41), channel_id=1, source_target_pairs={{0,6},{1,7},{2,0},{3,1},{4,2},{5,3},{6,4},{7,5},{8,14},{9,15},{10,... | collective-permute-start | bytes 1572872 | tf_op jit(solution)/shard_map/ppermute | solution.py:399
  72.4 2.7 %collective-permute-start.6 = (bf16[512,512]{1,0:T(8,128)(2,1)S(1)}, bf16[512,512]{1,0:T(8,128)(2,1)S(1)}, u32[]{:S(2)}, u32[]{:S(2)}) collective-permute-start(bf16[512,512]{1,0:T(8,128)(2,1)S(1)} %get-tuple-element.43), channel_id=1, source_target_pairs={{0,6},{1,7},{2,0},{3,1},{4,2},{5,3},{6,4},{7,5},{8,14},{9,15},{10,... | collective-permute-start | bytes 1572872 | tf_op jit(solution)/shard_map/ppermute | solution.py:402
  75.1 9.0 %collective-permute-done.5.refs_1_ = bf16[512,512]{1,0:T(8,128)(2,1)S(1)} collective-permute-done((bf16[512,512]{1,0:T(8,128)(2,1)S(1)}, bf16[512,512]{1,0:T(8,128)(2,1)S(1)}, u32[]{:S(2)}, u32[]{:S(2)}) %collective-permute-start.5) | collective-permute-done | bytes 524320 | tf_op jit(solution)/shard_map/ppermute | solution.py:399
  84.1 3.7 %collective-permute-done.4.refs_0_ = bf16[512,512]{1,0:T(8,128)(2,1)S(1)} collective-permute-done((bf16[512,512]{1,0:T(8,128)(2,1)S(1)}, bf16[512,512]{1,0:T(8,128)(2,1)S(1)}, u32[]{:S(2)}, u32[]{:S(2)}) %collective-permute-start.4) | collective-permute-done | bytes 524320 | tf_op jit(solution)/shard_map/ppermute | solution.py:398
  87.8 2.8 %summed.6 = (bf16[512,512]{1,0:T(8,128)(2,1)S(1)}, bf16[512,512]{1,0:T(8,128)(2,1)S(1)}) custom-call(s32[1]{0:T(128)} %bitcast.index_ref.after_ref, bf16[512,1024]{1,0:T(8,128)(2,1)S(1)} %norm.1.n_ref, bf16[1024,8192]{1,0:T(8,128)(2,1)} %w_ref.13, bf16[512,2048]{1,0:T(8,128)(2,1)S(1)} %collective-permute-done.3.r_ref, s32[1]{0:T(128)} %bitcast.index_ref.after_ref, ...), custom_call_target="tpu_custom_call" | custom-call | tf_op jit(solution)/shard_map/summed/pallas_call | solution.py:264
  92.7 2.6 %collective-permute-done.6.refs_0_ = bf16[512,512]{1,0:T(8,128)(2,1)S(1)} collective-permute-done((bf16[512,512]{1,0:T(8,128)(2,1)S(1)}, bf16[512,512]{1,0:T(8,128)(2,1)S(1)}, u32[]{:S(2)}, u32[]{:S(2)}) %collective-permute-start.6) | collective-permute-done | bytes 524320 | tf_op jit(solution)/shard_map/ppermute | solution.py:402
  95.3 3.7 %collective-permute-done.7.refs_1_ = bf16[512,512]{1,0:T(8,128)(2,1)S(1)} collective-permute-done((bf16[512,512]{1,0:T(8,128)(2,1)S(1)}, bf16[512,512]{1,0:T(8,128)(2,1)S(1)}, u32[]{:S(2)}, u32[]{:S(2)}) %collective-permute-start.7) | collective-permute-done | bytes 524320 | tf_op jit(solution)/shard_map/ppermute | solution.py:401
  99.0 2.7 %summed.7 = (f32[512,512]{1,0:T(8,128)S(1)}, f32[512,512]{1,0:T(8,128)S(1)}) custom-call(s32[1]{0:T(128)} %bitcast.index_ref.after_ref, bf16[512,1024]{1,0:T(8,128)(2,1)S(1)} %norm.1.n_ref, bf16[1024,8192]{1,0:T(8,128)(2,1)} %w_ref.13, bf16[512,2048]{1,0:T(8,128)(2,1)S(1)} %collective-permute-done.3.r_ref, bf16[512,512]{1,0:T(8,128)(2,1)S(1)} %get-tuple-element.42.after_ref, ...), custom_call_target="tpu_custom_call" | custom-call | tf_op jit(solution)/shard_map/summed/pallas_call | solution.py:264
  101.8 4.3 %collective-permute-done.9.b_ref = bf16[512,512]{1,0:T(8,128)(2,1)S(1)} collective-permute-done((bf16[512,512]{1,0:T(8,128)(2,1)S(1)}, bf16[512,512]{1,0:T(8,128)(2,1)S(1)}, u32[]{:S(2)}, u32[]{:S(2)}) %collective-permute-start.9) | collective-permute-done | bytes 524320 | tf_op jit(solution)/shard_map/ppermute | solution.py:406
  106.1 3.4 %collective-permute-done.8.a_ref = bf16[512,512]{1,0:T(8,128)(2,1)S(1)} collective-permute-done((bf16[512,512]{1,0:T(8,128)(2,1)S(1)}, bf16[512,512]{1,0:T(8,128)(2,1)S(1)}, u32[]{:S(2)}, u32[]{:S(2)}) %collective-permute-start.8) | collective-permute-done | bytes 524320 | tf_op jit(solution)/shard_map/ppermute | solution.py:405
  (14 shorter events, 6.9 us)
Async XLA Ops:
  0.7 9.1 %collective-permute-start = (bf16[8,1280]{1,0:T(8,128)(2,1)S(1)}, bf16[8,1280]{1,0:T(8,128)(2,1)S(1)}, u32[]{:S(2)}, u32[]{:S(2)}) collective-permute-start(bf16[8,1280]{1,0:T(8,128)(2,1)S(1)} %rim.1), channel_id=1, source_target_pairs={{0,8},{8,16},{16,24},{24,32},{32,40},{40,48},{48,56},{56,64},{64,7... | collective-permute-start | bytes 61448 | tf_op jit(solution)/shard_map/ppermute | solution.py:338
  15.6 18.9 %all-to-all-start = ((bf16[16,16,1024]{2,1,0:T(8,128)(2,1)}), bf16[16,16,1024]{2,1,0:T(8,128)(2,1)S(1)}, u32[]{:S(2)}, u32[]{:S(2)}) async-start(bf16[16,16,1024]{2,1,0:T(8,128)(2,1)} %get-tuple-element.28), calls=%async_computation | async-start | bytes 1048576 | tf_op jit(solution)/shard_map/all_to_all | solution.py:344
  36.0 12.2 %all-to-all-start.1 = ((bf16[16,8,1024]{2,1,0:T(8,128)(2,1)}), bf16[16,8,1024]{2,1,0:T(8,128)(2,1)S(1)}, u32[]{:S(2)}, u32[]{:S(2)}) async-start(bf16[16,8,1024]{2,1,0:T(8,128)(2,1)} %prefix.1), calls=%async_computation.1 | async-start | bytes 524288 | tf_op jit(solution)/shard_map/all_to_all | solution.py:373
  54.8 3.4 %collective-permute-start.2 = (bf16[512,1024]{1,0:T(8,128)(2,1)S(1)}, bf16[512,1024]{1,0:T(8,128)(2,1)S(1)}, u32[]{:S(2)}, u32[]{:S(2)}) collective-permute-start(bf16[512,1024]{1,0:T(8,128)(2,1)S(1)} %partial.3.after_ref), channel_id=1, source_target_pairs={{0,1},{1,0},{2,3},{3,2},{4,5},{5,4},{6,7},{7,6},{8,9},{9,8},{10,11... | collective-permute-start | bytes 3145736 | tf_op jit(solution)/shard_map/ppermute | solution.py:394
  57.7 3.3 %collective-permute-start.1 = (bf16[512,1024]{1,0:T(8,128)(2,1)S(1)}, bf16[512,1024]{1,0:T(8,128)(2,1)S(1)}, u32[]{:S(2)}, u32[]{:S(2)}) collective-permute-start(bf16[512,1024]{1,0:T(8,128)(2,1)S(1)} %partial.4.after_ref), channel_id=1, source_target_pairs={{0,1},{1,0},{2,3},{3,2},{4,5},{5,4},{6,7},{7,6},{8,9},{9,8},{10,11... | collective-permute-start | bytes 3145736 | tf_op jit(solution)/shard_map/ppermute | solution.py:396
  68.6 19.2 %collective-permute-start.3 = (bf16[512,2048]{1,0:T(8,128)(2,1)S(1)}, bf16[512,2048]{1,0:T(8,128)(2,1)S(1)}, u32[]{:S(2)}, u32[]{:S(2)}) collective-permute-start(bf16[512,2048]{1,0:T(8,128)(2,1)S(1)} %partial.5), channel_id=1, source_target_pairs={{0,1},{1,0},{2,3},{3,2},{4,5},{5,4},{6,7},{7,6},{8,9},{9,8},{10,11... | collective-permute-start | bytes 6291464 | tf_op jit(solution)/shard_map/ppermute | solution.py:403
  68.8 15.3 %collective-permute-start.5 = (bf16[512,512]{1,0:T(8,128)(2,1)S(1)}, bf16[512,512]{1,0:T(8,128)(2,1)S(1)}, u32[]{:S(2)}, u32[]{:S(2)}) collective-permute-start(bf16[512,512]{1,0:T(8,128)(2,1)S(1)} %get-tuple-element.41), channel_id=1, source_target_pairs={{0,6},{1,7},{2,0},{3,1},{4,2},{5,3},{6,4},{7,5},{8,14},{9,15},{10,... | collective-permute-start | bytes 1572872 | tf_op jit(solution)/shard_map/ppermute | solution.py:399
  71.8 16.0 %collective-permute-start.4 = (bf16[512,512]{1,0:T(8,128)(2,1)S(1)}, bf16[512,512]{1,0:T(8,128)(2,1)S(1)}, u32[]{:S(2)}, u32[]{:S(2)}) collective-permute-start(bf16[512,512]{1,0:T(8,128)(2,1)S(1)} %get-tuple-element.39.after_ref), channel_id=1, source_target_pairs={{0,2},{1,3},{2,4},{3,5},{4,6},{5,7},{6,0},{7,1},{8,10},{9,11},{10,... | collective-permute-start | bytes 1572872 | tf_op jit(solution)/shard_map/ppermute | solution.py:398
  71.8 27.2 %collective-permute-start.7 = (bf16[512,512]{1,0:T(8,128)(2,1)S(1)}, bf16[512,512]{1,0:T(8,128)(2,1)S(1)}, u32[]{:S(2)}, u32[]{:S(2)}) collective-permute-start(bf16[512,512]{1,0:T(8,128)(2,1)S(1)} %get-tuple-element.40.after_ref), channel_id=1, source_target_pairs={{0,2},{1,3},{2,4},{3,5},{4,6},{5,7},{6,0},{7,1},{8,10},{9,11},{10,... | collective-permute-start | bytes 1572872 | tf_op jit(solution)/shard_map/ppermute | solution.py:401
  72.4 22.9 %collective-permute-start.6 = (bf16[512,512]{1,0:T(8,128)(2,1)S(1)}, bf16[512,512]{1,0:T(8,128)(2,1)S(1)}, u32[]{:S(2)}, u32[]{:S(2)}) collective-permute-start(bf16[512,512]{1,0:T(8,128)(2,1)S(1)} %get-tuple-element.43), channel_id=1, source_target_pairs={{0,6},{1,7},{2,0},{3,1},{4,2},{5,3},{6,4},{7,5},{8,14},{9,15},{10,... | collective-permute-start | bytes 1572872 | tf_op jit(solution)/shard_map/ppermute | solution.py:402
  90.6 15.4 %collective-permute-start.9 = (bf16[512,512]{1,0:T(8,128)(2,1)S(1)}, bf16[512,512]{1,0:T(8,128)(2,1)S(1)}, u32[]{:S(2)}, u32[]{:S(2)}) collective-permute-start(bf16[512,512]{1,0:T(8,128)(2,1)S(1)} %get-tuple-element.46), channel_id=1, source_target_pairs={{0,6},{1,7},{2,0},{3,1},{4,2},{5,3},{6,4},{7,5},{8,14},{9,15},{10,... | collective-permute-start | bytes 1572872 | tf_op jit(solution)/shard_map/ppermute | solution.py:406
  90.7 18.8 %collective-permute-start.8 = (bf16[512,512]{1,0:T(8,128)(2,1)S(1)}, bf16[512,512]{1,0:T(8,128)(2,1)S(1)}, u32[]{:S(2)}, u32[]{:S(2)}) collective-permute-start(bf16[512,512]{1,0:T(8,128)(2,1)S(1)} %get-tuple-element.42.after_ref), channel_id=1, source_target_pairs={{0,2},{1,3},{2,4},{3,5},{4,6},{5,7},{6,0},{7,1},{8,10},{9,11},{10,... | collective-permute-start | bytes 1572872 | tf_op jit(solution)/shard_map/ppermute | solution.py:405

commit v3 on v2

v3 whole, which is shorter than its diff:
```python
import functools

import jax
import jax.numpy as jnp
from jax import lax
from jax.experimental import pallas as pl
from jax.experimental.pallas import tpu as pltpu
from jax.sharding import PartitionSpec as P

BF = jnp.bfloat16
F32 = jnp.float32
TOK = 512
HT = TOK // 2
WID = 1024
HALF = WID // 2
HEADS = 8
HW = 128
ST = 128
CTX = 16
CB = 512
NB = WID // CB
SEQ = TOK * CTX
DECAY = 12.288 / SEQ / 63.0
SCALE = 1.0 / (ST * SEQ) ** 0.5
ROWS = 32
SD = jax.ShapeDtypeStruct


def silu(v):
    half = 0.5 * v
    return half + half * jnp.tanh(half)


def mm(a, b):
    return jnp.dot(a, b, preferred_element_type=F32)


def triangle(first, rows, count):
    row = lax.broadcasted_iota(jnp.int32, (rows, count), 0) + first
    col = lax.broadcasted_iota(jnp.int32, (rows, count), 1)
    return jnp.where(row >= col, 1.0, 0.0).astype(BF)


def head_row(ref, factor):
    lane = lax.broadcasted_iota(jnp.int32, (1, HW), 1)
    row = jnp.zeros((1, HW), F32)
    for h in range(HEADS):
        row = jnp.where(lane == h, ref[h] * factor, row)
    return row


def spread(compact, head, rows=None):
    column = compact[:, head : head + 1]
    return jnp.broadcast_to(column, (compact.shape[0], HW))


def conv_part(xe, w_ref, bias_ref, r, lo, hi):
    total = bias_ref[:, lo:hi]
    for k in range(4):
        total = total + w_ref[k : k + 1, lo:hi] * xe[5 + k + r : 5 + k + r + ROWS, lo:hi]
    return silu(total)


def rim_body(x_ref, bc_ref, o_ref):
    o_ref[:, :WID] = x_ref[...]
    o_ref[:, WID:] = bc_ref[...]


def scan_in_body(
    last, rate_ref, x_ref, rim_ref, bc_ref, rimbc_ref, codes_ref, cx_ref, bx_ref, cbc_ref, bbc_ref, *refs
):
    if last:
        xc_ref, xt_ref, b_ref, c_ref, cum_ref, state_ref, xe, be = refs
    else:
        earlier_ref, later_ref, xc_ref, xt_ref, b_ref, c_ref, cum_ref, msg_ref, xe, be = refs
    be[0:8, :] = rimbc_ref[...].astype(F32)[-8:, :]
    be[8 : 8 + HT, :] = bc_ref[...].astype(F32)
    xe[0:8, :] = rim_ref[...].astype(F32)[-8:, :]
    xe[8 : 8 + HT, :] = x_ref[...].astype(F32)
    codes = jnp.concatenate([codes_ref[...].astype(F32), jnp.zeros((HW - HEADS, TOK), F32)], axis=0)
    first = HT if last else 0
    cum = lax.dot_general(
        triangle(first, HT, TOK), codes.astype(BF), (((1,), (1,)), ((), ())), preferred_element_type=F32
    )
    cum_ref[...] = cum
    grow = jnp.exp(head_row(rate_ref, DECAY) * cum)
    for r in range(0, HT, ROWS):
        b_ref[r : r + ROWS, :] = conv_part(be, cbc_ref, bbc_ref, r, 0, ST).astype(BF)
        c_ref[r : r + ROWS, :] = conv_part(be, cbc_ref, bbc_ref, r, ST, 2 * ST).astype(BF)
    bt = b_ref[...].astype(F32).T.astype(BF)
    for r in range(0, HT, ROWS):
        for h in range(HEADS):
            lo, hi = h * HW, (h + 1) * HW
            xc = conv_part(xe, cx_ref, bx_ref, r, lo, hi).astype(BF)
            xc_ref[r : r + ROWS, lo:hi] = xc
            scaled = xc.astype(F32) * spread(grow[r : r + ROWS, :], h)
            xt_ref[r : r + ROWS, lo:hi] = scaled.astype(BF)
    if last:
        state_ref[...] = mm(bt, xt_ref[...])
        return
    state = mm(bt, xt_ref[...]) + earlier_ref[...]
    total = later_ref[7:8, :]
    high = jnp.floor(total * (1.0 / 256.0))
    low = total - 256.0 * high
    row = lax.broadcasted_iota(jnp.int32, (8, HW), 0)
    pair = jnp.where(row == 0, high, jnp.where(row == 1, low, 0.0))
    extra = jnp.concatenate([spread(pair, h) for h in range(HEADS)], axis=1)
    for j in range(CTX):
        part = jnp.concatenate([state[8 * j : 8 * j + 8, :], extra], axis=0)
        msg_ref[j] = part.astype(BF)


def local_body(
    rate_ref, skip_ref, xt0_ref, xt1_ref, xc0_ref, xc1_ref, z_ref, cum0_ref, cum1_ref, b0_ref, b1_ref, c0_ref,
    c1_ref, a1_ref, a2_ref, gram, prod,
):
    for r in range(0, TOK, HW):
        c_ref = c0_ref if r < HT else c1_ref
        rows = c_ref[r % HT : r % HT + HW, :]
        row = lax.broadcasted_iota(jnp.int32, (HW, HT), 0) + r
        col = lax.broadcasted_iota(jnp.int32, (HW, HT), 1)
        for k, b_ref in enumerate((b0_ref, b1_ref)):
            part = lax.dot_general(rows, b_ref[...], (((1,), (1,)), ((), ())), preferred_element_type=F32)
            gram[r : r + HW, k * HT : (k + 1) * HT] = jnp.where(row >= col + k * HT, part, 0.0).astype(BF)
    prod[0:HT, :] = mm(gram[0:HT, 0:HT], xt0_ref[...])
    prod[HT:TOK, :] = mm(gram[HT:TOK, 0:HT], xt0_ref[...]) + mm(gram[HT:TOK, HT:TOK], xt1_ref[...])
    rate = head_row(rate_ref, -DECAY)
    for r in range(0, TOK, ROWS):
        cum_ref, xc_ref, p = (cum0_ref, xc0_ref, r) if r < HT else (cum1_ref, xc1_ref, r - HT)
        fades = SCALE * jnp.exp(rate * cum_ref[p : p + ROWS, :])
        for h in range(HEADS):
            lo, hi = h * HW, (h + 1) * HW
            gate = silu(z_ref[r : r + ROWS, lo:hi].astype(F32))
            fade = spread(fades, h)
            xc = xc_ref[p : p + ROWS, lo:hi].astype(F32)
            both = (prod[r : r + ROWS, lo:hi] * fade + skip_ref[h] * xc) * gate
            a1_ref[r : r + ROWS, lo:hi] = both.astype(BF)
            a2_ref[r : r + ROWS, lo:hi] = (fade * gate).astype(BF)


def prefix_body(rate_ref, r_ref, after_ref, q_ref):
    rate = jnp.concatenate([jnp.full((1, HW), rate_ref[h] * -DECAY, F32) for h in range(HEADS)], axis=1)
    state = jnp.zeros((8, WID), F32)
    for c in range(CTX):
        q_ref[c] = state.astype(BF)
        got = r_ref[c].astype(F32)
        total = 256.0 * got[8:9, :] + got[9:10, :]
        state = jnp.exp(rate * total) * (state + got[0:8, :])


def norm_body(q_ref, a1_ref, a2_ref, c0_ref, c1_ref, gain_ref, n_ref, prod):
    state = q_ref[...].astype(F32).reshape(ST, CB).astype(BF)
    prod[0:HT, :] = mm(c0_ref[...], state)
    prod[HT:TOK, :] = mm(c1_ref[...], state)
    for r in range(0, TOK, ROWS):
        for h in range(0, CB, HW):
            rs, hs = slice(r, r + ROWS), slice(h, h + HW)
            gated = a1_ref[rs, hs].astype(F32) + a2_ref[rs, hs].astype(F32) * prod[rs, hs]
            power = jnp.mean(gated * gated, axis=-1, keepdims=True)
            n_ref[rs, hs] = (gated * lax.rsqrt(power + 1e-05) * gain_ref[:, hs]).astype(BF)


def project_body(adds, place_ref, own_ref, sib_ref, w_ref, ws_ref, *refs):
    step = pl.program_id(0)
    outs = refs[-2:]
    for k in range(2):

        @pl.when(step // 2 == k)
        def _():
            total = mm(own_ref[...], w_ref[...]) + mm(sib_ref[...], ws_ref[...])
            for ref in refs[adds * k : adds * (k + 1)]:
                total = total + ref[...].astype(F32)
            outs[k][...] = total.astype(outs[k].dtype)


def final_body(m0_ref, m1_ref, a_ref, b_ref, o_ref):
    o_ref[:, :HALF] = (m0_ref[...] + a_ref[...].astype(F32)).astype(BF)
    o_ref[:, HALF:] = (m1_ref[...] + b_ref[...].astype(F32)).astype(BF)


def params(dims=1):
    return pltpu.CompilerParams(
        dimension_semantics=("arbitrary",) * dims if dims else None, vmem_limit_bytes=20 << 20
    )


SMEM = pl.BlockSpec(memory_space=pltpu.SMEM)
VMEM = pl.BlockSpec(memory_space=pltpu.VMEM)
ANY = pl.BlockSpec(memory_space=pl.ANY)


def whole(*shape):
    return pl.BlockSpec(shape, lambda i: (0,) * len(shape))


def cols(rows, at=0):
    return pl.BlockSpec((rows, CB), lambda i: (at, i))


def in_hbm(a):
    return pltpu.with_memory_space_constraint(a, pltpu.HBM)


QUART = HALF // 2


def project(place, normed, sibling, w, w_sib, targets, addends, kind):
    def column(i, place_ref):
        index = place_ref[0]
        far = jnp.where(i < 2, targets[0][0], targets[1][0])
        side = jnp.where(i < 2, targets[0][1], targets[1][1])
        return 0, ((((index >> 1) + far) & 3) * 2 + (index & 1)) * 4 + side * 2 + (i & 1)

    whole2 = pl.BlockSpec((TOK, WID), lambda i, ix: (0, 0))
    weight = pl.BlockSpec((WID, QUART), column)
    halves = [
        pl.BlockSpec((TOK, QUART), lambda i, ix: (0, jnp.minimum(i, 1))),
        pl.BlockSpec((TOK, QUART), lambda i, ix: (0, jnp.maximum(i - 2, 0))),
    ]
    count = len(addends[0])
    return pl.pallas_call(
        functools.partial(project_body, count),
        out_shape=[SD((TOK, HALF), kind)] * 2,
        grid_spec=pltpu.PrefetchScalarGridSpec(
            num_scalar_prefetch=1,
            grid=(4,),
            in_specs=[whole2, whole2, weight, weight] + [halves[0]] * count + [halves[1]] * count,
            out_specs=halves,
        ),
        compiler_params=params(),
        name="project",
    )(place, normed, sibling, w, w_sib, *addends[0], *addends[1])


def scan_in(last, rate, x_in, rim, bc_in, codes, conv_x, bias_x, conv_bc, bias_bc, *carry):
    at = 1 if last else 0
    if last:
        rims = [pl.BlockSpec((16, WID), lambda i: (15, 0)), pl.BlockSpec((16, 2 * ST), lambda i: (15, 0))]
        rim_args = (x_in, bc_in)
        extra_out = [SD((ST, WID), F32)]
    else:
        rims = [whole(8, WID), pl.BlockSpec((8, 2 * ST), lambda i: (0, WID // (2 * ST)))]
        rim_args = (rim, rim)
        extra_out = [SD((CTX, 16, WID), BF)]
    V = pltpu.HBM
    outs = [V((HT, WID), BF), V((HT, WID), BF), V((HT, ST), BF), V((HT, ST), BF), V((HT, HW), F32)]
    outs = outs + extra_out
    return pl.pallas_call(
        functools.partial(scan_in_body, last),
        grid=(1,),
        in_specs=[
            SMEM, pl.BlockSpec((HT, WID), lambda i: (at, 0)), rims[0],
            pl.BlockSpec((HT, 2 * ST), lambda i: (at, 0)), rims[1],
            whole(HEADS, TOK), whole(4, WID), whole(1, WID), whole(4, 2 * ST), whole(1, 2 * ST),
        ]
        + ([] if last else [whole(ST, WID), pl.BlockSpec((8, HW), lambda i: (HT // 8 - 1, 0))]),
        out_specs=[whole(*o.shape) for o in outs],
        out_shape=outs,
        scratch_shapes=[pltpu.VMEM((HT + 8, WID), F32), pltpu.VMEM((HT + 8, 2 * ST), F32)],
        compiler_params=params(),
        name="scan_in",
    )(rate, x_in, rim_args[0], bc_in, rim_args[1], codes, conv_x, bias_x, conv_bc, bias_bc, *carry)


def body(
    x_in, bc_in, z_in, codes, head_rate, conv_x, conv_bc, bias_x, bias_bc, skip, norm_gain, w_out
):
    place = lax.axis_index("tp")
    where = jnp.full((1,), place, jnp.int32)
    x_in, bc_in, z_in, w_out = in_hbm(x_in), in_hbm(bc_in), in_hbm(z_in), in_hbm(w_out)
    codes, conv_x, conv_bc = in_hbm(codes.T), in_hbm(conv_x), in_hbm(conv_bc)
    head_rate, skip = in_hbm(head_rate), in_hbm(skip)
    bias_x, bias_bc, gain = in_hbm(bias_x[None, :]), in_hbm(bias_bc[None, :]), in_hbm(norm_gain[None, :])

    swap = [(s, s ^ 1) for s in range(8)]
    w_sib = in_hbm(lax.ppermute(w_out, "tp", swap))
    rim = pl.pallas_call(
        rim_body,
        grid=(1,),
        in_specs=[
            pl.BlockSpec((8, WID), lambda i: (TOK // 8 - 1, 0)),
            pl.BlockSpec((8, 2 * ST), lambda i: (TOK // 8 - 1, 0)),
        ],
        out_specs=whole(8, WID + 2 * ST),
        out_shape=SD((8, WID + 2 * ST), BF),
        compiler_params=params(),
        name="rim",
    )(x_in, bc_in)
    rim = lax.ppermute(rim, "ctx", [(s, s + 1) for s in range(CTX - 1)])

    shared = (codes, conv_x, bias_x, conv_bc, bias_bc)
    xc1, xt1, b1, c1, cum1, state1 = scan_in(True, head_rate, x_in, None, bc_in, *shared)
    xc0, xt0, b0, c0, cum0, msg = scan_in(False, head_rate, x_in, rim, bc_in, *shared, state1, in_hbm(cum1))

    xt0, xt1, xc0, xc1, cum0, cum1, b0, b1, c0, c1 = map(
        in_hbm, (xt0, xt1, xc0, xc1, cum0, cum1, b0, b1, c0, c1)
    )
    got = lax.all_to_all(msg, "ctx", 0, 0, tiled=True)

    a1, a2 = pl.pallas_call(
        local_body,
        grid=(1,),
        in_specs=[
            SMEM, SMEM, whole(HT, WID), whole(HT, WID), whole(HT, WID), whole(HT, WID), whole(TOK, WID),
            whole(HT, HW), whole(HT, HW), whole(HT, ST), whole(HT, ST), whole(HT, ST), whole(HT, ST),
        ],
        out_specs=[whole(TOK, WID), whole(TOK, WID)],
        out_shape=[pltpu.HBM((TOK, WID), BF)] * 2,
        scratch_shapes=[pltpu.VMEM((TOK, TOK), BF), pltpu.VMEM((TOK, WID), F32)],
        compiler_params=params(),
        cost_estimate=pl.CostEstimate(flops=2 << 30, transcendentals=1 << 20, bytes_accessed=8 << 20),
        name="local",
    )(head_rate, skip, xt0, xt1, xc0, xc1, z_in, cum0, cum1, b0, b1, c0, c1)
    a1, a2 = in_hbm(a1), in_hbm(a2)

    prefix = pl.pallas_call(
        prefix_body,
        in_specs=[SMEM, VMEM, ANY],
        out_specs=VMEM,
        out_shape=SD((CTX, 8, WID), BF),
        compiler_params=params(0),
        name="prefix",
    )(head_rate, got, a1)
    incoming = lax.all_to_all(prefix, "ctx", 0, 0, tiled=True)

    normed = pl.pallas_call(
        norm_body,
        grid=(NB,),
        in_specs=[
            pl.BlockSpec((CTX, 8, CB), lambda i: (0, 0, i)), cols(TOK), cols(TOK), whole(HT, ST),
            whole(HT, ST), cols(1),
        ],
        out_specs=cols(TOK),
        out_shape=SD((TOK, WID), BF),
        scratch_shapes=[pltpu.VMEM((TOK, CB), F32)],
        compiler_params=params(),
        name="norm",
    )(incoming, a1, a2, c0, c1, gain)

    up = [(s, (s + 2) % 8) for s in range(8)]
    down = [(s, (s + 6) % 8) for s in range(8)]
    sibling = lax.ppermute(normed, "tp", swap)
    run = functools.partial(project, where, normed, sibling, w_out, w_sib)
    far_l, far_r = run(((2, 0), (2, 1)), ((), ()), BF)
    far_l, far_r = lax.ppermute(far_l, "tp", up), lax.ppermute(far_r, "tp", down)
    above_r, below_l = run(((1, 1), (3, 0)), ((), ()), BF)
    from_r, from_l = lax.ppermute(above_r, "tp", up), lax.ppermute(below_l, "tp", down)
    above_l, below_r = run(((1, 0), (3, 1)), ((far_l,), (far_r,)), BF)
    last_l, last_r = lax.ppermute(above_l, "tp", up), lax.ppermute(below_r, "tp", down)
    here_l, here_r = run(((0, 0), (0, 1)), ((from_l,), (from_r,)), F32)
    return pl.pallas_call(
        final_body,
        in_specs=[VMEM] * 4,
        out_specs=VMEM,
        out_shape=SD((TOK, WID), BF),
        compiler_params=params(0),
        name="final",
    )(here_l, here_r, last_l, last_r)


def solution(mesh):
    in_specs = (
        P("ctx", "tp"),
        P("ctx", None),
        P("ctx", "tp"),
        P("ctx", "tp"),
        P("tp"),
        P(None, "tp"),
        P(),
        P("tp"),
        P(),
        P("tp"),
        P("tp"),
        P("tp", None),
    )
    out_specs = P("ctx", "tp")
    return jax.shard_map(body, mesh=mesh, in_specs=in_specs, out_specs=out_specs, check_vma=False)
```

time: 112 us -> 95.3 us (0.85)
  waiting for transfers between devices: 40.3 us -> 24.4 us
  blocking collectives: 0 us -> 11.6 us
  Pallas kernels: 46.4 us -> 38.5 us
  starting transfers between devices: 23.8 us -> 19.8 us
    all_to_all x0 -> x1, blocking collectives: none -> 11.6 us  [body(): incoming = lax.all_to_all(prefix, 'ctx', 0, 0, tiled=True)]
    ppermute x9 -> x8, waiting for transfers between devices: 26.7 us -> 17.1 us  [the longest x1 5.8 us: body(): lax.ppermute(far_l, 'tp', up)]
    all_to_all x1 -> x0, waiting for transfers between devices: 8.65 us -> none  [body(): incoming = lax.all_to_all(prefix, 'ctx', 0, 0, tiled=True)]
    pallas_call x10 -> x7, Pallas kernels: 39.3 us -> 33.2 us  [the longest x4 19.5 us: project(): pl.pallas_call(functools.partial(project_body, count), out_shape=[SD((TOK...]
    all_to_all x1 -> x0, starting transfers between devices: 3.53 us -> none  [body(): incoming = lax.all_to_all(prefix, 'ctx', 0, 0, tiled=True)]
    all_to_all x1, waiting for transfers between devices: 4.95 us -> 7.37 us  [body(): got = lax.all_to_all(msg, 'ctx', 0, 0, tiled=True)]
    pallas_call x1, Pallas kernels: 3.74 us -> 2.44 us  [body(): pl.pallas_call(norm_body, grid=(NB,), in_specs=[pl.BlockSpec((CTX, 8, CB)...]
    ppermute x9 -> x8, starting transfers between devices: 9.17 us -> 8.79 us  [the longest x1 1.87 us: body(): lax.ppermute(below_l, 'tp', down)]
  transfers between devices with their start and end apart: 12 -> 10, of which waited for: 8 -> 6; matrix products, arithmetic and copies ran while one was open for 0% -> 0% of each run, Pallas kernels for 21% -> 34%
where the time goes in v3:
time: 95.3 us; the launch traced here: 94.4 us
  Pallas kernels  38.5 us (40%)
  waiting for transfers between devices  24.4 us (26%)
  starting transfers between devices  19.8 us (21%)
  blocking collectives  11.6 us (12%)
    pallas_call x4, Pallas kernels, project(): pl.pallas_call(functools.partial(project_body, count), out_shape=[SD((TOK...  19.5 us
    all_to_all x1, blocking collectives, body(): incoming = lax.all_to_all(prefix, 'ctx', 0, 0, tiled=True)  11.6 us
    pallas_call x2, Pallas kernels, scan_in(): pl.pallas_call(functools.partial(scan_in_body, last), grid=(1,), in_specs...  9.21 us
    all_to_all x1, starting transfers between devices, body(): got = lax.all_to_all(msg, 'ctx', 0, 0, tiled=True)  7.59 us
    all_to_all x1, waiting for transfers between devices, body(): got = lax.all_to_all(msg, 'ctx', 0, 0, tiled=True)  7.37 us
    ppermute x1, waiting for transfers between devices, body(): lax.ppermute(far_l, 'tp', up)  5.8 us
    ppermute x1, waiting for transfers between devices, body(): lax.ppermute(above_l, 'tp', up)  5.14 us
    pallas_call x1, Pallas kernels, body(): pl.pallas_call(local_body, grid=(1,), in_specs=[SMEM, SMEM, whole(HT, WID...  4.55 us
  transfers between devices with their start and end apart: 10, of which 6 were waited for; matrix products, arithmetic and copies ran while one was open for 0% of the time, Pallas kernels for 34%

profile of v3, /device:TPU:0, one launch (start us, length us, event | category | flops | bytes accessed | tf_op | source)
XLA Modules:
  0.0 94.4 jit_solution(8275101194200234594)
XLA Ops:
  0.0 0.7 rim.1
  0.7 3.5 %collective-permute-start = (bf16[8,1280]{1,0:T(8,128)(2,1)S(1)}, bf16[8,1280]{1,0:T(8,128)(2,1)S(1)}, u32[]{:S(2)}, u32[]{:S(2)}) collective-permute-start(bf16[8,1280]{1,0:T(8,128)(2,1)S(1)} %rim.1), channel_id=1, source_target_pairs={{0,8},{8,16},{16,24},{24,32},{32,40},{40,48},{48,56},{56,64},{64,7... | collective-permute-start | bytes 61448 | tf_op jit(solution)/shard_map/ppermute | solution.py:289
  4.2 4.5 %scan_in.2 = (bf16[256,1024]{1,0:T(8,128)(2,1)}, bf16[256,1024]{1,0:T(8,128)(2,1)}, bf16[256,128]{1,0:T(8,128)(2,1)}, bf16[256,128]{1,0:T(8,128)(2,1)}, f32[256,128]{1,0:T(8,128)}, /*index=5*/f32[128,1024]{1,0:T(8,128)S(1)}) custom-call(f32[8]{0:T(128)} %rate_ref.7, bf16[512,1024]{1,0:T(8,128)(2,1)} %x_ref.5, bf16[512,1024]{1,0:T(8,128)(2,1)} %x_ref.5, ...), custom_call_target="tpu_custom_call" | custom-call | tf_op jit(solution)/shard_map/scan_in/pallas_call | solution.py:248
  8.7 4.7 %scan_in.3 = (bf16[256,1024]{1,0:T(8,128)(2,1)}, bf16[256,1024]{1,0:T(8,128)(2,1)}, bf16[256,128]{1,0:T(8,128)(2,1)}, bf16[256,128]{1,0:T(8,128)(2,1)}, f32[256,...) custom-call(f32[8]{0:T(128)} %rate_ref.7, bf16[512,1024]{1,0:T(8,128)(2,1)} %x_ref.5, ...), custom_call_target="tpu_custom_call" | custom-call | tf_op jit(solution)/shard_map/scan_in/pallas_call | solution.py:248
  13.4 7.6 %all-to-all-start = ((bf16[16,16,1024]{2,1,0:T(8,128)(2,1)}), bf16[16,16,1024]{2,1,0:T(8,128)(2,1)S(1)}, u32[]{:S(2)}, u32[]{:S(2)}) async-start(bf16[16,16,1024]{2,1,0:T(8,128)(2,1)} %get-tuple-element.29), calls=%async_computation | async-start | bytes 1048576 | tf_op jit(solution)/shard_map/all_to_all | solution.py:298
  21.0 4.6 %local.1 = (bf16[512,1024]{1,0:T(8,128)(2,1)}, bf16[512,1024]{1,0:T(8,128)(2,1)}) custom-call(f32[8]{0:T(128)} %rate_ref.7, f32[8]{0:T(128)} %skip_ref.1, bf16[256,1024]{1,0:T(8,128)(2,1)} %get-tuple-element.30.xt0_ref, bf16[256,1024]{1,0:T(8,128)(2,1)} %get-tuple-element.31.xt1_ref, bf16[256,1024]{1,0:T(8,128)(2,1)} %get-tuple-element.32.xc0_ref, ...), custom_call_target="tpu_custom_call" | custom-call | flops 2147483648 | bytes 8388608 | tf_op jit(solution)/shard_map/local/pallas_call | solution.py:300
  25.6 7.4 %all-to-all-done.r_ref = bf16[16,16,1024]{2,1,0:T(8,128)(2,1)S(1)} async-done(((bf16[16,16,1024]{2,1,0:T(8,128)(2,1)}), bf16[16,16,1024]{2,1,0:T(8,128)(2,1)S(1)}, u32[]{:S(2)}, u32[]{:S(2)}) %all-to-all-start) | async-done | bytes 524320 | tf_op jit(solution)/shard_map/all_to_all | solution.py:298
  32.9 0.9 prefix.1
  33.8 11.6 %all_to_all.10.q_ref = bf16[16,8,1024]{2,1,0:T(8,128)(2,1)S(1)} all-to-all(bf16[16,8,1024]{2,1,0:T(8,128)(2,1)S(1)} %prefix.1), channel_id=1, replica_groups=mesh['ctx'=16,'tp'=8] {'ctx'}, dimensions={0} | all-to-all | bytes 524288 | tf_op jit(solution)/shard_map/all_to_all | solution.py:324
  45.4 2.4 %norm.1.own_ref = bf16[512,1024]{1,0:T(8,128)(2,1)S(1)} custom-call(bf16[16,8,1024]{2,1,0:T(8,128)(2,1)S(1)} %all_to_all.10.q_ref, bf16[512,1024]{1,0:T(8,128)(2,1)} %get-tuple-element.39.after_ref.a1_ref, bf16[512,1024]{1,0:T(8,128)(2,1)} %get-tuple-element.40.a2_ref, bf16[256,128]{1,0:T(8,128)(2,1)} %get-tuple-element.37.c0_ref, ...), custom_call_target="tpu_custom_call" | custom-call | tf_op jit(solution)/shard_map/norm/pallas_call | solution.py:326
  47.9 2.6 %collective-permute-done.1.sib_ref = bf16[512,1024]{1,0:T(8,128)(2,1)S(1)} collective-permute-done((bf16[512,1024]{1,0:T(8,128)(2,1)S(1)}, bf16[512,1024]{1,0:T(8,128)(2,1)S(1)}, u32[]{:S(2)}, u32[]{:S(2)}) %collective-permute-start.1) | collective-permute-done | bytes 1048608 | tf_op jit(solution)/shard_map/ppermute | solution.py:342
  50.6 4.8 %project.6 = (bf16[512,512]{1,0:T(8,128)(2,1)S(1)}, bf16[512,512]{1,0:T(8,128)(2,1)S(1)}) custom-call(s32[1]{0:T(128)} %bitcast.place_ref, bf16[512,1024]{1,0:T(8,128)(2,1)S(1)} %norm.1.own_ref, bf16[512,1024]{1,0:T(8,128)(2,1)S(1)} %collective-permute-done.1.sib_ref, bf16[1024,8192]{1,0:T(8,128)(2,1)} %w_ref.7, bf16[1024,8192]{1,0:T(8,128)(2,1)} %collective-permute-done.2.ws_ref), custom_call_target="tpu_custom_call" | custom-call | tf_op jit(solution)/shard_map/project/pallas_call | solution.py:221
  55.4 1.6 %collective-permute-start.5 = (bf16[512,512]{1,0:T(8,128)(2,1)S(1)}, bf16[512,512]{1,0:T(8,128)(2,1)S(1)}, u32[]{:S(2)}, u32[]{:S(2)}) collective-permute-start(bf16[512,512]{1,0:T(8,128)(2,1)S(1)} %get-tuple-element.45), channel_id=1, source_target_pairs={{0,2},{1,3},{2,4},{3,5},{4,6},{5,7},{6,0},{7,1},{8,10},{9,11},{10,... | collective-permute-start | bytes 1572872 | tf_op jit(solution)/shard_map/ppermute | solution.py:345
  57.0 1.7 %collective-permute-start.6 = (bf16[512,512]{1,0:T(8,128)(2,1)S(1)}, bf16[512,512]{1,0:T(8,128)(2,1)S(1)}, u32[]{:S(2)}, u32[]{:S(2)}) collective-permute-start(bf16[512,512]{1,0:T(8,128)(2,1)S(1)} %get-tuple-element.46), channel_id=1, source_target_pairs={{0,6},{1,7},{2,0},{3,1},{4,2},{5,3},{6,4},{7,5},{8,14},{9,15},{10,... | collective-permute-start | bytes 1572872 | tf_op jit(solution)/shard_map/ppermute | solution.py:345
  58.7 4.8 %project.4 = (bf16[512,512]{1,0:T(8,128)(2,1)S(1)}, bf16[512,512]{1,0:T(8,128)(2,1)S(1)}) custom-call(s32[1]{0:T(128)} %bitcast.place_ref, bf16[512,1024]{1,0:T(8,128)(2,1)S(1)} %norm.1.own_ref, bf16[512,1024]{1,0:T(8,128)(2,1)S(1)} %collective-permute-done.1.sib_ref, bf16[1024,8192]{1,0:T(8,128)(2,1)} %w_ref.7, bf16[1024,8192]{1,0:T(8,128)(2,1)} %collective-permute-done.2.ws_ref), custom_call_target="tpu_custom_call" | custom-call | tf_op jit(solution)/shard_map/project/pallas_call | solution.py:221
  63.5 1.9 %collective-permute-start.3 = (bf16[512,512]{1,0:T(8,128)(2,1)S(1)}, bf16[512,512]{1,0:T(8,128)(2,1)S(1)}, u32[]{:S(2)}, u32[]{:S(2)}) collective-permute-start(bf16[512,512]{1,0:T(8,128)(2,1)S(1)} %get-tuple-element.41), channel_id=1, source_target_pairs={{0,6},{1,7},{2,0},{3,1},{4,2},{5,3},{6,4},{7,5},{8,14},{9,15},{10,... | collective-permute-start | bytes 1572872 | tf_op jit(solution)/shard_map/ppermute | solution.py:347
  65.6 5.8 %collective-permute-done.5.refs_0_ = bf16[512,512]{1,0:T(8,128)(2,1)S(1)} collective-permute-done((bf16[512,512]{1,0:T(8,128)(2,1)S(1)}, bf16[512,512]{1,0:T(8,128)(2,1)S(1)}, u32[]{:S(2)}, u32[]{:S(2)}) %collective-permute-start.5) | collective-permute-done | bytes 524320 | tf_op jit(solution)/shard_map/ppermute | solution.py:345
  71.9 4.9 %project.7 = (bf16[512,512]{1,0:T(8,128)(2,1)S(1)}, bf16[512,512]{1,0:T(8,128)(2,1)S(1)}) custom-call(s32[1]{0:T(128)} %bitcast.place_ref, bf16[512,1024]{1,0:T(8,128)(2,1)S(1)} %norm.1.own_ref, bf16[512,1024]{1,0:T(8,128)(2,1)S(1)} %collective-permute-done.1.sib_ref, bf16[1024,8192]{1,0:T(8,128)(2,1)} %w_ref.7, ...), custom_call_target="tpu_custom_call" | custom-call | tf_op jit(solution)/shard_map/project/pallas_call | solution.py:221
  76.7 1.6 %collective-permute-start.7 = (bf16[512,512]{1,0:T(8,128)(2,1)S(1)}, bf16[512,512]{1,0:T(8,128)(2,1)S(1)}, u32[]{:S(2)}, u32[]{:S(2)}) collective-permute-start(bf16[512,512]{1,0:T(8,128)(2,1)S(1)} %get-tuple-element.47), channel_id=1, source_target_pairs={{0,2},{1,3},{2,4},{3,5},{4,6},{5,7},{6,0},{7,1},{8,10},{9,11},{10,... | collective-permute-start | bytes 1572872 | tf_op jit(solution)/shard_map/ppermute | solution.py:349
  78.4 1.7 %collective-permute-start.8 = (bf16[512,512]{1,0:T(8,128)(2,1)S(1)}, bf16[512,512]{1,0:T(8,128)(2,1)S(1)}, u32[]{:S(2)}, u32[]{:S(2)}) collective-permute-start(bf16[512,512]{1,0:T(8,128)(2,1)S(1)} %get-tuple-element.48), channel_id=1, source_target_pairs={{0,6},{1,7},{2,0},{3,1},{4,2},{5,3},{6,4},{7,5},{8,14},{9,15},{10,... | collective-permute-start | bytes 1572872 | tf_op jit(solution)/shard_map/ppermute | solution.py:349
  80.0 3.0 %collective-permute-done.3.refs_0_ = bf16[512,512]{1,0:T(8,128)(2,1)S(1)} collective-permute-done((bf16[512,512]{1,0:T(8,128)(2,1)S(1)}, bf16[512,512]{1,0:T(8,128)(2,1)S(1)}, u32[]{:S(2)}, u32[]{:S(2)}) %collective-permute-start.3) | collective-permute-done | bytes 524320 | tf_op jit(solution)/shard_map/ppermute | solution.py:347
  83.1 4.9 %project.5 = (f32[512,512]{1,0:T(8,128)S(1)}, f32[512,512]{1,0:T(8,128)S(1)}) custom-call(s32[1]{0:T(128)} %bitcast.place_ref, bf16[512,1024]{1,0:T(8,128)(2,1)S(1)} %norm.1.own_ref, bf16[512,1024]{1,0:T(8,128)(2,1)S(1)} %collective-permute-done.1.sib_ref, bf16[1024,8192]{1,0:T(8,128)(2,1)} %w_ref.7, bf16[1024,8192]{1,0:T(8,128)(2,1)} %collective-permute-done.2.ws_ref, ...), custom_call_target="tpu_custom_call" | custom-call | tf_op jit(solution)/shard_map/project/pallas_call | solution.py:221
  88.0 5.1 %collective-permute-done.7.a_ref = bf16[512,512]{1,0:T(8,128)(2,1)S(1)} collective-permute-done((bf16[512,512]{1,0:T(8,128)(2,1)S(1)}, bf16[512,512]{1,0:T(8,128)(2,1)S(1)}, u32[]{:S(2)}, u32[]{:S(2)}) %collective-permute-start.7) | collective-permute-done | bytes 524320 | tf_op jit(solution)/shard_map/ppermute | solution.py:349
  93.2 1.2 %final.1 = bf16[512,1024]{1,0:T(8,128)(2,1)} custom-call(f32[512,512]{1,0:T(8,128)S(1)} %get-tuple-element.43.m0_ref, f32[512,512]{1,0:T(8,128)S(1)} %get-tuple-element.44.m1_ref, bf16[512,512]{1,0:T(8,128)(2,1)S(1)} %collective-permute-done.7.a_ref, bf16[512,512]{1,0:T(8,128)(2,1)S(1)} %collective-permute-done.8.b_ref), custom_call_target="tpu_custom_call" | custom-call | tf_op jit(solution)/shard_map/final/pallas_call | solution.py:351
  (8 shorter events, 0.8 us)
Async XLA Ops:
  0.0 50.6 %collective-permute-start.2 = (bf16[1024,8192]{1,0:T(8,128)(2,1)}, bf16[1024,8192]{1,0:T(8,128)(2,1)}, u32[]{:S(2)}, u32[]{:S(2)}) collective-permute-start(bf16[1024,8192]{1,0:T(8,128)(2,1)} %w_ref.7), channel_id=1, source_target_pairs={{0,1},{1,0},{2,3},{3,2},{4,5},{5,4},{6,7},{7,6},{8,9},{9,8},{10,11... | collective-permute-start | bytes 50331656 | tf_op jit(solution)/shard_map/ppermute | solution.py:276
  0.7 8.0 %collective-permute-start = (bf16[8,1280]{1,0:T(8,128)(2,1)S(1)}, bf16[8,1280]{1,0:T(8,128)(2,1)S(1)}, u32[]{:S(2)}, u32[]{:S(2)}) collective-permute-start(bf16[8,1280]{1,0:T(8,128)(2,1)S(1)} %rim.1), channel_id=1, source_target_pairs={{0,8},{8,16},{16,24},{24,32},{32,40},{40,48},{48,56},{56,64},{64,7... | collective-permute-start | bytes 61448 | tf_op jit(solution)/shard_map/ppermute | solution.py:289
  13.4 19.5 %all-to-all-start = ((bf16[16,16,1024]{2,1,0:T(8,128)(2,1)}), bf16[16,16,1024]{2,1,0:T(8,128)(2,1)S(1)}, u32[]{:S(2)}, u32[]{:S(2)}) async-start(bf16[16,16,1024]{2,1,0:T(8,128)(2,1)} %get-tuple-element.29), calls=%async_computation | async-start | bytes 1048576 | tf_op jit(solution)/shard_map/all_to_all | solution.py:298
  47.8 2.7 %collective-permute-start.1 = (bf16[512,1024]{1,0:T(8,128)(2,1)S(1)}, bf16[512,1024]{1,0:T(8,128)(2,1)S(1)}, u32[]{:S(2)}, u32[]{:S(2)}) collective-permute-start(bf16[512,1024]{1,0:T(8,128)(2,1)S(1)} %norm.1.own_ref), channel_id=1, source_target_pairs={{0,1},{1,0},{2,3},{3,2},{4,5},{5,4},{6,7},{7,6},{8,9},{9,8},{10,11... | collective-permute-start | bytes 3145736 | tf_op jit(solution)/shard_map/ppermute | solution.py:342
  55.4 16.0 %collective-permute-start.5 = (bf16[512,512]{1,0:T(8,128)(2,1)S(1)}, bf16[512,512]{1,0:T(8,128)(2,1)S(1)}, u32[]{:S(2)}, u32[]{:S(2)}) collective-permute-start(bf16[512,512]{1,0:T(8,128)(2,1)S(1)} %get-tuple-element.45), channel_id=1, source_target_pairs={{0,2},{1,3},{2,4},{3,5},{4,6},{5,7},{6,0},{7,1},{8,10},{9,11},{10,... | collective-permute-start | bytes 1572872 | tf_op jit(solution)/shard_map/ppermute | solution.py:345
  57.0 14.8 %collective-permute-start.6 = (bf16[512,512]{1,0:T(8,128)(2,1)S(1)}, bf16[512,512]{1,0:T(8,128)(2,1)S(1)}, u32[]{:S(2)}, u32[]{:S(2)}) collective-permute-start(bf16[512,512]{1,0:T(8,128)(2,1)S(1)} %get-tuple-element.46), channel_id=1, source_target_pairs={{0,6},{1,7},{2,0},{3,1},{4,2},{5,3},{6,4},{7,5},{8,14},{9,15},{10,... | collective-permute-start | bytes 1572872 | tf_op jit(solution)/shard_map/ppermute | solution.py:345
  63.5 19.5 %collective-permute-start.3 = (bf16[512,512]{1,0:T(8,128)(2,1)S(1)}, bf16[512,512]{1,0:T(8,128)(2,1)S(1)}, u32[]{:S(2)}, u32[]{:S(2)}) collective-permute-start(bf16[512,512]{1,0:T(8,128)(2,1)S(1)} %get-tuple-element.41), channel_id=1, source_target_pairs={{0,6},{1,7},{2,0},{3,1},{4,2},{5,3},{6,4},{7,5},{8,14},{9,15},{10,... | collective-permute-start | bytes 1572872 | tf_op jit(solution)/shard_map/ppermute | solution.py:347
  65.4 17.7 %collective-permute-start.4 = (bf16[512,512]{1,0:T(8,128)(2,1)S(1)}, bf16[512,512]{1,0:T(8,128)(2,1)S(1)}, u32[]{:S(2)}, u32[]{:S(2)}) collective-permute-start(bf16[512,512]{1,0:T(8,128)(2,1)S(1)} %get-tuple-element.42), channel_id=1, source_target_pairs={{0,2},{1,3},{2,4},{3,5},{4,6},{5,7},{6,0},{7,1},{8,10},{9,11},{10,... | collective-permute-start | bytes 1572872 | tf_op jit(solution)/shard_map/ppermute | solution.py:347
  76.7 16.4 %collective-permute-start.7 = (bf16[512,512]{1,0:T(8,128)(2,1)S(1)}, bf16[512,512]{1,0:T(8,128)(2,1)S(1)}, u32[]{:S(2)}, u32[]{:S(2)}) collective-permute-start(bf16[512,512]{1,0:T(8,128)(2,1)S(1)} %get-tuple-element.47), channel_id=1, source_target_pairs={{0,2},{1,3},{2,4},{3,5},{4,6},{5,7},{6,0},{7,1},{8,10},{9,11},{10,... | collective-permute-start | bytes 1572872 | tf_op jit(solution)/shard_map/ppermute | solution.py:349
  78.4 14.8 %collective-permute-start.8 = (bf16[512,512]{1,0:T(8,128)(2,1)S(1)}, bf16[512,512]{1,0:T(8,128)(2,1)S(1)}, u32[]{:S(2)}, u32[]{:S(2)}) collective-permute-start(bf16[512,512]{1,0:T(8,128)(2,1)S(1)} %get-tuple-element.48), channel_id=1, source_target_pairs={{0,6},{1,7},{2,0},{3,1},{4,2},{5,3},{6,4},{7,5},{8,14},{9,15},{10,... | collective-permute-start | bytes 1572872 | tf_op jit(solution)/shard_map/ppermute | solution.py:349

commit v4 on v3

v4 whole, which is shorter than its diff:
```python
import functools

import jax
import jax.numpy as jnp
from jax import lax
from jax.experimental import pallas as pl
from jax.experimental.pallas import tpu as pltpu
from jax.sharding import PartitionSpec as P

BF = jnp.bfloat16
F32 = jnp.float32
TOK = 512
HT = TOK // 2
BT = 128
EDGE = 3
MSG = 1152
WID = 1024
HALF = WID // 2
HEADS = 8
HW = 128
ST = 128
CTX = 16
CB = 512
NB = WID // CB
SEQ = TOK * CTX
DECAY = 12.288 / SEQ / 63.0
SCALE = 1.0 / (ST * SEQ) ** 0.5
ROWS = 32
SD = jax.ShapeDtypeStruct


def silu(v):
    half = 0.5 * v
    return half + half * jnp.tanh(half)


def mm(a, b):
    return jnp.dot(a, b, preferred_element_type=F32)


def triangle():
    row = lax.broadcasted_iota(jnp.int32, (BT, BT), 0)
    col = lax.broadcasted_iota(jnp.int32, (BT, BT), 1)
    return jnp.where(row >= col, 1.0, 0.0).astype(BF)


def head_row(ref, factor, at=0):
    lane = lax.broadcasted_iota(jnp.int32, (1, HW), 1)
    row = jnp.zeros((1, HW), F32)
    for h in range(HEADS):
        row = jnp.where(lane == at + h, ref[h] * factor, row)
    return row


def spread(compact, lane, rows=None):
    column = compact[:, lane : lane + 1]
    return jnp.broadcast_to(column, (rows or compact.shape[0], HW))


def row_ids(rows, width):
    return lax.broadcasted_iota(jnp.int32, (rows, width), 0)


def conv_part(source, w_ref, bias, r, rows, lo, hi):
    total = bias
    for k in range(4):
        total = total + w_ref[k : k + 1, lo:hi] * source[5 + k + r : 5 + k + r + rows, lo:hi]
    return total


def scan_in_body(
    rate_ref, x_ref, bc_ref, codes_ref, cx_ref, bx_ref, cbc_ref, bbc_ref,
    xc_ref, xt_ref, b_ref, c_ref, cum_ref, msg_ref, xe, be, acc, run, first, cum_first, b_first,
):
    step = pl.program_id(0)

    @pl.when(step == 0)
    def _():
        xe[0:8, :] = jnp.zeros((8, WID), F32)
        be[0:8, :] = jnp.zeros((8, 2 * ST), F32)
        be[8 + BT : 16 + BT, :] = jnp.zeros((8, 2 * ST), F32)
        run[...] = jnp.zeros((8, HW), F32)

    @pl.when(step > 0)
    def _():
        xe[0:8, :] = xe[BT : BT + 8, :]
        be[0:8, :] = be[BT : BT + 8, :]

    be[8 : 8 + BT, :] = bc_ref[...].astype(F32)
    xe[8 : 8 + BT, :] = x_ref[...].astype(F32)
    codes = jnp.concatenate([codes_ref[...].astype(F32), jnp.zeros((HW - HEADS, BT), F32)], axis=0)
    cum = lax.dot_general(
        triangle(), codes.astype(BF), (((1,), (1,)), ((), ())), preferred_element_type=F32
    )
    cum = cum + run[0:1, :]
    cum_ref[...] = cum
    run[...] = jnp.broadcast_to(cum[BT - 1 : BT, :], (8, HW))
    grow = jnp.exp(head_row(rate_ref, DECAY) * cum)

    @pl.when(step == 0)
    def _():
        first[...] = xe[8:16, :]
        cum_first[...] = cum_ref[0:8, :]
        b_first[...] = conv_part(be, cbc_ref, bbc_ref[:, :ST], 0, 8, 0, ST)

    for r in range(0, BT, ROWS):
        for ref, lo in ((b_ref, 0), (c_ref, ST)):
            part = conv_part(be, cbc_ref, bbc_ref[:, lo : lo + ST], r, ROWS, lo, lo + ST)
            ref[r : r + ROWS, :] = silu(part).astype(BF)
    for r in range(0, BT, ROWS):
        for h in range(HEADS):
            lo, hi = h * HW, (h + 1) * HW
            xc = silu(conv_part(xe, cx_ref, bx_ref[:, lo:hi], r, ROWS, lo, hi)).astype(BF)
            xc_ref[r : r + ROWS, lo:hi] = xc
            scaled = xc.astype(F32) * spread(grow[r : r + ROWS, :], h)
            xt_ref[r : r + ROWS, lo:hi] = scaled.astype(BF)

    @pl.when(step == 0)
    def _():
        head = xt_ref[0:16, :].astype(F32)
        xt_ref[0:16, :] = jnp.where(row_ids(16, WID) < EDGE, 0.0, head).astype(BF)
        acc[...] = jnp.zeros((ST, WID), F32)

    bt = b_ref[...].astype(F32).T.astype(BF)
    acc[...] += mm(bt, xt_ref[...])

    @pl.when(step == TOK // BT - 1)
    def _():
        row = row_ids(8, WID)
        last = pltpu.roll(xe[BT : BT + 8, :], EDGE, 0)
        bc_rows = [be[BT + 8 - EDGE + k : BT + 9 - EDGE + k, :] for k in range(EDGE)]
        bc_row = jnp.concatenate(bc_rows + [jnp.zeros((1, WID - EDGE * 2 * ST), F32)], axis=1)
        rows = jnp.where(row < EDGE, last, jnp.where(row < 2 * EDGE, pltpu.roll(first[...], EDGE, 0), 0.0))
        rows = jnp.where(row == 2 * EDGE, jnp.broadcast_to(bc_row, (8, WID)), rows)
        row = row_ids(8, HW)
        total = run[0:1, :]
        high = jnp.floor(total * (1.0 / 256.0))
        low = total - 256.0 * high
        heads = jnp.where(row < 5, pltpu.roll(cum_first[...], 2, 0), 0.0)
        heads = jnp.where(row == 0, high, jnp.where(row == 1, low, heads))
        heads = pltpu.roll(heads, HW // 2, 1)
        pad = jnp.zeros((HW - 8, HW), F32)
        b_last = conv_part(be, cbc_ref, jnp.zeros((1, ST), F32), BT, 8, 0, ST)
        b_last = jnp.concatenate([b_last, pad], axis=0).T
        b_head = jnp.concatenate([b_first[...], pad], axis=0).T
        for j in range(CTX):
            at = slice(8 * j, 8 * j + 8)
            msg_ref[j, :, 0:WID] = jnp.concatenate([acc[at, :], rows], axis=0).astype(BF)
            side = jnp.concatenate([b_last[at, :] + heads, b_head[at, :]], axis=0)
            msg_ref[j, :, WID:MSG] = side.astype(BF)


def prefix_body(rate_ref, cx_ref, bx_ref, r_ref, q_ref):
    rate = head_row(rate_ref, DECAY, HW // 2)
    state = jnp.zeros((8, WID), F32)
    before = jnp.zeros((8, WID), F32)
    side_before = jnp.zeros((8, HW), F32)
    edge_row = row_ids(8, WID) < EDGE
    for c in range(CTX):
        q_ref[c] = state.astype(BF)
        main = r_ref[c, :, 0:WID].astype(F32)
        side = r_ref[c, :, WID:MSG].astype(F32)
        rows = jnp.where(edge_row, before, main[8:16, :])
        before = main[8:16, :]
        pre = bx_ref[...] + cx_ref[0:1, :] * rows
        for k in range(1, 4):
            pre = pre + cx_ref[k : k + 1, :] * pltpu.roll(rows, 8 - k, 0)
        edge = silu(pre).astype(BF).astype(F32)
        heads = side[0:8, :]
        grow = jnp.exp(rate * pltpu.roll(heads, 6, 0))
        fade = jnp.exp(-rate * (256.0 * heads[0:1, :] + heads[1:2, :]))
        b_edge = silu(side_before + side[8:16, :]).astype(BF).astype(F32)
        side_before = heads
        parts = []
        for h in range(HEADS):
            lo, hi = h * HW, (h + 1) * HW
            scaled = (edge[:, lo:hi] * spread(grow, HW // 2 + h)).astype(BF).astype(F32)
            part = state[:, lo:hi] + main[0:8, lo:hi]
            for k in range(EDGE):
                part = part + spread(b_edge, k) * jnp.broadcast_to(scaled[k : k + 1, :], (8, HW))
            parts.append(spread(fade, HW // 2 + h, 8) * part)
        state = jnp.concatenate(parts, axis=1)


def local_body(
    place_ref, rate_ref, skip_ref, xt_ref, xc_ref, z_ref, cum_ref, b_ref, c_ref, got_ref, x_ref, bc_ref, cx_ref,
    bx_ref, cbc_ref, bbc_ref, after_ref, a1_ref, a2_ref, cm_ref, gram, prod, xe, be, bm, xt_first, xc_first,
):
    rim = pltpu.roll(got_ref[0, 8:16, 0:WID].astype(F32), 8 - EDGE, 0)
    live = place_ref[0] > 0
    xe[0:8, :] = jnp.where(live, rim, 0.0)
    xe[8:24, :] = x_ref[...].astype(F32)
    bc_row = got_ref[0, 8:16, 0 : EDGE * 2 * ST].astype(F32)[2 * EDGE : 2 * EDGE + 1, :]
    for k in range(EDGE):
        part = bc_row[:, k * 2 * ST : (k + 1) * 2 * ST]
        be[8 - EDGE + k : 9 - EDGE + k, :] = jnp.where(live, part, 0.0)
    be[8:24, :] = bc_ref[...].astype(F32)
    bm[...] = b_ref[...]
    cm_ref[...] = c_ref[...]
    bm[0:16, :] = silu(conv_part(be, cbc_ref, bbc_ref[:, :ST], 0, 16, 0, ST)).astype(BF)
    cm_ref[0:16, :] = silu(conv_part(be, cbc_ref, bbc_ref[:, ST:], 0, 16, ST, 2 * ST)).astype(BF)
    xt_first[...] = xt_ref[0:BT, :]
    xc_first[...] = xc_ref[0:ROWS, :]
    grow = jnp.exp(head_row(rate_ref, DECAY) * cum_ref[0:16, :])
    for h in range(HEADS):
        lo, hi = h * HW, (h + 1) * HW
        xc = silu(conv_part(xe, cx_ref, bx_ref[:, lo:hi], 0, 16, lo, hi)).astype(BF)
        xc_first[0:16, lo:hi] = xc
        xt_first[0:16, lo:hi] = (xc.astype(F32) * spread(grow, h)).astype(BF)
    for r in range(0, TOK, BT):
        size = r + BT
        part = lax.dot_general(
            cm_ref[r:size, :], bm[0:size, :], (((1,), (1,)), ((), ())), preferred_element_type=F32
        )
        row = lax.broadcasted_iota(jnp.int32, (BT, size), 0) + r
        col = lax.broadcasted_iota(jnp.int32, (BT, size), 1)
        gram[r:size, 0:size] = jnp.where(row >= col, part, 0.0).astype(BF)
        total = mm(gram[r:size, 0:BT], xt_first[...])
        if r:
            total = total + mm(gram[r:size, BT:size], xt_ref[BT:size, :])
        prod[r:size, :] = total
    rate = head_row(rate_ref, -DECAY)
    for r in range(0, TOK, ROWS):
        rs = slice(r, r + ROWS)
        fades = SCALE * jnp.exp(rate * cum_ref[rs, :])
        for h in range(HEADS):
            lo, hi = h * HW, (h + 1) * HW
            gate = silu(z_ref[rs, lo:hi].astype(F32))
            fade = spread(fades, h)
            xc = (xc_ref[rs, lo:hi] if r else xc_first[:, lo:hi]).astype(F32)
            both = (prod[rs, lo:hi] * fade + skip_ref[h] * xc) * gate
            a1_ref[rs, lo:hi] = both.astype(BF)
            a2_ref[rs, lo:hi] = (fade * gate).astype(BF)


def norm_body(q_ref, a1_ref, a2_ref, c_ref, gain_ref, n_ref, prod):
    state = q_ref[...].astype(F32).reshape(ST, CB).astype(BF)
    prod[...] = mm(c_ref[...], state)
    for r in range(0, TOK, ROWS):
        for h in range(0, CB, HW):
            rs, hs = slice(r, r + ROWS), slice(h, h + HW)
            gated = a1_ref[rs, hs].astype(F32) + a2_ref[rs, hs].astype(F32) * prod[rs, hs]
            power = jnp.mean(gated * gated, axis=-1, keepdims=True)
            n_ref[rs, hs] = (gated * lax.rsqrt(power + 1e-05) * gain_ref[:, hs]).astype(BF)


def project_body(adds, place_ref, own_ref, sib_ref, w_ref, ws_ref, *refs):
    step = pl.program_id(0)
    outs = refs[-2:]
    for k in range(2):

        @pl.when(step // 2 == k)
        def _():
            total = mm(own_ref[...], w_ref[...]) + mm(sib_ref[...], ws_ref[...])
            for ref in refs[adds * k : adds * (k + 1)]:
                total = total + ref[...].astype(F32)
            outs[k][...] = total.astype(outs[k].dtype)


def final_body(m0_ref, m1_ref, a_ref, b_ref, o_ref):
    o_ref[:, :HALF] = (m0_ref[...] + a_ref[...].astype(F32)).astype(BF)
    o_ref[:, HALF:] = (m1_ref[...] + b_ref[...].astype(F32)).astype(BF)


def params(dims=1):
    return pltpu.CompilerParams(
        dimension_semantics=("arbitrary",) * dims if dims else None, vmem_limit_bytes=20 << 20
    )


SMEM = pl.BlockSpec(memory_space=pltpu.SMEM)
VMEM = pl.BlockSpec(memory_space=pltpu.VMEM)
ANY = pl.BlockSpec(memory_space=pl.ANY)


def whole(*shape):
    return pl.BlockSpec(shape, lambda i: (0,) * len(shape))


def cols(rows, at=0):
    return pl.BlockSpec((rows, CB), lambda i: (at, i))


def in_hbm(a):
    return pltpu.with_memory_space_constraint(a, pltpu.HBM)


QUART = HALF // 2


def project(place, normed, sibling, w, w_sib, targets, addends, kind):
    def column(i, place_ref):
        index = place_ref[0]
        far = jnp.where(i < 2, targets[0][0], targets[1][0])
        side = jnp.where(i < 2, targets[0][1], targets[1][1])
        return 0, ((((index >> 1) + far) & 3) * 2 + (index & 1)) * 4 + side * 2 + (i & 1)

    whole2 = pl.BlockSpec((TOK, WID), lambda i, ix: (0, 0))
    weight = pl.BlockSpec((WID, QUART), column)
    halves = [
        pl.BlockSpec((TOK, QUART), lambda i, ix: (0, jnp.minimum(i, 1))),
        pl.BlockSpec((TOK, QUART), lambda i, ix: (0, jnp.maximum(i - 2, 0))),
    ]
    count = len(addends[0])
    return pl.pallas_call(
        functools.partial(project_body, count),
        out_shape=[SD((TOK, HALF), kind)] * 2,
        grid_spec=pltpu.PrefetchScalarGridSpec(
            num_scalar_prefetch=1,
            grid=(4,),
            in_specs=[whole2, whole2, weight, weight] + [halves[0]] * count + [halves[1]] * count,
            out_specs=halves,
        ),
        compiler_params=params(),
        name="project",
    )(place, normed, sibling, w, w_sib, *addends[0], *addends[1])


def body(
    x_in, bc_in, z_in, codes, head_rate, conv_x, conv_bc, bias_x, bias_bc, skip, norm_gain, w_out
):
    place = lax.axis_index("tp")
    where = jnp.full((1,), place, jnp.int32)
    x_in, bc_in, z_in, w_out = in_hbm(x_in), in_hbm(bc_in), in_hbm(z_in), in_hbm(w_out)
    codes, conv_x, conv_bc = in_hbm(codes.T), in_hbm(conv_x), in_hbm(conv_bc)
    head_rate, skip = in_hbm(head_rate), in_hbm(skip)
    bias_x, bias_bc, gain = in_hbm(bias_x[None, :]), in_hbm(bias_bc[None, :]), in_hbm(norm_gain[None, :])

    swap = [(s, s ^ 1) for s in range(8)]
    w_sib = in_hbm(lax.ppermute(w_out, "tp", swap))
    taps = (conv_x, bias_x, conv_bc, bias_bc)
    taps_specs = [whole(4, WID), whole(1, WID), whole(4, 2 * ST), whole(1, 2 * ST)]

    def tokens(width):
        return pl.BlockSpec((BT, width), lambda i: (i, 0))

    xc, xt, b_map, c_map, cum, msg = pl.pallas_call(
        scan_in_body,
        grid=(TOK // BT,),
        in_specs=[
            SMEM, tokens(WID), tokens(2 * ST), pl.BlockSpec((HEADS, BT), lambda i: (0, i)), *taps_specs,
        ],
        out_specs=[tokens(WID), tokens(WID), tokens(ST), tokens(ST), tokens(HW), whole(CTX, 16, MSG)],
        out_shape=[
            pltpu.HBM((TOK, WID), BF), pltpu.HBM((TOK, WID), BF), pltpu.HBM((TOK, ST), BF),
            pltpu.HBM((TOK, ST), BF), pltpu.HBM((TOK, HW), F32), SD((CTX, 16, MSG), BF),
        ],
        scratch_shapes=[
            pltpu.VMEM((BT + 8, WID), F32), pltpu.VMEM((BT + 16, 2 * ST), F32), pltpu.VMEM((ST, WID), F32),
            pltpu.VMEM((8, HW), F32), pltpu.VMEM((8, WID), F32), pltpu.VMEM((8, HW), F32),
            pltpu.VMEM((8, ST), F32),
        ],
        compiler_params=params(),
        name="scan_in",
    )(head_rate, x_in, bc_in, codes, *taps)
    got = lax.all_to_all(msg, "ctx", 0, 0, tiled=True)

    prefix = pl.pallas_call(
        prefix_body,
        in_specs=[SMEM, VMEM, VMEM, VMEM],
        out_specs=VMEM,
        out_shape=SD((CTX, 8, WID), BF),
        compiler_params=params(0),
        name="prefix",
    )(head_rate, conv_x, bias_x, got)
    incoming = lax.all_to_all(prefix, "ctx", 0, 0, tiled=True)

    def fixed(*shape):
        return pl.BlockSpec(shape, lambda i, ix: (0,) * len(shape))

    ctx = jnp.full((1,), lax.axis_index("ctx"), jnp.int32)
    a1, a2, c_map = pl.pallas_call(
        local_body,
        out_shape=[pltpu.HBM((TOK, WID), BF)] * 2 + [SD((TOK, ST), BF)],
        grid_spec=pltpu.PrefetchScalarGridSpec(
            num_scalar_prefetch=1,
            grid=(1,),
            in_specs=[
                SMEM, SMEM, fixed(TOK, WID), fixed(TOK, WID), fixed(TOK, WID), fixed(TOK, HW), fixed(TOK, ST),
                fixed(TOK, ST), pl.BlockSpec((1, 16, MSG), lambda i, ix: (jnp.maximum(ix[0] - 1, 0), 0, 0)),
                fixed(16, WID), fixed(16, 2 * ST), fixed(4, WID), fixed(1, WID), fixed(4, 2 * ST),
                fixed(1, 2 * ST), ANY,
            ],
            out_specs=[fixed(TOK, WID), fixed(TOK, WID), fixed(TOK, ST)],
            scratch_shapes=[
                pltpu.VMEM((TOK, TOK), BF), pltpu.VMEM((TOK, WID), F32), pltpu.VMEM((24, WID), F32),
                pltpu.VMEM((24, 2 * ST), F32), pltpu.VMEM((TOK, ST), BF), pltpu.VMEM((BT, WID), BF),
                pltpu.VMEM((ROWS, WID), BF),
            ],
        ),
        compiler_params=params(),
        name="local",
    )(ctx, head_rate, skip, *map(in_hbm, (xt, xc)), z_in, *map(in_hbm, (cum, b_map, c_map)), got, x_in, bc_in,
      *taps, prefix)
    a1, a2 = in_hbm(a1), in_hbm(a2)

    normed = pl.pallas_call(
        norm_body,
        grid=(NB,),
        in_specs=[
            pl.BlockSpec((CTX, 8, CB), lambda i: (0, 0, i)), cols(TOK), cols(TOK), whole(TOK, ST), cols(1),
        ],
        out_specs=cols(TOK),
        out_shape=SD((TOK, WID), BF),
        scratch_shapes=[pltpu.VMEM((TOK, CB), F32)],
        compiler_params=params(),
        name="norm",
    )(incoming, a1, a2, c_map, gain)

    up = [(s, (s + 2) % 8) for s in range(8)]
    down = [(s, (s + 6) % 8) for s in range(8)]
    sibling = lax.ppermute(normed, "tp", swap)
    run = functools.partial(project, where, normed, sibling, w_out, w_sib)
    far_l, far_r = run(((2, 0), (2, 1)), ((), ()), BF)
    far_l, far_r = lax.ppermute(far_l, "tp", up), lax.ppermute(far_r, "tp", down)
    above_r, below_l = run(((1, 1), (3, 0)), ((), ()), BF)
    from_r, from_l = lax.ppermute(above_r, "tp", up), lax.ppermute(below_l, "tp", down)
    above_l, below_r = run(((1, 0), (3, 1)), ((far_l,), (far_r,)), BF)
    last_l, last_r = lax.ppermute(above_l, "tp", up), lax.ppermute(below_r, "tp", down)
    here_l, here_r = run(((0, 0), (0, 1)), ((from_l,), (from_r,)), F32)
    return pl.pallas_call(
        final_body,
        in_specs=[VMEM] * 4,
        out_specs=VMEM,
        out_shape=SD((TOK, WID), BF),
        compiler_params=params(0),
        name="final",
    )(here_l, here_r, last_l, last_r)


def solution(mesh):
    in_specs = (
        P("ctx", "tp"),
        P("ctx", None),
        P("ctx", "tp"),
        P("ctx", "tp"),
        P("tp"),
        P(None, "tp"),
        P(),
        P("tp"),
        P(),
        P("tp"),
        P("tp"),
        P("tp", None),
    )
    out_specs = P("ctx", "tp")
    return jax.shard_map(body, mesh=mesh, in_specs=in_specs, out_specs=out_specs, check_vma=False)
```

time: 95.3 us -> 92.8 us (0.974)
  blocking collectives: 11.6 us -> 20.7 us
  starting transfers between devices: 19.8 us -> 12.3 us
  waiting for transfers between devices: 24.4 us -> 20.7 us
    all_to_all x1, blocking collectives: 11.6 us -> 20.7 us  [body(): got = lax.all_to_all(msg, 'ctx', 0, 0, tiled=True)]
    all_to_all x1, starting transfers between devices: 7.59 us -> 3.53 us  [body(): incoming = lax.all_to_all(prefix, 'ctx', 0, 0, tiled=True)]
    all_to_all x1, waiting for transfers between devices: 7.37 us -> 3.62 us  [body(): incoming = lax.all_to_all(prefix, 'ctx', 0, 0, tiled=True)]
    ppermute x1 -> x0, starting transfers between devices: 3.47 us -> none  [body(): rim = lax.ppermute(rim, 'ctx', [(s, s + 1) for s in range(CTX - 1)])]
    pallas_call x5 -> x3, Pallas kernels: 15.3 us -> 15.1 us  [the longest x1 7.95 us: body(): pl.pallas_call(scan_in_body, grid=(TOK // BT,), in_specs=[SMEM, tokens(WI...]
  transfers between devices with their start and end apart: 10 -> 9, of which waited for: 6 -> 6; matrix products, arithmetic and copies ran while one was open for 0% -> 0% of each run, Pallas kernels for 34% -> 35%
where the time goes in v4:
time: 92.8 us; the launch traced here: 92 us
  Pallas kernels  38.2 us (41%)
  blocking collectives  20.7 us (22%)
  waiting for transfers between devices  20.7 us (22%)
  starting transfers between devices  12.3 us (13%)
    all_to_all x1, blocking collectives, body(): got = lax.all_to_all(msg, 'ctx', 0, 0, tiled=True)  20.7 us
    pallas_call x4, Pallas kernels, project(): pl.pallas_call(functools.partial(project_body, count), out_shape=[SD((TOK...  19.5 us
    pallas_call x1, Pallas kernels, body(): pl.pallas_call(scan_in_body, grid=(TOK // BT,), in_specs=[SMEM, tokens(WI...  7.95 us
    ppermute x1, waiting for transfers between devices, body(): lax.ppermute(far_l, 'tp', up)  5.8 us
    ppermute x1, waiting for transfers between devices, body(): lax.ppermute(above_l, 'tp', up)  5.14 us
    pallas_call x1, Pallas kernels, body(): pl.pallas_call(local_body, out_shape=[pltpu.HBM((TOK, WID), BF)] * 2 + [S...  5.03 us
    all_to_all x1, waiting for transfers between devices, body(): incoming = lax.all_to_all(prefix, 'ctx', 0, 0, tiled=True)  3.62 us
    all_to_all x1, starting transfers between devices, body(): incoming = lax.all_to_all(prefix, 'ctx', 0, 0, tiled=True)  3.53 us
  transfers between devices with their start and end apart: 9, of which 6 were waited for; matrix products, arithmetic and copies ran while one was open for 0% of the time, Pallas kernels for 35%

profile of v4, /device:TPU:0, one launch (start us, length us, event | category | flops | bytes accessed | tf_op | source)
XLA Modules:
  0.0 92.0 jit_solution(2909886134918795783)
XLA Ops:
  0.0 8.0 %scan_in.1 = (bf16[512,1024]{1,0:T(8,128)(2,1)}, bf16[512,1024]{1,0:T(8,128)(2,1)}, bf16[512,128]{1,0:T(8,128)(2,1)}, bf16[512,128]{1,0:T(8,128)(2,1)}, f32[512,...) custom-call(f32[8]{0:T(128)} %rate_ref.5, bf16[512,1024]{1,0:T(8,128)(2,1)} %x_ref.3, bf16[512,256]{1,0:T(8,128)(2,1)} %bc_ref.3, ...), custom_call_target="tpu_custom_call" | custom-call | tf_op jit(solution)/shard_map/scan_in/pallas_call | solution.py:337
  8.0 20.7 %all_to_all.10.r_ref.got_ref = bf16[16,16,1152]{2,1,0:T(8,128)(2,1)S(1)} all-to-all(bf16[16,16,1152]{2,1,0:T(8,128)(2,1)S(1)} %get-tuple-element.22), channel_id=1, replica_groups=mesh['ctx'=16,'tp'=8] {'ctx'}, dimensions={0} | all-to-all | bytes 1179648 | tf_op jit(solution)/shard_map/all_to_all | solution.py:356
  28.6 2.1 %prefix.1.after_ref = bf16[16,8,1024]{2,1,0:T(8,128)(2,1)} custom-call(f32[8]{0:T(128)} %rate_ref.5, f32[4,1024]{1,0:T(4,128)} %cx_ref.5, f32[1,1024]{1,0:T(1,128)} %bitcast.7, bf16[16,16,1152]{2,1,0:T(8,128)(2,1)S(1)} %all_to_all.10.r_ref.got_ref), custom_call_target="tpu_custom_call" | custom-call | tf_op jit(solution)/shard_map/prefix/pallas_call | solution.py:358
  30.8 3.5 %all-to-all-start.1 = ((bf16[16,8,1024]{2,1,0:T(8,128)(2,1)}), bf16[16,8,1024]{2,1,0:T(8,128)(2,1)S(1)}, u32[]{:S(2)}, u32[]{:S(2)}) async-start(bf16[16,8,1024]{2,1,0:T(8,128)(2,1)} %prefix.1.after_ref), calls=%async_computation.1 | async-start | bytes 524288 | tf_op jit(solution)/shard_map/all_to_all | solution.py:366
  34.3 5.0 %local.1 = (bf16[512,1024]{1,0:T(8,128)(2,1)}, bf16[512,1024]{1,0:T(8,128)(2,1)}, bf16[512,128]{1,0:T(8,128)(2,1)S(1)}) custom-call(s32[1]{0:T(128)} %bitcast.4.place_ref, f32[8]{0:T(128)} %rate_ref.5, f32[8]{0:T(128)} %skip_ref.1, bf16[512,1024]{1,0:T(8,128)(2,1)} %get-tuple-element.23.xt_ref, bf16[512,1024]{1,0:T(8,128)(2,1)} %get-tuple-element.24.xc_ref, ...), custom_call_target="tpu_custom_call" | custom-call | tf_op jit(solution)/shard_map/local/pallas_call | solution.py:372
  39.3 3.6 %all-to-all-done.1.q_ref = bf16[16,8,1024]{2,1,0:T(8,128)(2,1)S(1)} async-done(((bf16[16,8,1024]{2,1,0:T(8,128)(2,1)}), bf16[16,8,1024]{2,1,0:T(8,128)(2,1)S(1)}, u32[]{:S(2)}, u32[]{:S(2)}) %all-to-all-start.1) | async-done | bytes 262176 | tf_op jit(solution)/shard_map/all_to_all | solution.py:366
  43.0 2.4 %norm.1.own_ref = bf16[512,1024]{1,0:T(8,128)(2,1)S(1)} custom-call(bf16[16,8,1024]{2,1,0:T(8,128)(2,1)S(1)} %all-to-all-done.1.q_ref, bf16[512,1024]{1,0:T(8,128)(2,1)} %get-tuple-element.28.a1_ref, bf16[512,1024]{1,0:T(8,128)(2,1)} %get-tuple-element.29.a2_ref, bf16[512,128]{1,0:T(8,128)(2,1)S(1)} %get-tuple-element.30.c_ref, f32[1,1024]{1,0:T(1,128)} %bitcast.10), custom_call_target="tpu_custom_call" | custom-call | tf_op jit(solution)/shard_map/norm/pallas_call | solution.py:397
  45.4 0.1 collective-permute-start
  45.5 2.6 %collective-permute-done.sib_ref = bf16[512,1024]{1,0:T(8,128)(2,1)S(1)} collective-permute-done((bf16[512,1024]{1,0:T(8,128)(2,1)S(1)}, bf16[512,1024]{1,0:T(8,128)(2,1)S(1)}, u32[]{:S(2)}, u32[]{:S(2)}) %collective-permute-start) | collective-permute-done | bytes 1048608 | tf_op jit(solution)/shard_map/ppermute | solution.py:412
  48.1 4.8 %project.6 = (bf16[512,512]{1,0:T(8,128)(2,1)S(1)}, bf16[512,512]{1,0:T(8,128)(2,1)S(1)}) custom-call(s32[1]{0:T(128)} %bitcast.place_ref, bf16[512,1024]{1,0:T(8,128)(2,1)S(1)} %norm.1.own_ref, bf16[512,1024]{1,0:T(8,128)(2,1)S(1)} %collective-permute-done.sib_ref, bf16[1024,8192]{1,0:T(8,128)(2,1)} %w_ref.7, bf16[1024,8192]{1,0:T(8,128)(2,1)} %collective-permute-done.1.ws_ref), custom_call_target="tpu_custom_call" | custom-call | tf_op jit(solution)/shard_map/project/pallas_call | solution.py:305
  53.0 1.7 %collective-permute-start.4 = (bf16[512,512]{1,0:T(8,128)(2,1)S(1)}, bf16[512,512]{1,0:T(8,128)(2,1)S(1)}, u32[]{:S(2)}, u32[]{:S(2)}) collective-permute-start(bf16[512,512]{1,0:T(8,128)(2,1)S(1)} %get-tuple-element.35), channel_id=1, source_target_pairs={{0,2},{1,3},{2,4},{3,5},{4,6},{5,7},{6,0},{7,1},{8,10},{9,11},{10,... | collective-permute-start | bytes 1572872 | tf_op jit(solution)/shard_map/ppermute | solution.py:415
  54.6 1.7 %collective-permute-start.5 = (bf16[512,512]{1,0:T(8,128)(2,1)S(1)}, bf16[512,512]{1,0:T(8,128)(2,1)S(1)}, u32[]{:S(2)}, u32[]{:S(2)}) collective-permute-start(bf16[512,512]{1,0:T(8,128)(2,1)S(1)} %get-tuple-element.36), channel_id=1, source_target_pairs={{0,6},{1,7},{2,0},{3,1},{4,2},{5,3},{6,4},{7,5},{8,14},{9,15},{10,... | collective-permute-start | bytes 1572872 | tf_op jit(solution)/shard_map/ppermute | solution.py:415
  56.3 4.8 %project.4 = (bf16[512,512]{1,0:T(8,128)(2,1)S(1)}, bf16[512,512]{1,0:T(8,128)(2,1)S(1)}) custom-call(s32[1]{0:T(128)} %bitcast.place_ref, bf16[512,1024]{1,0:T(8,128)(2,1)S(1)} %norm.1.own_ref, bf16[512,1024]{1,0:T(8,128)(2,1)S(1)} %collective-permute-done.sib_ref, bf16[1024,8192]{1,0:T(8,128)(2,1)} %w_ref.7, bf16[1024,8192]{1,0:T(8,128)(2,1)} %collective-permute-done.1.ws_ref), custom_call_target="tpu_custom_call" | custom-call | tf_op jit(solution)/shard_map/project/pallas_call | solution.py:305
  61.1 1.9 %collective-permute-start.2 = (bf16[512,512]{1,0:T(8,128)(2,1)S(1)}, bf16[512,512]{1,0:T(8,128)(2,1)S(1)}, u32[]{:S(2)}, u32[]{:S(2)}) collective-permute-start(bf16[512,512]{1,0:T(8,128)(2,1)S(1)} %get-tuple-element.31), channel_id=1, source_target_pairs={{0,6},{1,7},{2,0},{3,1},{4,2},{5,3},{6,4},{7,5},{8,14},{9,15},{10,... | collective-permute-start | bytes 1572872 | tf_op jit(solution)/shard_map/ppermute | solution.py:417
  63.0 0.2 collective-permute-start.3
  63.2 5.8 %collective-permute-done.4.refs_0_ = bf16[512,512]{1,0:T(8,128)(2,1)S(1)} collective-permute-done((bf16[512,512]{1,0:T(8,128)(2,1)S(1)}, bf16[512,512]{1,0:T(8,128)(2,1)S(1)}, u32[]{:S(2)}, u32[]{:S(2)}) %collective-permute-start.4) | collective-permute-done | bytes 524320 | tf_op jit(solution)/shard_map/ppermute | solution.py:415
  69.0 0.4 collective-permute-done.5.refs_1_
  69.4 4.9 %project.7 = (bf16[512,512]{1,0:T(8,128)(2,1)S(1)}, bf16[512,512]{1,0:T(8,128)(2,1)S(1)}) custom-call(s32[1]{0:T(128)} %bitcast.place_ref, bf16[512,1024]{1,0:T(8,128)(2,1)S(1)} %norm.1.own_ref, bf16[512,1024]{1,0:T(8,128)(2,1)S(1)} %collective-permute-done.sib_ref, bf16[1024,8192]{1,0:T(8,128)(2,1)} %w_ref.7, ...), custom_call_target="tpu_custom_call" | custom-call | tf_op jit(solution)/shard_map/project/pallas_call | solution.py:305
  74.3 1.6 %collective-permute-start.6 = (bf16[512,512]{1,0:T(8,128)(2,1)S(1)}, bf16[512,512]{1,0:T(8,128)(2,1)S(1)}, u32[]{:S(2)}, u32[]{:S(2)}) collective-permute-start(bf16[512,512]{1,0:T(8,128)(2,1)S(1)} %get-tuple-element.37), channel_id=1, source_target_pairs={{0,2},{1,3},{2,4},{3,5},{4,6},{5,7},{6,0},{7,1},{8,10},{9,11},{10,... | collective-permute-start | bytes 1572872 | tf_op jit(solution)/shard_map/ppermute | solution.py:419
  76.0 1.7 %collective-permute-start.7 = (bf16[512,512]{1,0:T(8,128)(2,1)S(1)}, bf16[512,512]{1,0:T(8,128)(2,1)S(1)}, u32[]{:S(2)}, u32[]{:S(2)}) collective-permute-start(bf16[512,512]{1,0:T(8,128)(2,1)S(1)} %get-tuple-element.38), channel_id=1, source_target_pairs={{0,6},{1,7},{2,0},{3,1},{4,2},{5,3},{6,4},{7,5},{8,14},{9,15},{10,... | collective-permute-start | bytes 1572872 | tf_op jit(solution)/shard_map/ppermute | solution.py:419
  77.6 3.0 %collective-permute-done.2.refs_0_ = bf16[512,512]{1,0:T(8,128)(2,1)S(1)} collective-permute-done((bf16[512,512]{1,0:T(8,128)(2,1)S(1)}, bf16[512,512]{1,0:T(8,128)(2,1)S(1)}, u32[]{:S(2)}, u32[]{:S(2)}) %collective-permute-start.2) | collective-permute-done | bytes 524320 | tf_op jit(solution)/shard_map/ppermute | solution.py:417
  80.7 4.9 %project.5 = (f32[512,512]{1,0:T(8,128)S(1)}, f32[512,512]{1,0:T(8,128)S(1)}) custom-call(s32[1]{0:T(128)} %bitcast.place_ref, bf16[512,1024]{1,0:T(8,128)(2,1)S(1)} %norm.1.own_ref, bf16[512,1024]{1,0:T(8,128)(2,1)S(1)} %collective-permute-done.sib_ref, bf16[1024,8192]{1,0:T(8,128)(2,1)} %w_ref.7, bf16[1024,8192]{1,0:T(8,128)(2,1)} %collective-permute-done.1.ws_ref, ...), custom_call_target="tpu_custom_call" | custom-call | tf_op jit(solution)/shard_map/project/pallas_call | solution.py:305
  85.6 5.1 %collective-permute-done.6.a_ref = bf16[512,512]{1,0:T(8,128)(2,1)S(1)} collective-permute-done((bf16[512,512]{1,0:T(8,128)(2,1)S(1)}, bf16[512,512]{1,0:T(8,128)(2,1)S(1)}, u32[]{:S(2)}, u32[]{:S(2)}) %collective-permute-start.6) | collective-permute-done | bytes 524320 | tf_op jit(solution)/shard_map/ppermute | solution.py:419
  90.8 1.2 %final.1 = bf16[512,1024]{1,0:T(8,128)(2,1)} custom-call(f32[512,512]{1,0:T(8,128)S(1)} %get-tuple-element.33.m0_ref, f32[512,512]{1,0:T(8,128)S(1)} %get-tuple-element.34.m1_ref, bf16[512,512]{1,0:T(8,128)(2,1)S(1)} %collective-permute-done.6.a_ref, bf16[512,512]{1,0:T(8,128)(2,1)S(1)} %collective-permute-done.7.b_ref), custom_call_target="tpu_custom_call" | custom-call | tf_op jit(solution)/shard_map/final/pallas_call | solution.py:421
  (4 shorter events, 0.0 us)
Async XLA Ops:
  0.0 48.1 %collective-permute-start.1 = (bf16[1024,8192]{1,0:T(8,128)(2,1)}, bf16[1024,8192]{1,0:T(8,128)(2,1)}, u32[]{:S(2)}, u32[]{:S(2)}) collective-permute-start(bf16[1024,8192]{1,0:T(8,128)(2,1)} %w_ref.7), channel_id=1, source_target_pairs={{0,1},{1,0},{2,3},{3,2},{4,5},{5,4},{6,7},{7,6},{8,9},{9,8},{10,11... | collective-permute-start | bytes 50331656 | tf_op jit(solution)/shard_map/ppermute | solution.py:330
  30.8 12.2 %all-to-all-start.1 = ((bf16[16,8,1024]{2,1,0:T(8,128)(2,1)}), bf16[16,8,1024]{2,1,0:T(8,128)(2,1)S(1)}, u32[]{:S(2)}, u32[]{:S(2)}) async-start(bf16[16,8,1024]{2,1,0:T(8,128)(2,1)} %prefix.1.after_ref), calls=%async_computation.1 | async-start | bytes 524288 | tf_op jit(solution)/shard_map/all_to_all | solution.py:366
  45.4 2.7 %collective-permute-start = (bf16[512,1024]{1,0:T(8,128)(2,1)S(1)}, bf16[512,1024]{1,0:T(8,128)(2,1)S(1)}, u32[]{:S(2)}, u32[]{:S(2)}) collective-permute-start(bf16[512,1024]{1,0:T(8,128)(2,1)S(1)} %norm.1.own_ref), channel_id=1, source_target_pairs={{0,1},{1,0},{2,3},{3,2},{4,5},{5,4},{6,7},{7,6},{8,9},{9,8},{10,11... | collective-permute-start | bytes 3145736 | tf_op jit(solution)/shard_map/ppermute | solution.py:412
  53.0 16.0 %collective-permute-start.4 = (bf16[512,512]{1,0:T(8,128)(2,1)S(1)}, bf16[512,512]{1,0:T(8,128)(2,1)S(1)}, u32[]{:S(2)}, u32[]{:S(2)}) collective-permute-start(bf16[512,512]{1,0:T(8,128)(2,1)S(1)} %get-tuple-element.35), channel_id=1, source_target_pairs={{0,2},{1,3},{2,4},{3,5},{4,6},{5,7},{6,0},{7,1},{8,10},{9,11},{10,... | collective-permute-start | bytes 1572872 | tf_op jit(solution)/shard_map/ppermute | solution.py:415
  54.6 14.8 %collective-permute-start.5 = (bf16[512,512]{1,0:T(8,128)(2,1)S(1)}, bf16[512,512]{1,0:T(8,128)(2,1)S(1)}, u32[]{:S(2)}, u32[]{:S(2)}) collective-permute-start(bf16[512,512]{1,0:T(8,128)(2,1)S(1)} %get-tuple-element.36), channel_id=1, source_target_pairs={{0,6},{1,7},{2,0},{3,1},{4,2},{5,3},{6,4},{7,5},{8,14},{9,15},{10,... | collective-permute-start | bytes 1572872 | tf_op jit(solution)/shard_map/ppermute | solution.py:415
  61.1 19.6 %collective-permute-start.2 = (bf16[512,512]{1,0:T(8,128)(2,1)S(1)}, bf16[512,512]{1,0:T(8,128)(2,1)S(1)}, u32[]{:S(2)}, u32[]{:S(2)}) collective-permute-start(bf16[512,512]{1,0:T(8,128)(2,1)S(1)} %get-tuple-element.31), channel_id=1, source_target_pairs={{0,6},{1,7},{2,0},{3,1},{4,2},{5,3},{6,4},{7,5},{8,14},{9,15},{10,... | collective-permute-start | bytes 1572872 | tf_op jit(solution)/shard_map/ppermute | solution.py:417
  63.0 17.7 %collective-permute-start.3 = (bf16[512,512]{1,0:T(8,128)(2,1)S(1)}, bf16[512,512]{1,0:T(8,128)(2,1)S(1)}, u32[]{:S(2)}, u32[]{:S(2)}) collective-permute-start(bf16[512,512]{1,0:T(8,128)(2,1)S(1)} %get-tuple-element.32), channel_id=1, source_target_pairs={{0,2},{1,3},{2,4},{3,5},{4,6},{5,7},{6,0},{7,1},{8,10},{9,11},{10,... | collective-permute-start | bytes 1572872 | tf_op jit(solution)/shard_map/ppermute | solution.py:417
  74.3 16.4 %collective-permute-start.6 = (bf16[512,512]{1,0:T(8,128)(2,1)S(1)}, bf16[512,512]{1,0:T(8,128)(2,1)S(1)}, u32[]{:S(2)}, u32[]{:S(2)}) collective-permute-start(bf16[512,512]{1,0:T(8,128)(2,1)S(1)} %get-tuple-element.37), channel_id=1, source_target_pairs={{0,2},{1,3},{2,4},{3,5},{4,6},{5,7},{6,0},{7,1},{8,10},{9,11},{10,... | collective-permute-start | bytes 1572872 | tf_op jit(solution)/shard_map/ppermute | solution.py:419
  76.0 14.8 %collective-permute-start.7 = (bf16[512,512]{1,0:T(8,128)(2,1)S(1)}, bf16[512,512]{1,0:T(8,128)(2,1)S(1)}, u32[]{:S(2)}, u32[]{:S(2)}) collective-permute-start(bf16[512,512]{1,0:T(8,128)(2,1)S(1)} %get-tuple-element.38), channel_id=1, source_target_pairs={{0,6},{1,7},{2,0},{3,1},{4,2},{5,3},{6,4},{7,5},{8,14},{9,15},{10,... | collective-permute-start | bytes 1572872 | tf_op jit(solution)/shard_map/ppermute | solution.py:419

commit v5 on v4

v5 whole, which is shorter than its diff:
```python
import functools

import jax
import jax.numpy as jnp
from jax import lax
from jax.experimental import pallas as pl
from jax.experimental.pallas import tpu as pltpu
from jax.sharding import PartitionSpec as P

BF = jnp.bfloat16
F32 = jnp.float32
TOK = 512
HT = TOK // 2
BT = 128
EDGE = 3
MSG = 1152
WID = 1024
HALF = WID // 2
HEADS = 8
HW = 128
ST = 128
CTX = 16
SEQ = TOK * CTX
DECAY = 12.288 / SEQ / 63.0
SCALE = 1.0 / (ST * SEQ) ** 0.5
ROWS = 64
SD = jax.ShapeDtypeStruct


def silu(v):
    half = 0.5 * v
    return half + half * jnp.tanh(half)


def mm(a, b):
    return jnp.dot(a, b, preferred_element_type=F32)


def head_row(ref, factor, at=0):
    lane = lax.broadcasted_iota(jnp.int32, (1, HW), 1)
    row = jnp.zeros((1, HW), F32)
    for h in range(HEADS):
        row = jnp.where(lane == at + h, ref[h] * factor, row)
    return row


def spread(compact, lane, rows=None):
    column = compact[:, lane : lane + 1]
    return jnp.broadcast_to(column, (rows or compact.shape[0], HW))


def row_ids(rows, width):
    return lax.broadcasted_iota(jnp.int32, (rows, width), 0)


def conv_part(big, w_ref, bias, lo, hi):
    count = big.shape[0] // 8
    row = row_ids(8, hi - lo)
    total = bias + w_ref[3:4, lo:hi] * big[8:]
    for k in range(1, 4):
        rolled = [pltpu.roll(big[8 * t : 8 * t + 8], k, 0) for t in range(count)]
        moved = [jnp.where(row < k, rolled[t], rolled[t + 1]) for t in range(count - 1)]
        total = total + w_ref[3 - k : 4 - k, lo:hi] * jnp.concatenate(moved, axis=0)
    return total


def with_rim(ref, r, rows, lo, hi):
    body = ref[r : r + rows, lo:hi].astype(F32)
    if r == 0:
        return jnp.concatenate([jnp.zeros((8, hi - lo), F32), body], axis=0)
    return jnp.concatenate([ref[r - 16 : r, lo:hi].astype(F32)[8:], body], axis=0)


def code_sums(codes_ref, count=TOK):
    codes = jnp.concatenate([codes_ref[...].astype(F32), jnp.zeros((HW - HEADS, count), F32)], axis=0)
    row = lax.broadcasted_iota(jnp.int32, (count, count), 0)
    col = lax.broadcasted_iota(jnp.int32, (count, count), 1)
    return lax.dot_general(
        jnp.where(row >= col, 1.0, 0.0).astype(BF), codes.astype(BF), (((1,), (1,)), ((), ())),
        preferred_element_type=F32,
    )


def scan_in_body(
    rate_ref, x_hbm, bc_hbm, codes_hbm, cx_hbm, bx_hbm, cbc_hbm, bbc_hbm, xt_hbm, msg_ref,
    x_ref, bc_ref, codes_ref, cx_ref, bx_ref, cbc_ref, bbc_ref, xt_ref, b_ref, sems,
):
    chunks = [slice(r, r + BT) for r in range(0, TOK, BT)]
    pairs = [
        (codes_hbm, codes_ref), (bc_hbm, bc_ref), (cbc_hbm, cbc_ref), (bbc_hbm, bbc_ref), (cx_hbm, cx_ref),
        (bx_hbm, bx_ref),
    ]
    loads = [pltpu.make_async_copy(src, dst, sems.at[2, k]) for k, (src, dst) in enumerate(pairs)]

    def copy(src, dst, k, i):
        return pltpu.make_async_copy(src.at[chunks[i]], dst.at[chunks[i]], sems.at[k, i])

    for load in loads:
        load.start()
    for i in range(len(chunks)):
        copy(x_hbm, x_ref, 0, i).start()
    for load in loads[:4]:
        load.wait()
    cum = code_sums(codes_ref)
    grow = jnp.exp(head_row(rate_ref, DECAY) * cum)
    for r in range(0, TOK, ROWS):
        part = conv_part(with_rim(bc_ref, r, ROWS, 0, ST), cbc_ref, bbc_ref[:, :ST], 0, ST)
        b_ref[r : r + ROWS, :] = silu(part)
    bt = b_ref[...].T.astype(BF)
    for load in loads[4:]:
        load.wait()
    for i in range(len(chunks)):
        copy(x_hbm, x_ref, 0, i).wait()
        for r in range(i * BT, (i + 1) * BT, ROWS):
            for h in range(HEADS):
                lo, hi = h * HW, (h + 1) * HW
                part = conv_part(with_rim(x_ref, r, ROWS, lo, hi), cx_ref, bx_ref[:, lo:hi], lo, hi)
                xc = silu(part).astype(BF)
                scaled = xc.astype(F32) * spread(grow[r : r + ROWS, :], h)
                if r == 0:
                    scaled = jnp.where(row_ids(ROWS, HW) < EDGE, 0.0, scaled)
                xt_ref[r : r + ROWS, lo:hi] = scaled.astype(BF)
        copy(xt_ref, xt_hbm, 1, i).start()
    state = mm(bt, xt_ref[...])
    row = row_ids(8, WID)
    last = pltpu.roll(x_ref[TOK - 16 : TOK, :].astype(F32)[8:], EDGE, 0)
    head = pltpu.roll(x_ref[0:16, :].astype(F32)[0:8], EDGE, 0)
    bc_last = bc_ref[TOK - 16 : TOK, :].astype(F32)[8:]
    bc_head = bc_ref[0:16, :].astype(F32)[0:8]
    bc_rows = [bc_last[8 - EDGE + k : 9 - EDGE + k, :] for k in range(EDGE)]
    bc_row = jnp.concatenate(bc_rows + [jnp.zeros((1, WID - EDGE * 2 * ST), F32)], axis=1)
    rows = jnp.where(row < EDGE, last, jnp.where(row < 2 * EDGE, head, 0.0))
    rows = jnp.where(row == 2 * EDGE, jnp.broadcast_to(bc_row, (8, WID)), rows)
    row = row_ids(8, HW)
    total = cum[TOK - 1 : TOK, :]
    high = jnp.floor(total * (1.0 / 256.0))
    low = total - 256.0 * high
    heads = jnp.where(row < 5, pltpu.roll(cum[0:8, :], 2, 0), 0.0)
    heads = jnp.where(row == 0, high, jnp.where(row == 1, low, heads))
    heads = pltpu.roll(heads, HW // 2, 1)
    pad = jnp.zeros((HW - 8, HW), F32)
    none = jnp.zeros((8, ST), F32)
    b_last = conv_part(jnp.concatenate([bc_last[:, :ST], none], axis=0), cbc_ref, none[0:1], 0, ST)
    b_head = conv_part(jnp.concatenate([none, bc_head[:, :ST]], axis=0), cbc_ref, bbc_ref[:, :ST], 0, ST)
    b_last = jnp.concatenate([b_last, pad], axis=0).T
    b_head = jnp.concatenate([b_head, pad], axis=0).T
    for j in range(CTX):
        at = slice(8 * j, 8 * j + 8)
        msg_ref[j, :, 0:WID] = jnp.concatenate([state[at, :], rows], axis=0).astype(BF)
        side = jnp.concatenate([b_last[at, :] + heads, b_head[at, :]], axis=0)
        msg_ref[j, :, WID:MSG] = side.astype(BF)
    for i in range(len(chunks)):
        copy(xt_ref, xt_hbm, 1, i).wait()


def prefix_body(rate_ref, cx_ref, bx_ref, r_ref, after_ref, q_ref):
    rate = head_row(rate_ref, DECAY, HW // 2)
    state = jnp.zeros((8, WID), F32)
    before = jnp.zeros((8, WID), F32)
    side_before = jnp.zeros((8, HW), F32)
    edge_row = row_ids(8, WID) < EDGE
    for c in range(CTX):
        main = r_ref[c, :, 0:WID].astype(F32)
        side = r_ref[c, :, WID:MSG].astype(F32)
        rows = jnp.where(edge_row, before, main[8:16, :])
        before = main[8:16, :]
        pre = bx_ref[...] + cx_ref[0:1, :] * rows
        for k in range(1, 4):
            pre = pre + cx_ref[k : k + 1, :] * pltpu.roll(rows, 8 - k, 0)
        edge = silu(pre).astype(BF).astype(F32)
        heads = side[0:8, :]
        grow = jnp.exp(rate * pltpu.roll(heads, 6, 0))
        fade = jnp.exp(-rate * (256.0 * heads[0:1, :] + heads[1:2, :]))
        b_edge = silu(side_before + side[8:16, :]).astype(BF).astype(F32)
        side_before = heads
        parts = []
        for h in range(HEADS):
            lo, hi = h * HW, (h + 1) * HW
            scaled = (edge[:, lo:hi] * spread(grow, HW // 2 + h)).astype(BF).astype(F32)
            part = state[:, lo:hi]
            for k in range(EDGE):
                part = part + spread(b_edge, k) * jnp.broadcast_to(scaled[k : k + 1, :], (8, HW))
            q_ref[c, :, lo:hi] = part.astype(BF)
            parts.append(spread(fade, HW // 2 + h, 8) * (part + main[0:8, lo:hi]))
        state = jnp.concatenate(parts, axis=1)


def local_body(
    rate_ref, skip_ref, xt_ref, z_ref, codes_ref, bc_ref, cbc_ref, bbc_ref, a1_ref, a2_ref, cm_ref, gram, prod, bm,
):
    cum = code_sums(codes_ref)
    for r in range(0, TOK, ROWS):
        for ref, lo in ((bm, 0), (cm_ref, ST)):
            hi = lo + ST
            part = conv_part(with_rim(bc_ref, r, ROWS, lo, hi), cbc_ref, bbc_ref[:, lo:hi], lo, hi)
            ref[r : r + ROWS, :] = silu(part).astype(BF)
    for r in range(0, TOK, BT):
        size = r + BT
        part = lax.dot_general(
            cm_ref[r:size, :], bm[0:size, :], (((1,), (1,)), ((), ())), preferred_element_type=F32
        )
        row = lax.broadcasted_iota(jnp.int32, (BT, size), 0) + r
        col = lax.broadcasted_iota(jnp.int32, (BT, size), 1)
        gram[r:size, 0:size] = jnp.where(row >= col, part, 0.0).astype(BF)
        prod[r:size, :] = mm(gram[r:size, 0:size], xt_ref[0:size, :])
    fades = jnp.exp(head_row(rate_ref, -DECAY) * cum)
    for r in range(0, TOK, ROWS):
        rs = slice(r, r + ROWS)
        for h in range(HEADS):
            lo, hi = h * HW, (h + 1) * HW
            gate = silu(z_ref[rs, lo:hi].astype(F32))
            fade = spread(fades[rs, :], h)
            total = prod[rs, lo:hi] * SCALE + skip_ref[h] * xt_ref[rs, lo:hi].astype(F32)
            fade = fade * gate
            a1_ref[rs, lo:hi] = (total * fade).astype(BF)
            a2_ref[rs, lo:hi] = (SCALE * fade).astype(BF)


def patch_body(
    place_ref, rate_ref, skip_ref, got_ref, x_ref, bc_ref, z_ref, codes_ref, cx_ref, bx_ref, cbc_ref, bbc_ref,
    after_ref, a1_ref, cm_ref, xe, be,
):
    live = place_ref[0] > 0
    rim = got_ref[0, 8:16, 0:WID].astype(F32)
    xe[0:8, :] = jnp.where(live, pltpu.roll(rim, 8 - EDGE, 0), 0.0)
    xe[8:24, :] = x_ref[...].astype(F32)
    for k in range(EDGE):
        part = rim[2 * EDGE : 2 * EDGE + 1, k * 2 * ST : (k + 1) * 2 * ST]
        be[8 - EDGE + k : 9 - EDGE + k, :] = jnp.where(live, part, 0.0)
    be[8:24, :] = bc_ref[...].astype(F32)
    cum = code_sums(codes_ref, HW)[0:16, :]
    grow = jnp.exp(head_row(rate_ref, DECAY) * cum)
    fades = jnp.exp(head_row(rate_ref, -DECAY) * cum)
    bm = silu(conv_part(be[:, :ST], cbc_ref, bbc_ref[:, :ST], 0, ST)).astype(BF)
    cm = silu(conv_part(be[:, ST:], cbc_ref, bbc_ref[:, ST:], ST, 2 * ST)).astype(BF)
    cm_ref[...] = cm
    part = lax.dot_general(cm, bm, (((1,), (1,)), ((), ())), preferred_element_type=F32)
    row = lax.broadcasted_iota(jnp.int32, (16, 16), 0)
    col = lax.broadcasted_iota(jnp.int32, (16, 16), 1)
    edge = jnp.where(row < col, -part, 0.0)
    gram = jnp.where(col < EDGE, edge, jnp.where(row >= col, part, 0.0)).astype(BF)
    for h in range(HEADS):
        lo, hi = h * HW, (h + 1) * HW
        xc = silu(conv_part(xe[:, lo:hi], cx_ref, bx_ref[:, lo:hi], lo, hi)).astype(BF).astype(F32)
        total = mm(gram, (xc * spread(grow, h)).astype(BF))
        gate = silu(z_ref[:, lo:hi].astype(F32))
        a1_ref[:, lo:hi] = ((total * (SCALE * spread(fades, h)) + skip_ref[h] * xc) * gate).astype(BF)


def norm_body(first, q_ref, a1_ref, a2_ref, c_ref, gain_ref, *refs):
    n_ref, prod = refs[-2:]
    state = q_ref[...].astype(F32).reshape(ST, WID).astype(BF)
    prod[...] = mm(c_ref[...], state)
    if first:
        prod[0:16, :] = mm(refs[1][...], state)
    for r in range(0, HT, ROWS):
        for h in range(HEADS):
            rs, hs = slice(r, r + ROWS), slice(h * HW, (h + 1) * HW)
            local = a1_ref[rs, hs]
            if first and r == 0:
                local = jnp.concatenate([refs[0][:, hs], local[16:, :]], axis=0)
            gated = local.astype(F32) + a2_ref[rs, hs].astype(F32) * prod[rs, hs]
            power = jnp.mean(gated * gated, axis=-1, keepdims=True)
            n_ref[rs, hs] = (gated * lax.rsqrt(power + 1e-05) * gain_ref[:, hs]).astype(BF)


def project_body(parts, adds, place_ref, *refs):
    step = pl.program_id(0)
    owns, sibs, (w_ref, ws_ref), rest = refs[:parts], refs[parts : 2 * parts], refs[2 * parts : 2 * parts + 2], refs[
        2 * parts + 2 :
    ]
    outs = rest[-2:]
    for k in range(2):

        @pl.when(step // 2 == k)
        def _():
            for p in range(parts):
                total = mm(owns[p][...], w_ref[...]) + mm(sibs[p][...], ws_ref[...])
                rows = slice(p * HT, (p + 1) * HT)
                mine = rest[adds * k : adds * (k + 1)]
                if adds == 2:
                    total = total + mine[p][...].astype(F32)
                elif adds == 1:
                    total = total + mine[0][rows, :].astype(F32)
                outs[k][rows, :] = total.astype(outs[k].dtype)


def final_body(m0_ref, m1_ref, a_ref, b_ref, o_ref):
    o_ref[:, :HALF] = (m0_ref[...] + a_ref[...].astype(F32)).astype(BF)
    o_ref[:, HALF:] = (m1_ref[...] + b_ref[...].astype(F32)).astype(BF)


def params(dims=1):
    return pltpu.CompilerParams(
        dimension_semantics=("arbitrary",) * dims if dims else None, vmem_limit_bytes=20 << 20
    )


SMEM = pl.BlockSpec(memory_space=pltpu.SMEM)
VMEM = pl.BlockSpec(memory_space=pltpu.VMEM)
ANY = pl.BlockSpec(memory_space=pl.ANY)


def whole(*shape):
    return pl.BlockSpec(shape, lambda i: (0,) * len(shape))


def in_hbm(a):
    return pltpu.with_memory_space_constraint(a, pltpu.HBM)


QUART = HALF // 2


def project(place, owns, sibs, w, w_sib, targets, addends, kind):
    def column(i, place_ref):
        index = place_ref[0]
        far = jnp.where(i < 2, targets[0][0], targets[1][0])
        side = jnp.where(i < 2, targets[0][1], targets[1][1])
        return 0, ((((index >> 1) + far) & 3) * 2 + (index & 1)) * 4 + side * 2 + (i & 1)

    parts = len(owns)
    tokens = pl.BlockSpec((HT, WID), lambda i, ix: (0, 0))
    weight = pl.BlockSpec((WID, QUART), column)

    def halves(rows):
        return [
            pl.BlockSpec((rows, QUART), lambda i, ix: (0, jnp.minimum(i, 1))),
            pl.BlockSpec((rows, QUART), lambda i, ix: (0, jnp.maximum(i - 2, 0))),
        ]

    count = len(addends[0])
    add_specs = [halves(a.shape[0])[k] for k in range(2) for a in addends[k]]
    return pl.pallas_call(
        functools.partial(project_body, parts, count),
        out_shape=[SD((parts * HT, HALF), kind)] * 2,
        grid_spec=pltpu.PrefetchScalarGridSpec(
            num_scalar_prefetch=1,
            grid=(4,),
            in_specs=[tokens] * (2 * parts) + [weight, weight] + add_specs,
            out_specs=halves(parts * HT),
        ),
        compiler_params=params(),
        name="project",
    )(place, *owns, *sibs, w, w_sib, *addends[0], *addends[1])


def body(
    x_in, bc_in, z_in, codes, head_rate, conv_x, conv_bc, bias_x, bias_bc, skip, norm_gain, w_out
):
    place = lax.axis_index("tp")
    where = jnp.full((1,), place, jnp.int32)
    x_in, bc_in, z_in, w_out = in_hbm(x_in), in_hbm(bc_in), in_hbm(z_in), in_hbm(w_out)
    codes, conv_x, conv_bc = in_hbm(codes.T), in_hbm(conv_x), in_hbm(conv_bc)
    head_rate, skip = in_hbm(head_rate), in_hbm(skip)
    bias_x, bias_bc, gain = in_hbm(bias_x[None, :]), in_hbm(bias_bc[None, :]), in_hbm(norm_gain[None, :])

    swap = [(s, s ^ 1) for s in range(8)]
    w_sib = in_hbm(lax.ppermute(w_out, "tp", swap))
    taps = (conv_x, bias_x, conv_bc, bias_bc)
    buf = pltpu.VMEM
    xt, msg = pl.pallas_call(
        scan_in_body,
        in_specs=[SMEM] + [ANY] * 7,
        out_specs=[ANY, VMEM],
        out_shape=[pltpu.HBM((TOK, WID), BF), SD((CTX, 16, MSG), BF)],
        scratch_shapes=[
            buf((TOK, WID), BF), buf((TOK, 2 * ST), BF), buf((HEADS, TOK), jnp.int32), buf((4, WID), F32),
            buf((1, WID), F32), buf((4, 2 * ST), F32), buf((1, 2 * ST), F32), buf((TOK, WID), BF), buf((TOK, ST), F32),
            pltpu.SemaphoreType.DMA((3, 8)),
        ],
        compiler_params=params(0),
        name="scan_in",
    )(head_rate, x_in, bc_in, codes, *taps)
    got = lax.all_to_all(msg, "ctx", 0, 0, tiled=True)

    a1, a2, c_map = pl.pallas_call(
        local_body,
        grid=(1,),
        in_specs=[
            SMEM, SMEM, whole(TOK, WID), whole(TOK, WID), whole(HEADS, TOK), whole(TOK, 2 * ST), whole(4, 2 * ST),
            whole(1, 2 * ST),
        ],
        out_specs=[whole(TOK, WID), whole(TOK, WID), whole(TOK, ST)],
        out_shape=[pltpu.HBM((TOK, WID), BF), pltpu.HBM((TOK, WID), BF), pltpu.HBM((TOK, ST), BF)],
        scratch_shapes=[buf((TOK, TOK), BF), buf((TOK, WID), F32), buf((TOK, ST), BF)],
        compiler_params=params(),
        name="local",
    )(head_rate, skip, in_hbm(xt), z_in, codes, bc_in, conv_bc, bias_bc)
    a1, a2, c_map = in_hbm(a1), in_hbm(a2), in_hbm(c_map)

    prefix = pl.pallas_call(
        prefix_body,
        in_specs=[SMEM, VMEM, VMEM, VMEM, ANY],
        out_specs=VMEM,
        out_shape=SD((CTX, 8, WID), BF),
        compiler_params=params(0),
        name="prefix",
    )(head_rate, conv_x, bias_x, got, a1)
    incoming = lax.all_to_all(prefix, "ctx", 0, 0, tiled=True)

    def fixed(*shape):
        return pl.BlockSpec(shape, lambda i, ix: (0,) * len(shape))

    ctx = jnp.full((1,), lax.axis_index("ctx"), jnp.int32)
    a_first, c_first = pl.pallas_call(
        patch_body,
        out_shape=[SD((16, WID), BF), SD((16, ST), BF)],
        grid_spec=pltpu.PrefetchScalarGridSpec(
            num_scalar_prefetch=1,
            grid=(1,),
            in_specs=[
                SMEM, SMEM, pl.BlockSpec((1, 16, MSG), lambda i, ix: (jnp.maximum(ix[0] - 1, 0), 0, 0)),
                fixed(16, WID), fixed(16, 2 * ST), fixed(16, WID), fixed(HEADS, HW), fixed(4, WID), fixed(1, WID),
                fixed(4, 2 * ST), fixed(1, 2 * ST), ANY,
            ],
            out_specs=[fixed(16, WID), fixed(16, ST)],
            scratch_shapes=[buf((24, WID), F32), buf((24, 2 * ST), F32)],
        ),
        compiler_params=params(),
        name="patch",
    )(ctx, head_rate, skip, got, x_in, bc_in, z_in, codes, *taps, prefix)

    def norm(half, first):
        rows = pl.BlockSpec((HT, WID), lambda i: (half, 0))
        return pl.pallas_call(
            functools.partial(norm_body, half == 0),
            grid=(1,),
            in_specs=[
                whole(CTX, 8, WID), rows, rows, pl.BlockSpec((HT, ST), lambda i: (half, 0)), whole(1, WID),
                *[ANY if half else whole(*a.shape) for a in first],
            ],
            out_specs=whole(HT, WID),
            out_shape=SD((HT, WID), BF),
            scratch_shapes=[buf((HT, WID), F32)],
            compiler_params=params(),
            name="norm",
        )(incoming, a1, a2, c_map, gain, *first)

    up = [(s, (s + 2) % 8) for s in range(8)]
    down = [(s, (s + 6) % 8) for s in range(8)]
    n0 = norm(0, (a_first, c_first))
    s0 = lax.ppermute(n0, "tp", swap)
    n1 = norm(1, (a_first,))
    s1 = lax.ppermute(n1, "tp", swap)
    far = ((2, 0), (2, 1))
    fl0, fr0 = project(where, (n0,), (s0,), w_out, w_sib, far, ((), ()), BF)
    fl0, fr0 = lax.ppermute(fl0, "tp", up), lax.ppermute(fr0, "tp", down)
    fl1, fr1 = project(where, (n1,), (s1,), w_out, w_sib, far, ((), ()), BF)
    fl1, fr1 = lax.ppermute(fl1, "tp", up), lax.ppermute(fr1, "tp", down)
    run = functools.partial(project, where, (n0, n1), (s0, s1), w_out, w_sib)
    above_r, below_l = run(((1, 1), (3, 0)), ((), ()), BF)
    from_r, from_l = lax.ppermute(above_r, "tp", up), lax.ppermute(below_l, "tp", down)
    above_l, below_r = run(((1, 0), (3, 1)), ((fl0, fl1), (fr0, fr1)), BF)
    last_l, last_r = lax.ppermute(above_l, "tp", up), lax.ppermute(below_r, "tp", down)
    here_l, here_r = run(((0, 0), (0, 1)), ((from_l,), (from_r,)), F32)
    return pl.pallas_call(
        final_body,
        in_specs=[VMEM] * 4,
        out_specs=VMEM,
        out_shape=SD((TOK, WID), BF),
        compiler_params=params(0),
        name="final",
    )(here_l, here_r, last_l, last_r)


def solution(mesh):
    in_specs = (
        P("ctx", "tp"),
        P("ctx", None),
        P("ctx", "tp"),
        P("ctx", "tp"),
        P("tp"),
        P(None, "tp"),
        P(),
        P("tp"),
        P(),
        P("tp"),
        P("tp"),
        P("tp", None),
    )
    out_specs = P("ctx", "tp")
    return jax.shard_map(body, mesh=mesh, in_specs=in_specs, out_specs=out_specs, check_vma=False)
```

time: 92.8 us -> 92.3 us (level)
  blocking collectives: 20.7 us -> 0 us
  starting transfers between devices: 12.3 us -> 24.2 us
  waiting for transfers between devices: 20.7 us -> 26.1 us
  Pallas kernels: 38.2 us -> 41.2 us
    all_to_all x1 -> x0, blocking collectives: 20.7 us -> none  [body(): got = lax.all_to_all(msg, 'ctx', 0, 0, tiled=True)]
    ppermute x3 -> x6, waiting for transfers between devices: 8.87 us -> 0.02 us  [the longest x2 0.01 us: body(): fl1, fr1 = (lax.ppermute(fl1, 'tp', up), lax.ppermute(fr1, 'tp', down))]
    all_to_all x0 -> x1, waiting for transfers between devices: none -> 8.17 us  [body(): got = lax.all_to_all(msg, 'ctx', 0, 0, tiled=True)]
    all_to_all x0 -> x1, starting transfers between devices: none -> 7.97 us  [body(): got = lax.all_to_all(msg, 'ctx', 0, 0, tiled=True)]
    ppermute x3 -> x6, starting transfers between devices: 3.39 us -> 7.27 us  [the longest x2 3.31 us: body(): fl0, fr0 = (lax.ppermute(fl0, 'tp', up), lax.ppermute(fr0, 'tp', down))]
    all_to_all x1, waiting for transfers between devices: 3.62 us -> 7.45 us  [body(): incoming = lax.all_to_all(prefix, 'ctx', 0, 0, tiled=True)]
    pallas_call x8 -> x11, Pallas kernels: 37 us -> 40 us  [the longest x5 22.6 us: project(): pl.pallas_call(functools.partial(project_body, parts, count), out_shape=[...]
    ppermute x1, waiting for transfers between devices: 0.01 us -> 1.81 us  [body(): lax.ppermute(above_r, 'tp', up)]
  transfers between devices with their start and end apart: 9 -> 13, of which waited for: 6 -> 5; matrix products, arithmetic and copies ran while one was open for 0% -> 0% of each run, Pallas kernels for 35% -> 44%
where the time goes in v5:
time: 92.3 us; the launch traced here: 91.5 us
  Pallas kernels  41.2 us (45%)
  waiting for transfers between devices  26.1 us (28%)
  starting transfers between devices  24.2 us (26%)
    pallas_call x5, Pallas kernels, project(): pl.pallas_call(functools.partial(project_body, parts, count), out_shape=[...  22.6 us
    all_to_all x1, waiting for transfers between devices, body(): got = lax.all_to_all(msg, 'ctx', 0, 0, tiled=True)  8.17 us
    all_to_all x1, starting transfers between devices, body(): got = lax.all_to_all(msg, 'ctx', 0, 0, tiled=True)  7.97 us
    all_to_all x1, waiting for transfers between devices, body(): incoming = lax.all_to_all(prefix, 'ctx', 0, 0, tiled=True)  7.45 us
    pallas_call x1, Pallas kernels, body(): pl.pallas_call(scan_in_body, in_specs=[SMEM] + [ANY] * 7, out_specs=[ANY,...  5.69 us
    pallas_call x1, Pallas kernels, body(): pl.pallas_call(local_body, grid=(1,), in_specs=[SMEM, SMEM, whole(TOK, WI...  4.74 us
    ppermute x1, waiting for transfers between devices, body(): lax.ppermute(below_l, 'tp', down)  4.59 us
    ppermute x1, waiting for transfers between devices, body(): lax.ppermute(above_l, 'tp', up)  4.02 us
  transfers between devices with their start and end apart: 13, of which 5 were waited for; matrix products, arithmetic and copies ran while one was open for 0% of the time, Pallas kernels for 44%

profile of v5, /device:TPU:0, one launch (start us, length us, event | category | flops | bytes accessed | tf_op | source)
XLA Modules:
  0.0 91.5 jit_solution(8465306657587418506)
XLA Ops:
  0.0 5.7 %scan_in.1 = (bf16[512,1024]{1,0:T(8,128)(2,1)}, bf16[16,16,1152]{2,1,0:T(8,128)(2,1)}) custom-call(f32[8]{0:T(128)} %rate_ref.7, bf16[512,1024]{1,0:T(8,128)(2,1)} %x_ref.1, bf16[512,256]{1,0:T(8,128)(2,1)} %bc_ref.3, s32[8,512]{1,0:T(8,128)} %bitcast.6, f32[4,1024]{1,0:T(4,128)} %cx_ref.3, f32[1,1024]{1,0:T(1,128)} %bitcast.9, f32[4,256]{1,0:T(4,128)} %cbc_ref.3, ...), custom_call_target="tpu_custom_call" | custom-call | tf_op jit(solution)/shard_map/scan_in/pallas_call | solution.py:362
  5.7 8.0 %all-to-all-start = ((bf16[16,16,1152]{2,1,0:T(8,128)(2,1)}), bf16[16,16,1152]{2,1,0:T(8,128)(2,1)S(1)}, u32[]{:S(2)}, u32[]{:S(2)}) async-start(bf16[16,16,1152]{2,1,0:T(8,128)(2,1)} %get-tuple-element.22), calls=%async_computation | async-start | bytes 1179648 | tf_op jit(solution)/shard_map/all_to_all | solution.py:375
  13.7 4.7 %local.1 = (bf16[512,1024]{1,0:T(8,128)(2,1)}, bf16[512,1024]{1,0:T(8,128)(2,1)}, bf16[512,128]{1,0:T(8,128)(2,1)}) custom-call(f32[8]{0:T(128)} %rate_ref.7, f32[8]{0:T(128)} %skip_ref.3, bf16[512,1024]{1,0:T(8,128)(2,1)} %get-tuple-element.23.xt_ref, bf16[512,1024]{1,0:T(8,128)(2,1)} %z_ref.3, s32[8,512]{1,0:T(8,128)} %bitcast.7, bf16[512,256]{1,0:T(8,128)(2,1)} %bc_ref.3, ...), custom_call_target="tpu_custom_call" | custom-call | tf_op jit(solution)/shard_map/local/pallas_call | solution.py:377
  18.4 8.2 %all-to-all-done.r_ref.got_ref = bf16[16,16,1152]{2,1,0:T(8,128)(2,1)S(1)} async-done(((bf16[16,16,1152]{2,1,0:T(8,128)(2,1)}), bf16[16,16,1152]{2,1,0:T(8,128)(2,1)S(1)}, u32[]{:S(2)}, u32[]{:S(2)}) %all-to-all-start) | async-done | bytes 589856 | tf_op jit(solution)/shard_map/all_to_all | solution.py:375
  26.6 2.2 %prefix.1.after_ref = bf16[16,8,1024]{2,1,0:T(8,128)(2,1)} custom-call(f32[8]{0:T(128)} %rate_ref.7, f32[4,1024]{1,0:T(4,128)} %cx_ref.3, f32[1,1024]{1,0:T(1,128)} %bitcast.10, bf16[16,16,1152]{2,1,0:T(8,128)(2,1)S(1)} %all-to-all-done.r_ref.got_ref, bf16[512,1024]{1,0:T(8,128)(2,1)} %get-tuple-element.24.after_ref.a1_ref), custom_call_target="tpu_custom_call" | custom-call | tf_op jit(solution)/shard_map/prefix/pallas_call | solution.py:392
  28.8 3.5 %all-to-all-start.1 = ((bf16[16,8,1024]{2,1,0:T(8,128)(2,1)}), bf16[16,8,1024]{2,1,0:T(8,128)(2,1)S(1)}, u32[]{:S(2)}, u32[]{:S(2)}) async-start(bf16[16,8,1024]{2,1,0:T(8,128)(2,1)} %prefix.1.after_ref), calls=%async_computation.1 | async-start | bytes 524288 | tf_op jit(solution)/shard_map/all_to_all | solution.py:400
  32.3 1.2 %patch.1 = (bf16[16,1024]{1,0:T(8,128)(2,1)S(1)}, bf16[16,128]{1,0:T(8,128)(2,1)S(1)}) custom-call(s32[1]{0:T(128)} %bitcast.5.place_ref, f32[8]{0:T(128)} %rate_ref.7, f32[8]{0:T(128)} %skip_ref.3, bf16[16,16,1152]{2,1,0:T(8,128)(2,1)S(1)} %all-to-all-done.r_ref.got_ref, bf16[512,1024]{1,0:T(8,128)(2,1)} %x_ref.1, bf16[512,256]{1,0:T(8,128)(2,1)} %bc_ref.3, ...), custom_call_target="tpu_custom_call" | custom-call | tf_op jit(solution)/shard_map/patch/pallas_call | solution.py:406
  33.5 7.4 %all-to-all-done.1.q_ref = bf16[16,8,1024]{2,1,0:T(8,128)(2,1)S(1)} async-done(((bf16[16,8,1024]{2,1,0:T(8,128)(2,1)}), bf16[16,8,1024]{2,1,0:T(8,128)(2,1)S(1)}, u32[]{:S(2)}, u32[]{:S(2)}) %all-to-all-start.1) | async-done | bytes 262176 | tf_op jit(solution)/shard_map/all_to_all | solution.py:400
  41.0 1.8 %norm.3.refs_1_.refs_0_ = bf16[256,1024]{1,0:T(8,128)(2,1)S(1)} custom-call(bf16[16,8,1024]{2,1,0:T(8,128)(2,1)S(1)} %all-to-all-done.1.q_ref, bf16[512,1024]{1,0:T(8,128)(2,1)} %get-tuple-element.24.after_ref.a1_ref, bf16[512,1024]{1,0:T(8,128)(2,1)} %get-tuple-element.25.a2_ref, bf16[512,128]{1,0:T(8,128)(2,1)} %get-tuple-element.26.c_ref, ...), custom_call_target="tpu_custom_call" | custom-call | tf_op jit(solution)/shard_map/norm/pallas_call | solution.py:426
  42.8 1.8 %norm.2.refs_0_ = bf16[256,1024]{1,0:T(8,128)(2,1)S(1)} custom-call(bf16[16,8,1024]{2,1,0:T(8,128)(2,1)S(1)} %all-to-all-done.1.q_ref, bf16[512,1024]{1,0:T(8,128)(2,1)} %get-tuple-element.24.after_ref.a1_ref, bf16[512,1024]{1,0:T(8,128)(2,1)} %get-tuple-element.25.a2_ref, bf16[512,128]{1,0:T(8,128)(2,1)} %get-tuple-element.26.c_ref, f32[1,1024]{1,0:T(1,128)} %bitcast.13, ...), custom_call_target="tpu_custom_call" | custom-call | tf_op jit(solution)/shard_map/norm/pallas_call | solution.py:426
  45.2 4.0 %project.8 = (bf16[256,512]{1,0:T(8,128)(2,1)S(1)}, bf16[256,512]{1,0:T(8,128)(2,1)S(1)}) custom-call(s32[1]{0:T(128)} %bitcast.place_ref, bf16[256,1024]{1,0:T(8,128)(2,1)S(1)} %norm.3.refs_1_.refs_0_, bf16[256,1024]{1,0:T(8,128)(2,1)S(1)} %collective-permute-done.1.refs_3_.refs_1_, bf16[1024,8192]{1,0:T(8,128)(2,1)} %refs_4_.5, ...), custom_call_target="tpu_custom_call" | custom-call | tf_op jit(solution)/shard_map/project/pallas_call | solution.py:334
  49.2 1.6 %collective-permute-start.6 = (bf16[256,512]{1,0:T(8,128)(2,1)S(1)}, bf16[256,512]{1,0:T(8,128)(2,1)S(1)}, u32[]{:S(2)}, u32[]{:S(2)}) collective-permute-start(bf16[256,512]{1,0:T(8,128)(2,1)S(1)} %get-tuple-element.34), channel_id=1, source_target_pairs={{0,2},{1,3},{2,4},{3,5},{4,6},{5,7},{6,0},{7,1},{8,10},{9,11},{10,... | collective-permute-start | bytes 786440 | tf_op jit(solution)/shard_map/ppermute | solution.py:450
  50.8 1.7 %collective-permute-start.8 = (bf16[256,512]{1,0:T(8,128)(2,1)S(1)}, bf16[256,512]{1,0:T(8,128)(2,1)S(1)}, u32[]{:S(2)}, u32[]{:S(2)}) collective-permute-start(bf16[256,512]{1,0:T(8,128)(2,1)S(1)} %get-tuple-element.36), channel_id=1, source_target_pairs={{0,6},{1,7},{2,0},{3,1},{4,2},{5,3},{6,4},{7,5},{8,14},{9,15},{10,... | collective-permute-start | bytes 786440 | tf_op jit(solution)/shard_map/ppermute | solution.py:450
  52.5 4.0 %project.7 = (bf16[256,512]{1,0:T(8,128)(2,1)S(1)}, bf16[256,512]{1,0:T(8,128)(2,1)S(1)}) custom-call(s32[1]{0:T(128)} %bitcast.place_ref, bf16[256,1024]{1,0:T(8,128)(2,1)S(1)} %norm.2.refs_0_, bf16[256,1024]{1,0:T(8,128)(2,1)S(1)} %collective-permute-done.refs_2_.refs_1_, bf16[1024,8192]{1,0:T(8,128)(2,1)} %refs_4_.5, ...), custom_call_target="tpu_custom_call" | custom-call | tf_op jit(solution)/shard_map/project/pallas_call | solution.py:334
  56.9 2.9 %collective-permute-start.7 = (bf16[256,512]{1,0:T(8,128)(2,1)S(1)}, bf16[256,512]{1,0:T(8,128)(2,1)S(1)}, u32[]{:S(2)}, u32[]{:S(2)}) collective-permute-start(bf16[256,512]{1,0:T(8,128)(2,1)S(1)} %get-tuple-element.35), channel_id=1, source_target_pairs={{0,6},{1,7},{2,0},{3,1},{4,2},{5,3},{6,4},{7,5},{8,14},{9,15},{10,... | collective-permute-start | bytes 786440 | tf_op jit(solution)/shard_map/ppermute | solution.py:448
  59.8 4.8 %project.5 = (bf16[512,512]{1,0:T(8,128)(2,1)S(1)}, bf16[512,512]{1,0:T(8,128)(2,1)S(1)}) custom-call(s32[1]{0:T(128)} %bitcast.place_ref, bf16[256,1024]{1,0:T(8,128)(2,1)S(1)} %norm.2.refs_0_, bf16[256,1024]{1,0:T(8,128)(2,1)S(1)} %norm.3.refs_1_.refs_0_, bf16[256,1024]{1,0:T(8,128)(2,1)S(1)} %collective-permute-done.refs_2_.refs_1_, ...), custom_call_target="tpu_custom_call" | custom-call | tf_op jit(solution)/shard_map/project/pallas_call | solution.py:334
  65.3 1.4 %collective-permute-start.4 = (bf16[512,512]{1,0:T(8,128)(2,1)S(1)}, bf16[512,512]{1,0:T(8,128)(2,1)S(1)}, u32[]{:S(2)}, u32[]{:S(2)}) collective-permute-start(bf16[512,512]{1,0:T(8,128)(2,1)S(1)} %get-tuple-element.30), channel_id=1, source_target_pairs={{0,2},{1,3},{2,4},{3,5},{4,6},{5,7},{6,0},{7,1},{8,10},{9,11},{10,... | collective-permute-start | bytes 1572872 | tf_op jit(solution)/shard_map/ppermute | solution.py:453
  66.7 4.9 %project.9 = (bf16[512,512]{1,0:T(8,128)(2,1)S(1)}, bf16[512,512]{1,0:T(8,128)(2,1)S(1)}) custom-call(s32[1]{0:T(128)} %bitcast.place_ref, bf16[256,1024]{1,0:T(8,128)(2,1)S(1)} %norm.2.refs_0_, bf16[256,1024]{1,0:T(8,128)(2,1)S(1)} %norm.3.refs_1_.refs_0_, bf16[256,1024]{1,0:T(8,128)(2,1)S(1)} %collective-permute-done.refs_2_.refs_1_, ...), custom_call_target="tpu_custom_call" | custom-call | tf_op jit(solution)/shard_map/project/pallas_call | solution.py:334
  71.7 3.2 %collective-permute-start.10 = (bf16[512,512]{1,0:T(8,128)(2,1)S(1)}, bf16[512,512]{1,0:T(8,128)(2,1)S(1)}, u32[]{:S(2)}, u32[]{:S(2)}) collective-permute-start(bf16[512,512]{1,0:T(8,128)(2,1)S(1)} %get-tuple-element.38), channel_id=1, source_target_pairs={{0,6},{1,7},{2,0},{3,1},{4,2},{5,3},{6,4},{7,5},{8,14},{9,15},{10,... | collective-permute-start | bytes 1572872 | tf_op jit(solution)/shard_map/ppermute | solution.py:455
  75.0 4.6 %collective-permute-done.3.refs_6_ = bf16[512,512]{1,0:T(8,128)(2,1)S(1)} collective-permute-done((bf16[512,512]{1,0:T(8,128)(2,1)S(1)}, bf16[512,512]{1,0:T(8,128)(2,1)S(1)}, u32[]{:S(2)}, u32[]{:S(2)}) %collective-permute-start.3) | collective-permute-done | bytes 524320 | tf_op jit(solution)/shard_map/ppermute | solution.py:453
  79.6 1.8 %collective-permute-done.4.refs_7_ = bf16[512,512]{1,0:T(8,128)(2,1)S(1)} collective-permute-done((bf16[512,512]{1,0:T(8,128)(2,1)S(1)}, bf16[512,512]{1,0:T(8,128)(2,1)S(1)}, u32[]{:S(2)}, u32[]{:S(2)}) %collective-permute-start.4) | collective-permute-done | bytes 524320 | tf_op jit(solution)/shard_map/ppermute | solution.py:453
  81.4 4.9 %project.6 = (f32[512,512]{1,0:T(8,128)S(1)}, f32[512,512]{1,0:T(8,128)S(1)}) custom-call(s32[1]{0:T(128)} %bitcast.place_ref, bf16[256,1024]{1,0:T(8,128)(2,1)S(1)} %norm.2.refs_0_, bf16[256,1024]{1,0:T(8,128)(2,1)S(1)} %norm.3.refs_1_.refs_0_, bf16[256,1024]{1,0:T(8,128)(2,1)S(1)} %collective-permute-done.refs_2_.refs_1_, ...), custom_call_target="tpu_custom_call" | custom-call | tf_op jit(solution)/shard_map/project/pallas_call | solution.py:334
  86.3 4.0 %collective-permute-done.9.a_ref = bf16[512,512]{1,0:T(8,128)(2,1)S(1)} collective-permute-done((bf16[512,512]{1,0:T(8,128)(2,1)S(1)}, bf16[512,512]{1,0:T(8,128)(2,1)S(1)}, u32[]{:S(2)}, u32[]{:S(2)}) %collective-permute-start.9) | collective-permute-done | bytes 524320 | tf_op jit(solution)/shard_map/ppermute | solution.py:455
  90.3 1.2 %final.1 = bf16[512,1024]{1,0:T(8,128)(2,1)} custom-call(f32[512,512]{1,0:T(8,128)S(1)} %get-tuple-element.31.m0_ref, f32[512,512]{1,0:T(8,128)S(1)} %get-tuple-element.32.m1_ref, bf16[512,512]{1,0:T(8,128)(2,1)S(1)} %collective-permute-done.9.a_ref, bf16[512,512]{1,0:T(8,128)(2,1)S(1)} %collective-permute-done.10.b_ref), custom_call_target="tpu_custom_call" | custom-call | tf_op jit(solution)/shard_map/final/pallas_call | solution.py:457
  (14 shorter events, 1.9 us)
Async XLA Ops:
  0.0 45.2 %collective-permute-start.2 = (bf16[1024,8192]{1,0:T(8,128)(2,1)}, bf16[1024,8192]{1,0:T(8,128)(2,1)}, u32[]{:S(2)}, u32[]{:S(2)}) collective-permute-start(bf16[1024,8192]{1,0:T(8,128)(2,1)} %refs_4_.5), channel_id=1, source_target_pairs={{0,1},{1,0},{2,3},{3,2},{4,5},{5,4},{6,7},{7,6},{8,9},{9,8},{10,11... | collective-permute-start | bytes 50331656 | tf_op jit(solution)/shard_map/ppermute | solution.py:359
  5.7 20.9 %all-to-all-start = ((bf16[16,16,1152]{2,1,0:T(8,128)(2,1)}), bf16[16,16,1152]{2,1,0:T(8,128)(2,1)S(1)}, u32[]{:S(2)}, u32[]{:S(2)}) async-start(bf16[16,16,1152]{2,1,0:T(8,128)(2,1)} %get-tuple-element.22), calls=%async_computation | async-start | bytes 1179648 | tf_op jit(solution)/shard_map/all_to_all | solution.py:375
  28.8 12.2 %all-to-all-start.1 = ((bf16[16,8,1024]{2,1,0:T(8,128)(2,1)}), bf16[16,8,1024]{2,1,0:T(8,128)(2,1)S(1)}, u32[]{:S(2)}, u32[]{:S(2)}) async-start(bf16[16,8,1024]{2,1,0:T(8,128)(2,1)} %prefix.1.after_ref), calls=%async_computation.1 | async-start | bytes 524288 | tf_op jit(solution)/shard_map/all_to_all | solution.py:400
  42.7 2.4 %collective-permute-start.1 = (bf16[256,1024]{1,0:T(8,128)(2,1)S(1)}, bf16[256,1024]{1,0:T(8,128)(2,1)S(1)}, u32[]{:S(2)}, u32[]{:S(2)}) collective-permute-start(bf16[256,1024]{1,0:T(8,128)(2,1)S(1)} %norm.3.refs_1_.refs_0_), channel_id=1, source_target_pairs={{0,1},{1,0},{2,3},{3,2},{4,5},{5,4},{6,7},{7,6},{8,9},{9,8},{10,11... | collective-permute-start | bytes 1572872 | tf_op jit(solution)/shard_map/ppermute | solution.py:445
  44.6 7.9 %collective-permute-start = (bf16[256,1024]{1,0:T(8,128)(2,1)S(1)}, bf16[256,1024]{1,0:T(8,128)(2,1)S(1)}, u32[]{:S(2)}, u32[]{:S(2)}) collective-permute-start(bf16[256,1024]{1,0:T(8,128)(2,1)S(1)} %norm.2.refs_0_), channel_id=1, source_target_pairs={{0,1},{1,0},{2,3},{3,2},{4,5},{5,4},{6,7},{7,6},{8,9},{9,8},{10,11... | collective-permute-start | bytes 1572872 | tf_op jit(solution)/shard_map/ppermute | solution.py:443
  49.2 16.1 %collective-permute-start.6 = (bf16[256,512]{1,0:T(8,128)(2,1)S(1)}, bf16[256,512]{1,0:T(8,128)(2,1)S(1)}, u32[]{:S(2)}, u32[]{:S(2)}) collective-permute-start(bf16[256,512]{1,0:T(8,128)(2,1)S(1)} %get-tuple-element.34), channel_id=1, source_target_pairs={{0,2},{1,3},{2,4},{3,5},{4,6},{5,7},{6,0},{7,1},{8,10},{9,11},{10,... | collective-permute-start | bytes 786440 | tf_op jit(solution)/shard_map/ppermute | solution.py:450
  50.8 15.9 %collective-permute-start.8 = (bf16[256,512]{1,0:T(8,128)(2,1)S(1)}, bf16[256,512]{1,0:T(8,128)(2,1)S(1)}, u32[]{:S(2)}, u32[]{:S(2)}) collective-permute-start(bf16[256,512]{1,0:T(8,128)(2,1)S(1)} %get-tuple-element.36), channel_id=1, source_target_pairs={{0,6},{1,7},{2,0},{3,1},{4,2},{5,3},{6,4},{7,5},{8,14},{9,15},{10,... | collective-permute-start | bytes 786440 | tf_op jit(solution)/shard_map/ppermute | solution.py:450
  56.5 10.2 %collective-permute-start.5 = (bf16[256,512]{1,0:T(8,128)(2,1)S(1)}, bf16[256,512]{1,0:T(8,128)(2,1)S(1)}, u32[]{:S(2)}, u32[]{:S(2)}) collective-permute-start(bf16[256,512]{1,0:T(8,128)(2,1)S(1)} %get-tuple-element.33), channel_id=1, source_target_pairs={{0,2},{1,3},{2,4},{3,5},{4,6},{5,7},{6,0},{7,1},{8,10},{9,11},{10,... | collective-permute-start | bytes 786440 | tf_op jit(solution)/shard_map/ppermute | solution.py:448
  56.9 9.8 %collective-permute-start.7 = (bf16[256,512]{1,0:T(8,128)(2,1)S(1)}, bf16[256,512]{1,0:T(8,128)(2,1)S(1)}, u32[]{:S(2)}, u32[]{:S(2)}) collective-permute-start(bf16[256,512]{1,0:T(8,128)(2,1)S(1)} %get-tuple-element.35), channel_id=1, source_target_pairs={{0,6},{1,7},{2,0},{3,1},{4,2},{5,3},{6,4},{7,5},{8,14},{9,15},{10,... | collective-permute-start | bytes 786440 | tf_op jit(solution)/shard_map/ppermute | solution.py:448
  64.6 14.9 %collective-permute-start.3 = (bf16[512,512]{1,0:T(8,128)(2,1)S(1)}, bf16[512,512]{1,0:T(8,128)(2,1)S(1)}, u32[]{:S(2)}, u32[]{:S(2)}) collective-permute-start(bf16[512,512]{1,0:T(8,128)(2,1)S(1)} %get-tuple-element.29), channel_id=1, source_target_pairs={{0,6},{1,7},{2,0},{3,1},{4,2},{5,3},{6,4},{7,5},{8,14},{9,15},{10,... | collective-permute-start | bytes 1572872 | tf_op jit(solution)/shard_map/ppermute | solution.py:453
  65.3 16.1 %collective-permute-start.4 = (bf16[512,512]{1,0:T(8,128)(2,1)S(1)}, bf16[512,512]{1,0:T(8,128)(2,1)S(1)}, u32[]{:S(2)}, u32[]{:S(2)}) collective-permute-start(bf16[512,512]{1,0:T(8,128)(2,1)S(1)} %get-tuple-element.30), channel_id=1, source_target_pairs={{0,2},{1,3},{2,4},{3,5},{4,6},{5,7},{6,0},{7,1},{8,10},{9,11},{10,... | collective-permute-start | bytes 1572872 | tf_op jit(solution)/shard_map/ppermute | solution.py:453
  71.7 18.6 %collective-permute-start.9 = (bf16[512,512]{1,0:T(8,128)(2,1)S(1)}, bf16[512,512]{1,0:T(8,128)(2,1)S(1)}, u32[]{:S(2)}, u32[]{:S(2)}) collective-permute-start(bf16[512,512]{1,0:T(8,128)(2,1)S(1)} %get-tuple-element.37), channel_id=1, source_target_pairs={{0,2},{1,3},{2,4},{3,5},{4,6},{5,7},{6,0},{7,1},{8,10},{9,11},{10,... | collective-permute-start | bytes 1572872 | tf_op jit(solution)/shard_map/ppermute | solution.py:455
  71.7 18.6 %collective-permute-start.10 = (bf16[512,512]{1,0:T(8,128)(2,1)S(1)}, bf16[512,512]{1,0:T(8,128)(2,1)S(1)}, u32[]{:S(2)}, u32[]{:S(2)}) collective-permute-start(bf16[512,512]{1,0:T(8,128)(2,1)S(1)} %get-tuple-element.38), channel_id=1, source_target_pairs={{0,6},{1,7},{2,0},{3,1},{4,2},{5,3},{6,4},{7,5},{8,14},{9,15},{10,... | collective-permute-start | bytes 1572872 | tf_op jit(solution)/shard_map/ppermute | solution.py:455

commit v6 on v5

--- a/solution.py
+++ b/solution.py
@@ -247,42 +247,87 @@
         a1_ref[:, lo:hi] = ((total * (SCALE * spread(fades, h)) + skip_ref[h] * xc) * gate).astype(BF)
 
 
-def norm_body(first, q_ref, a1_ref, a2_ref, c_ref, gain_ref, *refs):
-    n_ref, prod = refs[-2:]
+def norm_body(half, q_ref, a1_hbm, a2_hbm, c_hbm, gain_hbm, first_ref, cm_ref, n_ref, a1_ref, a2_ref, c_ref, gain_ref, prod, sems):
+    tokens = pl.ds(half * HT, HT)
+    pairs = [
+        (c_hbm.at[tokens], c_ref), (a1_hbm.at[tokens], a1_ref), (a2_hbm.at[tokens], a2_ref), (gain_hbm, gain_ref),
+    ]
+    loads = [pltpu.make_async_copy(src, dst, sems.at[k]) for k, (src, dst) in enumerate(pairs)]
+    for load in loads:
+        load.start()
     state = q_ref[...].astype(F32).reshape(ST, WID).astype(BF)
+    loads[0].wait()
     prod[...] = mm(c_ref[...], state)
-    if first:
-        prod[0:16, :] = mm(refs[1][...], state)
+    if half == 0:
+        prod[0:16, :] = mm(cm_ref[...], state)
+    for load in loads[1:]:
+        load.wait()
     for r in range(0, HT, ROWS):
         for h in range(HEADS):
             rs, hs = slice(r, r + ROWS), slice(h * HW, (h + 1) * HW)
             local = a1_ref[rs, hs]
-            if first and r == 0:
-                local = jnp.concatenate([refs[0][:, hs], local[16:, :]], axis=0)
+            if half == 0 and r == 0:
+                local = jnp.concatenate([first_ref[:, hs], local[16:, :]], axis=0)
             gated = local.astype(F32) + a2_ref[rs, hs].astype(F32) * prod[rs, hs]
             power = jnp.mean(gated * gated, axis=-1, keepdims=True)
             n_ref[rs, hs] = (gated * lax.rsqrt(power + 1e-05) * gain_ref[:, hs]).astype(BF)
 
 
-def project_body(parts, adds, place_ref, *refs):
-    step = pl.program_id(0)
-    owns, sibs, (w_ref, ws_ref), rest = refs[:parts], refs[parts : 2 * parts], refs[2 * parts : 2 * parts + 2], refs[
-        2 * parts + 2 :
+def target_column(place_ref, far, side):
+    index = place_ref[0]
+    column = ((((index >> 1) + far) & 3) * 2 + (index & 1)) * WID + side * HALF
+    return pl.multiple_of(column, HALF)
+
+
+def fetch_body(place_ref, w_hbm, ws_hbm, after_ref, own_ref, sib_ref, token_ref, sems):
+    source = pl.ds(target_column(place_ref, 2, 0), WID)
+    loads = [
+        pltpu.make_async_copy(w_hbm.at[:, source], own_ref, sems.at[0]),
+        pltpu.make_async_copy(ws_hbm.at[:, source], sib_ref, sems.at[1]),
     ]
-    outs = rest[-2:]
-    for k in range(2):
-
-        @pl.when(step // 2 == k)
-        def _():
-            for p in range(parts):
-                total = mm(owns[p][...], w_ref[...]) + mm(sibs[p][...], ws_ref[...])
-                rows = slice(p * HT, (p + 1) * HT)
-                mine = rest[adds * k : adds * (k + 1)]
-                if adds == 2:
-                    total = total + mine[p][...].astype(F32)
-                elif adds == 1:
-                    total = total + mine[0][rows, :].astype(F32)
-                outs[k][rows, :] = total.astype(outs[k].dtype)
+    token_ref[...] = jnp.zeros((8, HW), F32)
+    for load in loads:
+        load.start()
+    for load in loads:
+        load.wait()
+
+
+def project_far_body(own_ref, sib_ref, w_ref, ws_ref, l_ref, r_ref):
+    for i in range(4):
+        at = slice(i * QUART, (i + 1) * QUART)
+        cols = slice((i & 1) * QUART, (i & 1) * QUART + QUART)
+        total = mm(own_ref[...], w_ref[:, at]) + mm(sib_ref[...], ws_ref[:, at])
+        (l_ref, r_ref)[i // 2][:, cols] = total.astype(BF)
+
+
+def project_body(parts, adds, targets, place_ref, *refs):
+    owns, sibs = refs[:parts], refs[parts : 2 * parts]
+    weights = refs[2 * parts : 2 * parts + 2]
+    addends = refs[2 * parts + 2 : 2 * parts + 2 + 2 * adds]
+    outs = refs[-4:-2]
+    blocks, sems = refs[-2:]
+
+    def load(k, i):
+        column = target_column(place_ref, *targets[i // 2]) + (i & 1) * QUART
+        source = weights[k].at[:, pl.ds(pl.multiple_of(column, QUART), QUART)]
+        return pltpu.make_async_copy(source, blocks.at[k, i], sems.at[k, i])
+
+    for i in range(4):
+        for k in range(2):
+            load(k, i).start()
+    for i in range(4):
+        cols = slice((i & 1) * QUART, (i & 1) * QUART + QUART)
+        mine = addends[adds * (i // 2) : adds * (i // 2 + 1)]
+        for k in range(2):
+            load(k, i).wait()
+        for p in range(parts):
+            rows = slice(p * HT, (p + 1) * HT)
+            total = mm(owns[p][...], blocks[0, i]) + mm(sibs[p][...], blocks[1, i])
+            if adds == 2:
+                total = total + mine[p][:, cols].astype(F32)
+            elif adds == 1:
+                total = total + mine[0][rows, cols].astype(F32)
+            outs[i // 2][rows, cols] = total.astype(outs[i // 2].dtype)
 
 
 def final_body(m0_ref, m1_ref, a_ref, b_ref, o_ref):
@@ -290,9 +335,9 @@
     o_ref[:, HALF:] = (m1_ref[...] + b_ref[...].astype(F32)).astype(BF)
 
 
-def params(dims=1):
+def params(dims=1, room=20):
     return pltpu.CompilerParams(
-        dimension_semantics=("arbitrary",) * dims if dims else None, vmem_limit_bytes=20 << 20
+        dimension_semantics=("arbitrary",) * dims if dims else None, vmem_limit_bytes=room << 20
     )
 
 
@@ -313,34 +358,14 @@
 
 
 def project(place, owns, sibs, w, w_sib, targets, addends, kind):
-    def column(i, place_ref):
-        index = place_ref[0]
-        far = jnp.where(i < 2, targets[0][0], targets[1][0])
-        side = jnp.where(i < 2, targets[0][1], targets[1][1])
-        return 0, ((((index >> 1) + far) & 3) * 2 + (index & 1)) * 4 + side * 2 + (i & 1)
-
-    parts = len(owns)
-    tokens = pl.BlockSpec((HT, WID), lambda i, ix: (0, 0))
-    weight = pl.BlockSpec((WID, QUART), column)
-
-    def halves(rows):
-        return [
-            pl.BlockSpec((rows, QUART), lambda i, ix: (0, jnp.minimum(i, 1))),
-            pl.BlockSpec((rows, QUART), lambda i, ix: (0, jnp.maximum(i - 2, 0))),
-        ]
-
-    count = len(addends[0])
-    add_specs = [halves(a.shape[0])[k] for k in range(2) for a in addends[k]]
+    parts, count = len(owns), len(addends[0])
     return pl.pallas_call(
-        functools.partial(project_body, parts, count),
+        functools.partial(project_body, parts, count, targets),
         out_shape=[SD((parts * HT, HALF), kind)] * 2,
-        grid_spec=pltpu.PrefetchScalarGridSpec(
-            num_scalar_prefetch=1,
-            grid=(4,),
-            in_specs=[tokens] * (2 * parts) + [weight, weight] + add_specs,
-            out_specs=halves(parts * HT),
-        ),
-        compiler_params=params(),
+        in_specs=[SMEM] + [VMEM] * (2 * parts) + [ANY, ANY] + [VMEM] * (2 * count),
+        out_specs=[VMEM, VMEM],
+        scratch_shapes=[pltpu.VMEM((2, 4, WID, QUART), BF), pltpu.SemaphoreType.DMA((2, 4))],
+        compiler_params=params(0),
         name="project",
     )(place, *owns, *sibs, w, w_sib, *addends[0], *addends[1])
 
@@ -402,6 +427,26 @@
     def fixed(*shape):
         return pl.BlockSpec(shape, lambda i, ix: (0,) * len(shape))
 
+    far_own, far_sib, token = pl.pallas_call(
+        fetch_body,
+        in_specs=[SMEM, ANY, ANY, ANY],
+        out_specs=[VMEM] * 3,
+        out_shape=[SD((WID, WID), BF)] * 2 + [SD((8, HW), F32)],
+        scratch_shapes=[pltpu.SemaphoreType.DMA((2,))],
+        compiler_params=params(0, 2),
+        name="fetch",
+    )(where, w_out, w_sib, prefix)
+
+    def project_far(own, sib):
+        return pl.pallas_call(
+            project_far_body,
+            in_specs=[VMEM] * 4,
+            out_specs=[VMEM, VMEM],
+            out_shape=[SD((HT, HALF), BF)] * 2,
+            compiler_params=params(0, 6),
+            name="project_far",
+        )(own, sib, far_own, far_sib)
+
     ctx = jnp.full((1,), lax.axis_index("ctx"), jnp.int32)
     a_first, c_first = pl.pallas_call(
         patch_body,
@@ -417,36 +462,33 @@
             out_specs=[fixed(16, WID), fixed(16, ST)],
             scratch_shapes=[buf((24, WID), F32), buf((24, 2 * ST), F32)],
         ),
-        compiler_params=params(),
+        compiler_params=params(1, 6),
         name="patch",
-    )(ctx, head_rate, skip, got, x_in, bc_in, z_in, codes, *taps, prefix)
-
-    def norm(half, first):
-        rows = pl.BlockSpec((HT, WID), lambda i: (half, 0))
+    )(ctx, head_rate, skip, got, x_in, bc_in, z_in, codes, *taps, token)
+
+    def norm(half):
         return pl.pallas_call(
-            functools.partial(norm_body, half == 0),
-            grid=(1,),
-            in_specs=[
-                whole(CTX, 8, WID), rows, rows, pl.BlockSpec((HT, ST), lambda i: (half, 0)), whole(1, WID),
-                *[ANY if half else whole(*a.shape) for a in first],
+            functools.partial(norm_body, half),
+            in_specs=[VMEM] + [ANY] * 4 + [VMEM] * 2,
+            out_specs=VMEM,
+            out_shape=SD((HT, WID), BF),
+            scratch_shapes=[
+                buf((HT, WID), BF), buf((HT, WID), BF), buf((HT, ST), BF), buf((1, WID), F32), buf((HT, WID), F32),
+                pltpu.SemaphoreType.DMA((4,)),
             ],
-            out_specs=whole(HT, WID),
-            out_shape=SD((HT, WID), BF),
-            scratch_shapes=[buf((HT, WID), F32)],
-            compiler_params=params(),
+            compiler_params=params(0, 6),
             name="norm",
-        )(incoming, a1, a2, c_map, gain, *first)
+        )(incoming, a1, a2, c_map, gain, a_first, c_first)
 
     up = [(s, (s + 2) % 8) for s in range(8)]
     down = [(s, (s + 6) % 8) for s in range(8)]
-    n0 = norm(0, (a_first, c_first))
+    n0 = norm(0)
     s0 = lax.ppermute(n0, "tp", swap)
-    n1 = norm(1, (a_first,))
+    n1 = norm(1)
     s1 = lax.ppermute(n1, "tp", swap)
-    far = ((2, 0), (2, 1))
-    fl0, fr0 = project(where, (n0,), (s0,), w_out, w_sib, far, ((), ()), BF)
+    fl0, fr0 = project_far(n0, s0)
     fl0, fr0 = lax.ppermute(fl0, "tp", up), lax.ppermute(fr0, "tp", down)
-    fl1, fr1 = project(where, (n1,), (s1,), w_out, w_sib, far, ((), ()), BF)
+    fl1, fr1 = project_far(n1, s1)
     fl1, fr1 = lax.ppermute(fl1, "tp", up), lax.ppermute(fr1, "tp", down)
     run = functools.partial(project, where, (n0, n1), (s0, s1), w_out, w_sib)
     above_r, below_l = run(((1, 1), (3, 0)), ((), ()), BF)

time: 92.3 us -> 87.3 us (0.946)
  Pallas kernels: 41.2 us -> 35.5 us
  local copies, waits for them, and re-layouts: 0 us -> 2.92 us
  waiting for transfers between devices: 26.1 us -> 24 us
    pallas_call x7 -> x8, Pallas kernels: 26.2 us -> 20.6 us  [the longest x3 12.4 us: project(): pl.pallas_call(functools.partial(project_body, parts, count, targets), ou...]
    all_to_all x1, waiting for transfers between devices: 7.45 us -> 3.85 us  [body(): incoming = lax.all_to_all(prefix, 'ctx', 0, 0, tiled=True)]
    unnamed x0 -> x4, local copies, waits for them, and re-layouts: none -> 2.92 us
    ppermute x2, waiting for transfers between devices: 0.01 us -> 2.34 us  [body(): fl1, fr1 = (lax.ppermute(fl1, 'tp', up), lax.ppermute(fr1, 'tp', down))]
    ppermute x1, starting transfers between devices: 3.22 us -> 1.66 us  [body(): lax.ppermute(below_r, 'tp', down)]
    ppermute x1, starting transfers between devices: 0.09 us -> 1.64 us  [body(): lax.ppermute(above_l, 'tp', up)]
  transfers between devices with their start and end apart: 13 -> 13, of which waited for: 5 -> 7; matrix products, arithmetic and copies ran while one was open for 0% -> 0% of each run, Pallas kernels for 44% -> 38%
where the time goes in v6:
time: 87.3 us; the launch traced here: 86.7 us
  Pallas kernels  35.5 us (41%)
  starting transfers between devices  24.2 us (28%)
  waiting for transfers between devices  24 us (27%)
  local copies, waits for them, and re-layouts  2.92 us (3%)
    pallas_call x3, Pallas kernels, project(): pl.pallas_call(functools.partial(project_body, parts, count, targets), ou...  12.4 us
    all_to_all x1, waiting for transfers between devices, body(): got = lax.all_to_all(msg, 'ctx', 0, 0, tiled=True)  8.18 us
    all_to_all x1, starting transfers between devices, body(): got = lax.all_to_all(msg, 'ctx', 0, 0, tiled=True)  7.97 us
    pallas_call x1, Pallas kernels, body(): pl.pallas_call(scan_in_body, in_specs=[SMEM] + [ANY] * 7, out_specs=[ANY,...  5.7 us
    ppermute x1, waiting for transfers between devices, body(): lax.ppermute(above_l, 'tp', up)  4.74 us
    pallas_call x1, Pallas kernels, body(): pl.pallas_call(local_body, grid=(1,), in_specs=[SMEM, SMEM, whole(TOK, WI...  4.73 us
    all_to_all x1, waiting for transfers between devices, body(): incoming = lax.all_to_all(prefix, 'ctx', 0, 0, tiled=True)  3.85 us
    ppermute x1, waiting for transfers between devices, body(): lax.ppermute(below_l, 'tp', down)  3.77 us
  transfers between devices with their start and end apart: 13, of which 7 were waited for; matrix products, arithmetic and copies ran while one was open for 0% of the time, Pallas kernels for 38%

profile of v6, /device:TPU:0, one launch (start us, length us, event | category | flops | bytes accessed | tf_op | source)
XLA Modules:
  0.0 86.7 jit_solution(12415931841430084494)
XLA Ops:
  0.0 5.7 %scan_in.1 = (bf16[512,1024]{1,0:T(8,128)(2,1)}, bf16[16,16,1152]{2,1,0:T(8,128)(2,1)}) custom-call(f32[8]{0:T(128)} %rate_ref.7, bf16[512,1024]{1,0:T(8,128)(2,1)} %x_ref.1, bf16[512,256]{1,0:T(8,128)(2,1)} %bc_ref.3, s32[8,512]{1,0:T(8,128)} %bitcast.6, f32[4,1024]{1,0:T(4,128)} %cx_ref.3, f32[1,1024]{1,0:T(1,128)} %bitcast.9, f32[4,256]{1,0:T(4,128)} %cbc_ref.3, ...), custom_call_target="tpu_custom_call" | custom-call | tf_op jit(solution)/shard_map/scan_in/pallas_call | solution.py:387
  5.7 8.0 %all-to-all-start = ((bf16[16,16,1152]{2,1,0:T(8,128)(2,1)}), bf16[16,16,1152]{2,1,0:T(8,128)(2,1)S(1)}, u32[]{:S(2)}, u32[]{:S(2)}) async-start(bf16[16,16,1152]{2,1,0:T(8,128)(2,1)} %get-tuple-element.25), calls=%async_computation | async-start | bytes 1179648 | tf_op jit(solution)/shard_map/all_to_all | solution.py:400
  13.7 4.7 %local.1 = (bf16[512,1024]{1,0:T(8,128)(2,1)}, bf16[512,1024]{1,0:T(8,128)(2,1)}, bf16[512,128]{1,0:T(8,128)(2,1)}) custom-call(f32[8]{0:T(128)} %rate_ref.7, f32[8]{0:T(128)} %skip_ref.3, bf16[512,1024]{1,0:T(8,128)(2,1)} %get-tuple-element.26.xt_ref, bf16[512,1024]{1,0:T(8,128)(2,1)} %z_ref.3, s32[8,512]{1,0:T(8,128)} %bitcast.7, bf16[512,256]{1,0:T(8,128)(2,1)} %bc_ref.3, ...), custom_call_target="tpu_custom_call" | custom-call | tf_op jit(solution)/shard_map/local/pallas_call | solution.py:402
  18.4 8.2 %all-to-all-done.r_ref.got_ref = bf16[16,16,1152]{2,1,0:T(8,128)(2,1)S(1)} async-done(((bf16[16,16,1152]{2,1,0:T(8,128)(2,1)}), bf16[16,16,1152]{2,1,0:T(8,128)(2,1)S(1)}, u32[]{:S(2)}, u32[]{:S(2)}) %all-to-all-start) | async-done | bytes 589856 | tf_op jit(solution)/shard_map/all_to_all | solution.py:400
  26.6 2.2 %prefix.1.after_ref = bf16[16,8,1024]{2,1,0:T(8,128)(2,1)} custom-call(f32[8]{0:T(128)} %rate_ref.7, f32[4,1024]{1,0:T(4,128)} %cx_ref.3, f32[1,1024]{1,0:T(1,128)} %bitcast.10, bf16[16,16,1152]{2,1,0:T(8,128)(2,1)S(1)} %all-to-all-done.r_ref.got_ref, bf16[512,1024]{1,0:T(8,128)(2,1)} %get-tuple-element.27.after_ref.a1_hbm), custom_call_target="tpu_custom_call" | custom-call | tf_op jit(solution)/shard_map/prefix/pallas_call | solution.py:417
  28.8 3.5 %all-to-all-start.1 = ((bf16[16,8,1024]{2,1,0:T(8,128)(2,1)}), bf16[16,8,1024]{2,1,0:T(8,128)(2,1)S(1)}, u32[]{:S(2)}, u32[]{:S(2)}) async-start(bf16[16,8,1024]{2,1,0:T(8,128)(2,1)} %prefix.1.after_ref), calls=%async_computation.1 | async-start | bytes 524288 | tf_op jit(solution)/shard_map/all_to_all | solution.py:425
  32.3 2.3 %fetch.1 = (bf16[1024,1024]{1,0:T(8,128)(2,1)S(1)}, bf16[1024,1024]{1,0:T(8,128)(2,1)S(1)}, f32[8,128]{1,0:T(8,128)S(1)}) custom-call(s32[1]{0:T(128)} %bitcast.place_ref, bf16[1024,8192]{1,0:T(8,128)(2,1)} %refs_4_.5, bf16[1024,8192]{1,0:T(8,128)(2,1)} %collective-permute-done.ws_hbm.refs_5_, bf16[16,8,1024]{2,1,0:T(8,128)(2,1)} %prefix.1.after_ref), custom_call_target="tpu_custom_call" | custom-call | tf_op jit(solution)/shard_map/fetch/pallas_call | solution.py:430
  34.6 1.3 %copy-done = bf16[1024,1024]{1,0:T(8,128)(2,1)} copy-done((bf16[1024,1024]{1,0:T(8,128)(2,1)}, bf16[1024,1024]{1,0:T(8,128)(2,1)S(1)}, u32[]{:S(2)}) %copy-start) | copy-done | bytes 2097176
  37.1 3.8 %all-to-all-done.1.q_ref = bf16[16,8,1024]{2,1,0:T(8,128)(2,1)S(1)} async-done(((bf16[16,8,1024]{2,1,0:T(8,128)(2,1)}), bf16[16,8,1024]{2,1,0:T(8,128)(2,1)S(1)}, u32[]{:S(2)}, u32[]{:S(2)}) %all-to-all-start.1) | async-done | bytes 262176 | tf_op jit(solution)/shard_map/all_to_all | solution.py:425
  41.0 1.7 %norm.2.refs_0_.own_ref = bf16[256,1024]{1,0:T(8,128)(2,1)S(1)} custom-call(bf16[16,8,1024]{2,1,0:T(8,128)(2,1)S(1)} %all-to-all-done.1.q_ref, bf16[512,1024]{1,0:T(8,128)(2,1)} %get-tuple-element.27.after_ref.a1_hbm, bf16[512,1024]{1,0:T(8,128)(2,1)} %get-tuple-element.28.a2_hbm, bf16[512,128]{1,0:T(8,128)(2,1)} %get-tuple-element.29.c_hbm, ...), custom_call_target="tpu_custom_call" | custom-call | tf_op jit(solution)/shard_map/norm/pallas_call | solution.py:470
  42.8 1.7 %norm.3.refs_1_.own_ref = bf16[256,1024]{1,0:T(8,128)(2,1)S(1)} custom-call(bf16[16,8,1024]{2,1,0:T(8,128)(2,1)S(1)} %all-to-all-done.1.q_ref, bf16[512,1024]{1,0:T(8,128)(2,1)} %get-tuple-element.27.after_ref.a1_hbm, bf16[512,1024]{1,0:T(8,128)(2,1)} %get-tuple-element.28.a2_hbm, bf16[512,128]{1,0:T(8,128)(2,1)} %get-tuple-element.29.c_hbm, ...), custom_call_target="tpu_custom_call" | custom-call | tf_op jit(solution)/shard_map/norm/pallas_call | solution.py:470
  45.1 1.6 %copy-done.1 = bf16[1024,1024]{1,0:T(8,128)(2,1)S(1)} copy-done((bf16[1024,1024]{1,0:T(8,128)(2,1)S(1)}, bf16[1024,1024]{1,0:T(8,128)(2,1)}, u32[]{:S(2)}) %copy-start.1) | copy-done | bytes 2097176
  47.9 1.6 %collective-permute-start.5 = (bf16[256,512]{1,0:T(8,128)(2,1)S(1)}, bf16[256,512]{1,0:T(8,128)(2,1)S(1)}, u32[]{:S(2)}, u32[]{:S(2)}) collective-permute-start(bf16[256,512]{1,0:T(8,128)(2,1)S(1)} %get-tuple-element.39), channel_id=1, source_target_pairs={{0,2},{1,3},{2,4},{3,5},{4,6},{5,7},{6,0},{7,1},{8,10},{9,11},{10,... | collective-permute-start | bytes 786440 | tf_op jit(solution)/shard_map/ppermute | solution.py:490
  49.6 1.7 %collective-permute-start.7 = (bf16[256,512]{1,0:T(8,128)(2,1)S(1)}, bf16[256,512]{1,0:T(8,128)(2,1)S(1)}, u32[]{:S(2)}, u32[]{:S(2)}) collective-permute-start(bf16[256,512]{1,0:T(8,128)(2,1)S(1)} %get-tuple-element.41), channel_id=1, source_target_pairs={{0,6},{1,7},{2,0},{3,1},{4,2},{5,3},{6,4},{7,5},{8,14},{9,15},{10,... | collective-permute-start | bytes 786440 | tf_op jit(solution)/shard_map/ppermute | solution.py:490
  52.9 2.9 %collective-permute-start.8 = (bf16[256,512]{1,0:T(8,128)(2,1)S(1)}, bf16[256,512]{1,0:T(8,128)(2,1)S(1)}, u32[]{:S(2)}, u32[]{:S(2)}) collective-permute-start(bf16[256,512]{1,0:T(8,128)(2,1)S(1)} %get-tuple-element.42), channel_id=1, source_target_pairs={{0,6},{1,7},{2,0},{3,1},{4,2},{5,3},{6,4},{7,5},{8,14},{9,15},{10,... | collective-permute-start | bytes 786440 | tf_op jit(solution)/shard_map/ppermute | solution.py:492
  55.8 4.1 %project.3 = (bf16[512,512]{1,0:T(8,128)(2,1)S(1)}, bf16[512,512]{1,0:T(8,128)(2,1)S(1)}) custom-call(s32[1]{0:T(128)} %bitcast.place_ref, bf16[256,1024]{1,0:T(8,128)(2,1)S(1)} %norm.2.refs_0_.own_ref, bf16[256,1024]{1,0:T(8,128)(2,1)S(1)} %norm.3.refs_1_.own_ref, bf16[256,1024]{1,0:T(8,128)(2,1)S(1)} %collective-permute-done.1.refs_2_.sib_ref, ...), custom_call_target="tpu_custom_call" | custom-call | tf_op jit(solution)/shard_map/project/pallas_call | solution.py:362
  60.6 1.4 %collective-permute-start.4 = (bf16[512,512]{1,0:T(8,128)(2,1)S(1)}, bf16[512,512]{1,0:T(8,128)(2,1)S(1)}, u32[]{:S(2)}, u32[]{:S(2)}) collective-permute-start(bf16[512,512]{1,0:T(8,128)(2,1)S(1)} %get-tuple-element.34), channel_id=1, source_target_pairs={{0,2},{1,3},{2,4},{3,5},{4,6},{5,7},{6,0},{7,1},{8,10},{9,11},{10,... | collective-permute-start | bytes 1572872 | tf_op jit(solution)/shard_map/ppermute | solution.py:495
  63.1 1.3 %collective-permute-done.8.refs_9_ = bf16[256,512]{1,0:T(8,128)(2,1)S(1)} collective-permute-done((bf16[256,512]{1,0:T(8,128)(2,1)S(1)}, bf16[256,512]{1,0:T(8,128)(2,1)S(1)}, u32[]{:S(2)}, u32[]{:S(2)}) %collective-permute-start.8) | collective-permute-done | bytes 262176 | tf_op jit(solution)/shard_map/ppermute | solution.py:492
  64.4 4.1 %project.5 = (bf16[512,512]{1,0:T(8,128)(2,1)S(1)}, bf16[512,512]{1,0:T(8,128)(2,1)S(1)}) custom-call(s32[1]{0:T(128)} %bitcast.place_ref, bf16[256,1024]{1,0:T(8,128)(2,1)S(1)} %norm.2.refs_0_.own_ref, bf16[256,1024]{1,0:T(8,128)(2,1)S(1)} %norm.3.refs_1_.own_ref, bf16[256,1024]{1,0:T(8,128)(2,1)S(1)} %collective-permute-done.1.refs_2_.sib_ref, ...), custom_call_target="tpu_custom_call" | custom-call | tf_op jit(solution)/shard_map/project/pallas_call | solution.py:362
  68.5 1.6 %collective-permute-start.9 = (bf16[512,512]{1,0:T(8,128)(2,1)S(1)}, bf16[512,512]{1,0:T(8,128)(2,1)S(1)}, u32[]{:S(2)}, u32[]{:S(2)}) collective-permute-start(bf16[512,512]{1,0:T(8,128)(2,1)S(1)} %get-tuple-element.43), channel_id=1, source_target_pairs={{0,2},{1,3},{2,4},{3,5},{4,6},{5,7},{6,0},{7,1},{8,10},{9,11},{10,... | collective-permute-start | bytes 1572872 | tf_op jit(solution)/shard_map/ppermute | solution.py:497
  70.2 1.7 %collective-permute-start.10 = (bf16[512,512]{1,0:T(8,128)(2,1)S(1)}, bf16[512,512]{1,0:T(8,128)(2,1)S(1)}, u32[]{:S(2)}, u32[]{:S(2)}) collective-permute-start(bf16[512,512]{1,0:T(8,128)(2,1)S(1)} %get-tuple-element.44), channel_id=1, source_target_pairs={{0,6},{1,7},{2,0},{3,1},{4,2},{5,3},{6,4},{7,5},{8,14},{9,15},{10,... | collective-permute-start | bytes 1572872 | tf_op jit(solution)/shard_map/ppermute | solution.py:497
  71.8 3.8 %collective-permute-done.3.refs_6_ = bf16[512,512]{1,0:T(8,128)(2,1)S(1)} collective-permute-done((bf16[512,512]{1,0:T(8,128)(2,1)S(1)}, bf16[512,512]{1,0:T(8,128)(2,1)S(1)}, u32[]{:S(2)}, u32[]{:S(2)}) %collective-permute-start.3) | collective-permute-done | bytes 524320 | tf_op jit(solution)/shard_map/ppermute | solution.py:495
  76.7 4.1 %project.4 = (f32[512,512]{1,0:T(8,128)S(1)}, f32[512,512]{1,0:T(8,128)S(1)}) custom-call(s32[1]{0:T(128)} %bitcast.place_ref, bf16[256,1024]{1,0:T(8,128)(2,1)S(1)} %norm.2.refs_0_.own_ref, bf16[256,1024]{1,0:T(8,128)(2,1)S(1)} %norm.3.refs_1_.own_ref, bf16[256,1024]{1,0:T(8,128)(2,1)S(1)} %collective-permute-done.1.refs_2_.sib_ref, ...), custom_call_target="tpu_custom_call" | custom-call | tf_op jit(solution)/shard_map/project/pallas_call | solution.py:362
  80.8 4.7 %collective-permute-done.9.a_ref = bf16[512,512]{1,0:T(8,128)(2,1)S(1)} collective-permute-done((bf16[512,512]{1,0:T(8,128)(2,1)S(1)}, bf16[512,512]{1,0:T(8,128)(2,1)S(1)}, u32[]{:S(2)}, u32[]{:S(2)}) %collective-permute-start.9) | collective-permute-done | bytes 524320 | tf_op jit(solution)/shard_map/ppermute | solution.py:497
  (19 shorter events, 8.8 us)
Async XLA Ops:
  0.0 32.3 %collective-permute-start = (bf16[1024,8192]{1,0:T(8,128)(2,1)}, bf16[1024,8192]{1,0:T(8,128)(2,1)}, u32[]{:S(2)}, u32[]{:S(2)}) collective-permute-start(bf16[1024,8192]{1,0:T(8,128)(2,1)} %refs_4_.5), channel_id=1, source_target_pairs={{0,1},{1,0},{2,3},{3,2},{4,5},{5,4},{6,7},{7,6},{8,9},{9,8},{10,11... | collective-permute-start | bytes 50331656 | tf_op jit(solution)/shard_map/ppermute | solution.py:384
  5.7 20.9 %all-to-all-start = ((bf16[16,16,1152]{2,1,0:T(8,128)(2,1)}), bf16[16,16,1152]{2,1,0:T(8,128)(2,1)S(1)}, u32[]{:S(2)}, u32[]{:S(2)}) async-start(bf16[16,16,1152]{2,1,0:T(8,128)(2,1)} %get-tuple-element.25), calls=%async_computation | async-start | bytes 1179648 | tf_op jit(solution)/shard_map/all_to_all | solution.py:400
  28.8 12.2 %all-to-all-start.1 = ((bf16[16,8,1024]{2,1,0:T(8,128)(2,1)}), bf16[16,8,1024]{2,1,0:T(8,128)(2,1)S(1)}, u32[]{:S(2)}, u32[]{:S(2)}) async-start(bf16[16,8,1024]{2,1,0:T(8,128)(2,1)} %prefix.1.after_ref), calls=%async_computation.1 | async-start | bytes 524288 | tf_op jit(solution)/shard_map/all_to_all | solution.py:425
  34.6 1.3 %copy-start = (bf16[1024,1024]{1,0:T(8,128)(2,1)}, bf16[1024,1024]{1,0:T(8,128)(2,1)S(1)}, u32[]{:S(2)}) copy-start(bf16[1024,1024]{1,0:T(8,128)(2,1)S(1)} %get-tuple-element.38.ws_ref) | copy-start | bytes 6291460
  42.7 2.4 %collective-permute-start.1 = (bf16[256,1024]{1,0:T(8,128)(2,1)S(1)}, bf16[256,1024]{1,0:T(8,128)(2,1)S(1)}, u32[]{:S(2)}, u32[]{:S(2)}) collective-permute-start(bf16[256,1024]{1,0:T(8,128)(2,1)S(1)} %norm.2.refs_0_.own_ref), channel_id=1, source_target_pairs={{0,1},{1,0},{2,3},{3,2},{4,5},{5,4},{6,7},{7,6},{8,9},{9,8},{10,11... | collective-permute-start | bytes 1572872 | tf_op jit(solution)/shard_map/ppermute | solution.py:486
  44.5 6.7 %collective-permute-start.2 = (bf16[256,1024]{1,0:T(8,128)(2,1)S(1)}, bf16[256,1024]{1,0:T(8,128)(2,1)S(1)}, u32[]{:S(2)}, u32[]{:S(2)}) collective-permute-start(bf16[256,1024]{1,0:T(8,128)(2,1)S(1)} %norm.3.refs_1_.own_ref), channel_id=1, source_target_pairs={{0,1},{1,0},{2,3},{3,2},{4,5},{5,4},{6,7},{7,6},{8,9},{9,8},{10,11... | collective-permute-start | bytes 1572872 | tf_op jit(solution)/shard_map/ppermute | solution.py:488
  45.1 1.6 %copy-start.1 = (bf16[1024,1024]{1,0:T(8,128)(2,1)S(1)}, bf16[1024,1024]{1,0:T(8,128)(2,1)}, u32[]{:S(2)}) copy-start(bf16[1024,1024]{1,0:T(8,128)(2,1)} %copy-done) | copy-start | bytes 6291460
  47.9 12.7 %collective-permute-start.5 = (bf16[256,512]{1,0:T(8,128)(2,1)S(1)}, bf16[256,512]{1,0:T(8,128)(2,1)S(1)}, u32[]{:S(2)}, u32[]{:S(2)}) collective-permute-start(bf16[256,512]{1,0:T(8,128)(2,1)S(1)} %get-tuple-element.39), channel_id=1, source_target_pairs={{0,2},{1,3},{2,4},{3,5},{4,6},{5,7},{6,0},{7,1},{8,10},{9,11},{10,... | collective-permute-start | bytes 786440 | tf_op jit(solution)/shard_map/ppermute | solution.py:490
  49.6 12.5 %collective-permute-start.7 = (bf16[256,512]{1,0:T(8,128)(2,1)S(1)}, bf16[256,512]{1,0:T(8,128)(2,1)S(1)}, u32[]{:S(2)}, u32[]{:S(2)}) collective-permute-start(bf16[256,512]{1,0:T(8,128)(2,1)S(1)} %get-tuple-element.41), channel_id=1, source_target_pairs={{0,6},{1,7},{2,0},{3,1},{4,2},{5,3},{6,4},{7,5},{8,14},{9,15},{10,... | collective-permute-start | bytes 786440 | tf_op jit(solution)/shard_map/ppermute | solution.py:490
  52.5 10.6 %collective-permute-start.6 = (bf16[256,512]{1,0:T(8,128)(2,1)S(1)}, bf16[256,512]{1,0:T(8,128)(2,1)S(1)}, u32[]{:S(2)}, u32[]{:S(2)}) collective-permute-start(bf16[256,512]{1,0:T(8,128)(2,1)S(1)} %get-tuple-element.40), channel_id=1, source_target_pairs={{0,2},{1,3},{2,4},{3,5},{4,6},{5,7},{6,0},{7,1},{8,10},{9,11},{10,... | collective-permute-start | bytes 786440 | tf_op jit(solution)/shard_map/ppermute | solution.py:492
  52.9 11.5 %collective-permute-start.8 = (bf16[256,512]{1,0:T(8,128)(2,1)S(1)}, bf16[256,512]{1,0:T(8,128)(2,1)S(1)}, u32[]{:S(2)}, u32[]{:S(2)}) collective-permute-start(bf16[256,512]{1,0:T(8,128)(2,1)S(1)} %get-tuple-element.42), channel_id=1, source_target_pairs={{0,6},{1,7},{2,0},{3,1},{4,2},{5,3},{6,4},{7,5},{8,14},{9,15},{10,... | collective-permute-start | bytes 786440 | tf_op jit(solution)/shard_map/ppermute | solution.py:492
  59.9 15.7 %collective-permute-start.3 = (bf16[512,512]{1,0:T(8,128)(2,1)S(1)}, bf16[512,512]{1,0:T(8,128)(2,1)S(1)}, u32[]{:S(2)}, u32[]{:S(2)}) collective-permute-start(bf16[512,512]{1,0:T(8,128)(2,1)S(1)} %get-tuple-element.33), channel_id=1, source_target_pairs={{0,6},{1,7},{2,0},{3,1},{4,2},{5,3},{6,4},{7,5},{8,14},{9,15},{10,... | collective-permute-start | bytes 1572872 | tf_op jit(solution)/shard_map/ppermute | solution.py:495
  60.6 16.1 %collective-permute-start.4 = (bf16[512,512]{1,0:T(8,128)(2,1)S(1)}, bf16[512,512]{1,0:T(8,128)(2,1)S(1)}, u32[]{:S(2)}, u32[]{:S(2)}) collective-permute-start(bf16[512,512]{1,0:T(8,128)(2,1)S(1)} %get-tuple-element.34), channel_id=1, source_target_pairs={{0,2},{1,3},{2,4},{3,5},{4,6},{5,7},{6,0},{7,1},{8,10},{9,11},{10,... | collective-permute-start | bytes 1572872 | tf_op jit(solution)/shard_map/ppermute | solution.py:495
  68.5 17.0 %collective-permute-start.9 = (bf16[512,512]{1,0:T(8,128)(2,1)S(1)}, bf16[512,512]{1,0:T(8,128)(2,1)S(1)}, u32[]{:S(2)}, u32[]{:S(2)}) collective-permute-start(bf16[512,512]{1,0:T(8,128)(2,1)S(1)} %get-tuple-element.43), channel_id=1, source_target_pairs={{0,2},{1,3},{2,4},{3,5},{4,6},{5,7},{6,0},{7,1},{8,10},{9,11},{10,... | collective-permute-start | bytes 1572872 | tf_op jit(solution)/shard_map/ppermute | solution.py:497
  70.2 15.4 %collective-permute-start.10 = (bf16[512,512]{1,0:T(8,128)(2,1)S(1)}, bf16[512,512]{1,0:T(8,128)(2,1)S(1)}, u32[]{:S(2)}, u32[]{:S(2)}) collective-permute-start(bf16[512,512]{1,0:T(8,128)(2,1)S(1)} %get-tuple-element.44), channel_id=1, source_target_pairs={{0,6},{1,7},{2,0},{3,1},{4,2},{5,3},{6,4},{7,5},{8,14},{9,15},{10,... | collective-permute-start | bytes 1572872 | tf_op jit(solution)/shard_map/ppermute | solution.py:497

commit v7 on v6

--- a/solution.py
+++ b/solution.py
@@ -82,7 +82,7 @@
 
 
 def scan_in_body(
-    rate_ref, x_hbm, bc_hbm, codes_hbm, cx_hbm, bx_hbm, cbc_hbm, bbc_hbm, xt_hbm, msg_ref,
+    rate_ref, x_hbm, bc_hbm, codes_hbm, cx_hbm, bx_hbm, cbc_hbm, bbc_hbm, msg_ref, token_ref,
     x_ref, bc_ref, codes_ref, cx_ref, bx_ref, cbc_ref, bbc_ref, xt_ref, b_ref, sems,
 ):
     chunks = [slice(r, r + BT) for r in range(0, TOK, BT)]
@@ -90,15 +90,16 @@
         (codes_hbm, codes_ref), (bc_hbm, bc_ref), (cbc_hbm, cbc_ref), (bbc_hbm, bbc_ref), (cx_hbm, cx_ref),
         (bx_hbm, bx_ref),
     ]
-    loads = [pltpu.make_async_copy(src, dst, sems.at[2, k]) for k, (src, dst) in enumerate(pairs)]
-
-    def copy(src, dst, k, i):
-        return pltpu.make_async_copy(src.at[chunks[i]], dst.at[chunks[i]], sems.at[k, i])
-
+    loads = [pltpu.make_async_copy(src, dst, sems.at[1, k]) for k, (src, dst) in enumerate(pairs)]
+
+    def fetch(i):
+        return pltpu.make_async_copy(x_hbm.at[chunks[i]], x_ref.at[chunks[i]], sems.at[0, i])
+
+    token_ref[...] = jnp.zeros((8, HW), F32)
     for load in loads:
         load.start()
     for i in range(len(chunks)):
-        copy(x_hbm, x_ref, 0, i).start()
+        fetch(i).start()
     for load in loads[:4]:
         load.wait()
     cum = code_sums(codes_ref)
@@ -110,7 +111,7 @@
     for load in loads[4:]:
         load.wait()
     for i in range(len(chunks)):
-        copy(x_hbm, x_ref, 0, i).wait()
+        fetch(i).wait()
         for r in range(i * BT, (i + 1) * BT, ROWS):
             for h in range(HEADS):
                 lo, hi = h * HW, (h + 1) * HW
@@ -120,7 +121,6 @@
                 if r == 0:
                     scaled = jnp.where(row_ids(ROWS, HW) < EDGE, 0.0, scaled)
                 xt_ref[r : r + ROWS, lo:hi] = scaled.astype(BF)
-        copy(xt_ref, xt_hbm, 1, i).start()
     state = mm(bt, xt_ref[...])
     row = row_ids(8, WID)
     last = pltpu.roll(x_ref[TOK - 16 : TOK, :].astype(F32)[8:], EDGE, 0)
@@ -149,8 +149,6 @@
         msg_ref[j, :, 0:WID] = jnp.concatenate([state[at, :], rows], axis=0).astype(BF)
         side = jnp.concatenate([b_last[at, :] + heads, b_head[at, :]], axis=0)
         msg_ref[j, :, WID:MSG] = side.astype(BF)
-    for i in range(len(chunks)):
-        copy(xt_ref, xt_hbm, 1, i).wait()
 
 
 def prefix_body(rate_ref, cx_ref, bx_ref, r_ref, after_ref, q_ref):
@@ -186,9 +184,21 @@
 
 
 def local_body(
-    rate_ref, skip_ref, xt_ref, z_ref, codes_ref, bc_ref, cbc_ref, bbc_ref, a1_ref, a2_ref, cm_ref, gram, prod, bm,
+    rate_ref, skip_ref, x_ref, z_ref, codes_ref, bc_ref, cx_ref, bx_ref, cbc_ref, bbc_ref, after_ref, a1_ref, a2_ref,
+    cm_ref, gram, prod, bm, xc_ref, xt_ref,
 ):
     cum = code_sums(codes_ref)
+    grow = jnp.exp(head_row(rate_ref, DECAY) * cum)
+    for r in range(0, TOK, ROWS):
+        for h in range(HEADS):
+            lo, hi = h * HW, (h + 1) * HW
+            part = conv_part(with_rim(x_ref, r, ROWS, lo, hi), cx_ref, bx_ref[:, lo:hi], lo, hi)
+            xc = silu(part).astype(BF)
+            xc_ref[r : r + ROWS, lo:hi] = xc
+            scaled = xc.astype(F32) * spread(grow[r : r + ROWS, :], h)
+            if r == 0:
+                scaled = jnp.where(row_ids(ROWS, HW) < EDGE, 0.0, scaled)
+            xt_ref[r : r + ROWS, lo:hi] = scaled.astype(BF)
     for r in range(0, TOK, ROWS):
         for ref, lo in ((bm, 0), (cm_ref, ST)):
             hi = lo + ST
@@ -210,10 +220,10 @@
             lo, hi = h * HW, (h + 1) * HW
             gate = silu(z_ref[rs, lo:hi].astype(F32))
             fade = spread(fades[rs, :], h)
-            total = prod[rs, lo:hi] * SCALE + skip_ref[h] * xt_ref[rs, lo:hi].astype(F32)
-            fade = fade * gate
-            a1_ref[rs, lo:hi] = (total * fade).astype(BF)
-            a2_ref[rs, lo:hi] = (SCALE * fade).astype(BF)
+            fade = SCALE * fade
+            total = prod[rs, lo:hi] * fade + skip_ref[h] * xc_ref[rs, lo:hi].astype(F32)
+            a1_ref[rs, lo:hi] = (total * gate).astype(BF)
+            a2_ref[rs, lo:hi] = (fade * gate).astype(BF)
 
 
 def patch_body(
@@ -247,7 +257,11 @@
         a1_ref[:, lo:hi] = ((total * (SCALE * spread(fades, h)) + skip_ref[h] * xc) * gate).astype(BF)
 
 
-def norm_body(half, q_ref, a1_hbm, a2_hbm, c_hbm, gain_hbm, first_ref, cm_ref, n_ref, a1_ref, a2_ref, c_ref, gain_ref, prod, sems):
+def norm_body(half, place_ref, q_ref, a1_hbm, a2_hbm, c_hbm, gain_hbm, first_ref, cm_ref, ws_hbm, n_ref, *refs):
+    a1_ref, a2_ref, c_ref, gain_ref, prod, sems = refs[-6:]
+    if half == 0:
+        source = pl.ds(target_column(place_ref, 2, 0), WID)
+        weights = pltpu.make_async_copy(ws_hbm.at[:, source], refs[0], sems.at[4])
     tokens = pl.ds(half * HT, HT)
     pairs = [
         (c_hbm.at[tokens], c_ref), (a1_hbm.at[tokens], a1_ref), (a2_hbm.at[tokens], a2_ref), (gain_hbm, gain_ref),
@@ -255,6 +269,8 @@
     loads = [pltpu.make_async_copy(src, dst, sems.at[k]) for k, (src, dst) in enumerate(pairs)]
     for load in loads:
         load.start()
+    if half == 0:
+        weights.start()
     state = q_ref[...].astype(F32).reshape(ST, WID).astype(BF)
     loads[0].wait()
     prod[...] = mm(c_ref[...], state)
@@ -271,6 +287,8 @@
             gated = local.astype(F32) + a2_ref[rs, hs].astype(F32) * prod[rs, hs]
             power = jnp.mean(gated * gated, axis=-1, keepdims=True)
             n_ref[rs, hs] = (gated * lax.rsqrt(power + 1e-05) * gain_ref[:, hs]).astype(BF)
+    if half == 0:
+        weights.wait()
 
 
 def target_column(place_ref, far, side):
@@ -279,17 +297,11 @@
     return pl.multiple_of(column, HALF)
 
 
-def fetch_body(place_ref, w_hbm, ws_hbm, after_ref, own_ref, sib_ref, token_ref, sems):
-    source = pl.ds(target_column(place_ref, 2, 0), WID)
-    loads = [
-        pltpu.make_async_copy(w_hbm.at[:, source], own_ref, sems.at[0]),
-        pltpu.make_async_copy(ws_hbm.at[:, source], sib_ref, sems.at[1]),
-    ]
+def fetch_body(place_ref, w_hbm, after_ref, own_ref, token_ref, sem):
+    load = pltpu.make_async_copy(w_hbm.at[:, pl.ds(target_column(place_ref, 2, 0), WID)], own_ref, sem.at[0])
+    load.start()
     token_ref[...] = jnp.zeros((8, HW), F32)
-    for load in loads:
-        load.start()
-    for load in loads:
-        load.wait()
+    load.wait()
 
 
 def project_far_body(own_ref, sib_ref, w_ref, ws_ref, l_ref, r_ref):
@@ -384,15 +396,15 @@
     w_sib = in_hbm(lax.ppermute(w_out, "tp", swap))
     taps = (conv_x, bias_x, conv_bc, bias_bc)
     buf = pltpu.VMEM
-    xt, msg = pl.pallas_call(
+    msg, begun = pl.pallas_call(
         scan_in_body,
         in_specs=[SMEM] + [ANY] * 7,
-        out_specs=[ANY, VMEM],
-        out_shape=[pltpu.HBM((TOK, WID), BF), SD((CTX, 16, MSG), BF)],
+        out_specs=[VMEM, VMEM],
+        out_shape=[SD((CTX, 16, MSG), BF), SD((8, HW), F32)],
         scratch_shapes=[
             buf((TOK, WID), BF), buf((TOK, 2 * ST), BF), buf((HEADS, TOK), jnp.int32), buf((4, WID), F32),
             buf((1, WID), F32), buf((4, 2 * ST), F32), buf((1, 2 * ST), F32), buf((TOK, WID), BF), buf((TOK, ST), F32),
-            pltpu.SemaphoreType.DMA((3, 8)),
+            pltpu.SemaphoreType.DMA((2, 8)),
         ],
         compiler_params=params(0),
         name="scan_in",
@@ -403,15 +415,17 @@
         local_body,
         grid=(1,),
         in_specs=[
-            SMEM, SMEM, whole(TOK, WID), whole(TOK, WID), whole(HEADS, TOK), whole(TOK, 2 * ST), whole(4, 2 * ST),
-            whole(1, 2 * ST),
+            SMEM, SMEM, whole(TOK, WID), whole(TOK, WID), whole(HEADS, TOK), whole(TOK, 2 * ST), whole(4, WID),
+            whole(1, WID), whole(4, 2 * ST), whole(1, 2 * ST), ANY,
         ],
         out_specs=[whole(TOK, WID), whole(TOK, WID), whole(TOK, ST)],
         out_shape=[pltpu.HBM((TOK, WID), BF), pltpu.HBM((TOK, WID), BF), pltpu.HBM((TOK, ST), BF)],
-        scratch_shapes=[buf((TOK, TOK), BF), buf((TOK, WID), F32), buf((TOK, ST), BF)],
+        scratch_shapes=[
+            buf((TOK, TOK), BF), buf((TOK, WID), F32), buf((TOK, ST), BF), buf((TOK, WID), BF), buf((TOK, WID), BF),
+        ],
         compiler_params=params(),
         name="local",
-    )(head_rate, skip, in_hbm(xt), z_in, codes, bc_in, conv_bc, bias_bc)
+    )(head_rate, skip, x_in, z_in, codes, bc_in, *taps, begun)
     a1, a2, c_map = in_hbm(a1), in_hbm(a2), in_hbm(c_map)
 
     prefix = pl.pallas_call(
@@ -427,15 +441,15 @@
     def fixed(*shape):
         return pl.BlockSpec(shape, lambda i, ix: (0,) * len(shape))
 
-    far_own, far_sib, token = pl.pallas_call(
+    far_own, token = pl.pallas_call(
         fetch_body,
-        in_specs=[SMEM, ANY, ANY, ANY],
-        out_specs=[VMEM] * 3,
-        out_shape=[SD((WID, WID), BF)] * 2 + [SD((8, HW), F32)],
-        scratch_shapes=[pltpu.SemaphoreType.DMA((2,))],
+        in_specs=[SMEM, ANY, ANY],
+        out_specs=[VMEM, VMEM],
+        out_shape=[SD((WID, WID), BF), SD((8, HW), F32)],
+        scratch_shapes=[pltpu.SemaphoreType.DMA((1,))],
         compiler_params=params(0, 2),
         name="fetch",
-    )(where, w_out, w_sib, prefix)
+    )(where, w_out, prefix)
 
     def project_far(own, sib):
         return pl.pallas_call(
@@ -467,24 +481,25 @@
     )(ctx, head_rate, skip, got, x_in, bc_in, z_in, codes, *taps, token)
 
     def norm(half):
+        outs = [SD((HT, WID), BF)] + ([] if half else [SD((WID, WID), BF)])
         return pl.pallas_call(
             functools.partial(norm_body, half),
-            in_specs=[VMEM] + [ANY] * 4 + [VMEM] * 2,
-            out_specs=VMEM,
-            out_shape=SD((HT, WID), BF),
+            in_specs=[SMEM, VMEM] + [ANY] * 4 + [VMEM] * 2 + [ANY],
+            out_specs=[VMEM] * len(outs),
+            out_shape=outs,
             scratch_shapes=[
                 buf((HT, WID), BF), buf((HT, WID), BF), buf((HT, ST), BF), buf((1, WID), F32), buf((HT, WID), F32),
-                pltpu.SemaphoreType.DMA((4,)),
+                pltpu.SemaphoreType.DMA((5,)),
             ],
             compiler_params=params(0, 6),
             name="norm",
-        )(incoming, a1, a2, c_map, gain, a_first, c_first)
+        )(where, incoming, a1, a2, c_map, gain, a_first, c_first, w_sib)
 
     up = [(s, (s + 2) % 8) for s in range(8)]
     down = [(s, (s + 6) % 8) for s in range(8)]
-    n0 = norm(0)
+    n0, far_sib = norm(0)
     s0 = lax.ppermute(n0, "tp", swap)
-    n1 = norm(1)
+    (n1,) = norm(1)
     s1 = lax.ppermute(n1, "tp", swap)
     fl0, fr0 = project_far(n0, s0)
     fl0, fr0 = lax.ppermute(fl0, "tp", up), lax.ppermute(fr0, "tp", down)

time: 87.3 us -> 85.5 us (0.979)
  local copies, waits for them, and re-layouts: 2.92 us -> 0 us
  Pallas kernels: 35.5 us -> 36.8 us
    unnamed x4 -> x0, local copies, waits for them, and re-layouts: 2.92 us -> none
    pallas_call x1, Pallas kernels: 4.73 us -> 6.87 us  [body(): pl.pallas_call(local_body, grid=(1,), in_specs=[SMEM, SMEM, whole(TOK, WI...]
    all_to_all x1, waiting for transfers between devices: 8.18 us -> 6.04 us  [body(): got = lax.all_to_all(msg, 'ctx', 0, 0, tiled=True)]
    all_to_all x1, waiting for transfers between devices: 3.85 us -> 5.83 us  [body(): incoming = lax.all_to_all(prefix, 'ctx', 0, 0, tiled=True)]
    pallas_call x4, Pallas kernels: 11.3 us -> 10.4 us  [the longest x1 5.1 us: body(): pl.pallas_call(scan_in_body, in_specs=[SMEM] + [ANY] * 7, out_specs=[VMEM...]
  transfers between devices with their start and end apart: 13 -> 13, of which waited for: 7 -> 7; matrix products, arithmetic and copies ran while one was open for 0% -> 0% of each run, Pallas kernels for 38% -> 40%
where the time goes in v7:
time: 85.5 us; the launch traced here: 84.9 us
  Pallas kernels  36.8 us (43%)
  starting transfers between devices  24.2 us (28%)
  waiting for transfers between devices  23.8 us (28%)
    pallas_call x3, Pallas kernels, project(): pl.pallas_call(functools.partial(project_body, parts, count, targets), ou...  12.4 us
    all_to_all x1, starting transfers between devices, body(): got = lax.all_to_all(msg, 'ctx', 0, 0, tiled=True)  7.97 us
    pallas_call x1, Pallas kernels, body(): pl.pallas_call(local_body, grid=(1,), in_specs=[SMEM, SMEM, whole(TOK, WI...  6.87 us
    all_to_all x1, waiting for transfers between devices, body(): got = lax.all_to_all(msg, 'ctx', 0, 0, tiled=True)  6.04 us
    all_to_all x1, waiting for transfers between devices, body(): incoming = lax.all_to_all(prefix, 'ctx', 0, 0, tiled=True)  5.83 us
    pallas_call x1, Pallas kernels, body(): pl.pallas_call(scan_in_body, in_specs=[SMEM] + [ANY] * 7, out_specs=[VMEM...  5.1 us
    ppermute x1, waiting for transfers between devices, body(): lax.ppermute(above_l, 'tp', up)  4.77 us
    ppermute x1, waiting for transfers between devices, body(): lax.ppermute(below_l, 'tp', down)  3.78 us
  transfers between devices with their start and end apart: 13, of which 7 were waited for; matrix products, arithmetic and copies ran while one was open for 0% of the time, Pallas kernels for 40%

profile of v7, /device:TPU:0, one launch (start us, length us, event | category | flops | bytes accessed | tf_op | source)
XLA Modules:
  0.0 84.9 jit_solution(6615154304877374389)
XLA Ops:
  0.0 5.1 %scan_in.1 = (bf16[16,16,1152]{2,1,0:T(8,128)(2,1)}, f32[8,128]{1,0:T(8,128)S(1)}) custom-call(f32[8]{0:T(128)} %rate_ref.7, bf16[512,1024]{1,0:T(8,128)(2,1)} %x_ref.3, bf16[512,256]{1,0:T(8,128)(2,1)} %bc_ref.3, s32[8,512]{1,0:T(8,128)} %bitcast.6, f32[4,1024]{1,0:T(4,128)} %cx_ref.5, f32[1,1024]{1,0:T(1,128)} %bitcast.9, f32[4,256]{1,0:T(4,128)} %cbc_ref.3, ...), custom_call_target="tpu_custom_call" | custom-call | tf_op jit(solution)/shard_map/scan_in/pallas_call | solution.py:399
  5.1 8.0 %all-to-all-start = ((bf16[16,16,1152]{2,1,0:T(8,128)(2,1)}), bf16[16,16,1152]{2,1,0:T(8,128)(2,1)S(1)}, u32[]{:S(2)}, u32[]{:S(2)}) async-start(bf16[16,16,1152]{2,1,0:T(8,128)(2,1)} %get-tuple-element.26), calls=%async_computation | async-start | bytes 1179648 | tf_op jit(solution)/shard_map/all_to_all | solution.py:412
  13.1 6.9 %local.1 = (bf16[512,1024]{1,0:T(8,128)(2,1)}, bf16[512,1024]{1,0:T(8,128)(2,1)}, bf16[512,128]{1,0:T(8,128)(2,1)}) custom-call(f32[8]{0:T(128)} %rate_ref.7, f32[8]{0:T(128)} %skip_ref.3, bf16[512,1024]{1,0:T(8,128)(2,1)} %x_ref.3, bf16[512,1024]{1,0:T(8,128)(2,1)} %z_ref.3, s32[8,512]{1,0:T(8,128)} %bitcast.7, bf16[512,256]{1,0:T(8,128)(2,1)} %bc_ref.3, ...), custom_call_target="tpu_custom_call" | custom-call | tf_op jit(solution)/shard_map/local/pallas_call | solution.py:414
  20.0 6.0 %all-to-all-done.r_ref.got_ref = bf16[16,16,1152]{2,1,0:T(8,128)(2,1)S(1)} async-done(((bf16[16,16,1152]{2,1,0:T(8,128)(2,1)}), bf16[16,16,1152]{2,1,0:T(8,128)(2,1)S(1)}, u32[]{:S(2)}, u32[]{:S(2)}) %all-to-all-start) | async-done | bytes 589856 | tf_op jit(solution)/shard_map/all_to_all | solution.py:412
  26.0 2.2 %prefix.1.after_ref = bf16[16,8,1024]{2,1,0:T(8,128)(2,1)} custom-call(f32[8]{0:T(128)} %rate_ref.7, f32[4,1024]{1,0:T(4,128)} %cx_ref.5, f32[1,1024]{1,0:T(1,128)} %bitcast.11, bf16[16,16,1152]{2,1,0:T(8,128)(2,1)S(1)} %all-to-all-done.r_ref.got_ref, bf16[512,1024]{1,0:T(8,128)(2,1)} %get-tuple-element.28.after_ref.a1_hbm), custom_call_target="tpu_custom_call" | custom-call | tf_op jit(solution)/shard_map/prefix/pallas_call | solution.py:431
  28.2 3.5 %all-to-all-start.1 = ((bf16[16,8,1024]{2,1,0:T(8,128)(2,1)}), bf16[16,8,1024]{2,1,0:T(8,128)(2,1)S(1)}, u32[]{:S(2)}, u32[]{:S(2)}) async-start(bf16[16,8,1024]{2,1,0:T(8,128)(2,1)} %prefix.1.after_ref), calls=%async_computation.1 | async-start | bytes 524288 | tf_op jit(solution)/shard_map/all_to_all | solution.py:439
  31.7 1.6 %fetch.1 = (bf16[1024,1024]{1,0:T(8,128)(2,1)S(1)}, f32[8,128]{1,0:T(8,128)S(1)}) custom-call(s32[1]{0:T(128)} %bitcast.place_ref, bf16[1024,8192]{1,0:T(8,128)(2,1)} %refs_4_.5, bf16[16,8,1024]{2,1,0:T(8,128)(2,1)} %prefix.1.after_ref), custom_call_target="tpu_custom_call" | custom-call | tf_op jit(solution)/shard_map/fetch/pallas_call | solution.py:444
  34.5 5.8 %all-to-all-done.1.q_ref = bf16[16,8,1024]{2,1,0:T(8,128)(2,1)S(1)} async-done(((bf16[16,8,1024]{2,1,0:T(8,128)(2,1)}), bf16[16,8,1024]{2,1,0:T(8,128)(2,1)S(1)}, u32[]{:S(2)}, u32[]{:S(2)}) %all-to-all-start.1) | async-done | bytes 262176 | tf_op jit(solution)/shard_map/all_to_all | solution.py:439
  40.4 2.0 %norm.2 = (bf16[256,1024]{1,0:T(8,128)(2,1)S(1)}, bf16[1024,1024]{1,0:T(8,128)(2,1)S(1)}) custom-call(s32[1]{0:T(128)} %bitcast.place_ref, bf16[16,8,1024]{2,1,0:T(8,128)(2,1)S(1)} %all-to-all-done.1.q_ref, bf16[512,1024]{1,0:T(8,128)(2,1)} %get-tuple-element.28.after_ref.a1_hbm, bf16[512,1024]{1,0:T(8,128)(2,1)} %get-tuple-element.29.a2_hbm, ...), custom_call_target="tpu_custom_call" | custom-call | tf_op jit(solution)/shard_map/norm/pallas_call | solution.py:485
  42.5 1.7 %norm.3.refs_1_.own_ref = bf16[256,1024]{1,0:T(8,128)(2,1)S(1)} custom-call(s32[1]{0:T(128)} %bitcast.place_ref, bf16[16,8,1024]{2,1,0:T(8,128)(2,1)S(1)} %all-to-all-done.1.q_ref, bf16[512,1024]{1,0:T(8,128)(2,1)} %get-tuple-element.28.after_ref.a1_hbm, bf16[512,1024]{1,0:T(8,128)(2,1)} %get-tuple-element.29.a2_hbm, ...), custom_call_target="tpu_custom_call" | custom-call | tf_op jit(solution)/shard_map/norm/pallas_call | solution.py:485
  44.8 1.3 %project_far.2 = (bf16[256,512]{1,0:T(8,128)(2,1)S(1)}, bf16[256,512]{1,0:T(8,128)(2,1)S(1)}) custom-call(bf16[256,1024]{1,0:T(8,128)(2,1)S(1)} %get-tuple-element.34.refs_0_.own_ref, bf16[256,1024]{1,0:T(8,128)(2,1)S(1)} %collective-permute-done.1.refs_2_.sib_ref, bf16[1024,1024]{1,0:T(8,128)(2,1)S(1)} %get-tuple-element.39.w_ref, ...), custom_call_target="tpu_custom_call" | custom-call | tf_op jit(solution)/shard_map/project_far/pallas_call | solution.py:455
  46.1 1.6 %collective-permute-start.5 = (bf16[256,512]{1,0:T(8,128)(2,1)S(1)}, bf16[256,512]{1,0:T(8,128)(2,1)S(1)}, u32[]{:S(2)}, u32[]{:S(2)}) collective-permute-start(bf16[256,512]{1,0:T(8,128)(2,1)S(1)} %get-tuple-element.41), channel_id=1, source_target_pairs={{0,2},{1,3},{2,4},{3,5},{4,6},{5,7},{6,0},{7,1},{8,10},{9,11},{10,... | collective-permute-start | bytes 786440 | tf_op jit(solution)/shard_map/ppermute | solution.py:505
  47.7 1.7 %collective-permute-start.7 = (bf16[256,512]{1,0:T(8,128)(2,1)S(1)}, bf16[256,512]{1,0:T(8,128)(2,1)S(1)}, u32[]{:S(2)}, u32[]{:S(2)}) collective-permute-start(bf16[256,512]{1,0:T(8,128)(2,1)S(1)} %get-tuple-element.43), channel_id=1, source_target_pairs={{0,6},{1,7},{2,0},{3,1},{4,2},{5,3},{6,4},{7,5},{8,14},{9,15},{10,... | collective-permute-start | bytes 786440 | tf_op jit(solution)/shard_map/ppermute | solution.py:505
  49.4 1.3 %project_far.3 = (bf16[256,512]{1,0:T(8,128)(2,1)S(1)}, bf16[256,512]{1,0:T(8,128)(2,1)S(1)}) custom-call(bf16[256,1024]{1,0:T(8,128)(2,1)S(1)} %norm.3.refs_1_.own_ref, bf16[256,1024]{1,0:T(8,128)(2,1)S(1)} %collective-permute-done.2.refs_3_.sib_ref, bf16[1024,1024]{1,0:T(8,128)(2,1)S(1)} %get-tuple-element.39.w_ref, ...), custom_call_target="tpu_custom_call" | custom-call | tf_op jit(solution)/shard_map/project_far/pallas_call | solution.py:455
  51.1 2.9 %collective-permute-start.8 = (bf16[256,512]{1,0:T(8,128)(2,1)S(1)}, bf16[256,512]{1,0:T(8,128)(2,1)S(1)}, u32[]{:S(2)}, u32[]{:S(2)}) collective-permute-start(bf16[256,512]{1,0:T(8,128)(2,1)S(1)} %get-tuple-element.44), channel_id=1, source_target_pairs={{0,6},{1,7},{2,0},{3,1},{4,2},{5,3},{6,4},{7,5},{8,14},{9,15},{10,... | collective-permute-start | bytes 786440 | tf_op jit(solution)/shard_map/ppermute | solution.py:507
  54.0 4.1 %project.3 = (bf16[512,512]{1,0:T(8,128)(2,1)S(1)}, bf16[512,512]{1,0:T(8,128)(2,1)S(1)}) custom-call(s32[1]{0:T(128)} %bitcast.place_ref, bf16[256,1024]{1,0:T(8,128)(2,1)S(1)} %get-tuple-element.34.refs_0_.own_ref, bf16[256,1024]{1,0:T(8,128)(2,1)S(1)} %norm.3.refs_1_.own_ref, bf16[256,1024]{1,0:T(8,128)(2,1)S(1)} %collective-permute-done.1.refs_2_.sib_ref, ...), custom_call_target="tpu_custom_call" | custom-call | tf_op jit(solution)/shard_map/project/pallas_call | solution.py:374
  58.8 1.5 %collective-permute-start.4 = (bf16[512,512]{1,0:T(8,128)(2,1)S(1)}, bf16[512,512]{1,0:T(8,128)(2,1)S(1)}, u32[]{:S(2)}, u32[]{:S(2)}) collective-permute-start(bf16[512,512]{1,0:T(8,128)(2,1)S(1)} %get-tuple-element.36), channel_id=1, source_target_pairs={{0,2},{1,3},{2,4},{3,5},{4,6},{5,7},{6,0},{7,1},{8,10},{9,11},{10,... | collective-permute-start | bytes 1572872 | tf_op jit(solution)/shard_map/ppermute | solution.py:510
  61.2 1.3 %collective-permute-done.8.refs_9_ = bf16[256,512]{1,0:T(8,128)(2,1)S(1)} collective-permute-done((bf16[256,512]{1,0:T(8,128)(2,1)S(1)}, bf16[256,512]{1,0:T(8,128)(2,1)S(1)}, u32[]{:S(2)}, u32[]{:S(2)}) %collective-permute-start.8) | collective-permute-done | bytes 262176 | tf_op jit(solution)/shard_map/ppermute | solution.py:507
  62.5 4.1 %project.5 = (bf16[512,512]{1,0:T(8,128)(2,1)S(1)}, bf16[512,512]{1,0:T(8,128)(2,1)S(1)}) custom-call(s32[1]{0:T(128)} %bitcast.place_ref, bf16[256,1024]{1,0:T(8,128)(2,1)S(1)} %get-tuple-element.34.refs_0_.own_ref, bf16[256,1024]{1,0:T(8,128)(2,1)S(1)} %norm.3.refs_1_.own_ref, bf16[256,1024]{1,0:T(8,128)(2,1)S(1)} %collective-permute-done.1.refs_2_.sib_ref, ...), custom_call_target="tpu_custom_call" | custom-call | tf_op jit(solution)/shard_map/project/pallas_call | solution.py:374
  66.7 1.6 %collective-permute-start.9 = (bf16[512,512]{1,0:T(8,128)(2,1)S(1)}, bf16[512,512]{1,0:T(8,128)(2,1)S(1)}, u32[]{:S(2)}, u32[]{:S(2)}) collective-permute-start(bf16[512,512]{1,0:T(8,128)(2,1)S(1)} %get-tuple-element.45), channel_id=1, source_target_pairs={{0,2},{1,3},{2,4},{3,5},{4,6},{5,7},{6,0},{7,1},{8,10},{9,11},{10,... | collective-permute-start | bytes 1572872 | tf_op jit(solution)/shard_map/ppermute | solution.py:512
  68.3 1.7 %collective-permute-start.10 = (bf16[512,512]{1,0:T(8,128)(2,1)S(1)}, bf16[512,512]{1,0:T(8,128)(2,1)S(1)}, u32[]{:S(2)}, u32[]{:S(2)}) collective-permute-start(bf16[512,512]{1,0:T(8,128)(2,1)S(1)} %get-tuple-element.46), channel_id=1, source_target_pairs={{0,6},{1,7},{2,0},{3,1},{4,2},{5,3},{6,4},{7,5},{8,14},{9,15},{10,... | collective-permute-start | bytes 1572872 | tf_op jit(solution)/shard_map/ppermute | solution.py:512
  70.0 3.8 %collective-permute-done.3.refs_6_ = bf16[512,512]{1,0:T(8,128)(2,1)S(1)} collective-permute-done((bf16[512,512]{1,0:T(8,128)(2,1)S(1)}, bf16[512,512]{1,0:T(8,128)(2,1)S(1)}, u32[]{:S(2)}, u32[]{:S(2)}) %collective-permute-start.3) | collective-permute-done | bytes 524320 | tf_op jit(solution)/shard_map/ppermute | solution.py:510
  74.8 4.1 %project.4 = (f32[512,512]{1,0:T(8,128)S(1)}, f32[512,512]{1,0:T(8,128)S(1)}) custom-call(s32[1]{0:T(128)} %bitcast.place_ref, bf16[256,1024]{1,0:T(8,128)(2,1)S(1)} %get-tuple-element.34.refs_0_.own_ref, bf16[256,1024]{1,0:T(8,128)(2,1)S(1)} %norm.3.refs_1_.own_ref, bf16[256,1024]{1,0:T(8,128)(2,1)S(1)} %collective-permute-done.1.refs_2_.sib_ref, ...), custom_call_target="tpu_custom_call" | custom-call | tf_op jit(solution)/shard_map/project/pallas_call | solution.py:374
  79.0 4.8 %collective-permute-done.9.a_ref = bf16[512,512]{1,0:T(8,128)(2,1)S(1)} collective-permute-done((bf16[512,512]{1,0:T(8,128)(2,1)S(1)}, bf16[512,512]{1,0:T(8,128)(2,1)S(1)}, u32[]{:S(2)}, u32[]{:S(2)}) %collective-permute-start.9) | collective-permute-done | bytes 524320 | tf_op jit(solution)/shard_map/ppermute | solution.py:512
  (15 shorter events, 6.1 us)
Async XLA Ops:
  0.0 40.4 %collective-permute-start = (bf16[1024,8192]{1,0:T(8,128)(2,1)}, bf16[1024,8192]{1,0:T(8,128)(2,1)}, u32[]{:S(2)}, u32[]{:S(2)}) collective-permute-start(bf16[1024,8192]{1,0:T(8,128)(2,1)} %refs_4_.5), channel_id=1, source_target_pairs={{0,1},{1,0},{2,3},{3,2},{4,5},{5,4},{6,7},{7,6},{8,9},{9,8},{10,11... | collective-permute-start | bytes 50331656 | tf_op jit(solution)/shard_map/ppermute | solution.py:396
  5.1 20.9 %all-to-all-start = ((bf16[16,16,1152]{2,1,0:T(8,128)(2,1)}), bf16[16,16,1152]{2,1,0:T(8,128)(2,1)S(1)}, u32[]{:S(2)}, u32[]{:S(2)}) async-start(bf16[16,16,1152]{2,1,0:T(8,128)(2,1)} %get-tuple-element.26), calls=%async_computation | async-start | bytes 1179648 | tf_op jit(solution)/shard_map/all_to_all | solution.py:412
  28.2 12.2 %all-to-all-start.1 = ((bf16[16,8,1024]{2,1,0:T(8,128)(2,1)}), bf16[16,8,1024]{2,1,0:T(8,128)(2,1)S(1)}, u32[]{:S(2)}, u32[]{:S(2)}) async-start(bf16[16,8,1024]{2,1,0:T(8,128)(2,1)} %prefix.1.after_ref), calls=%async_computation.1 | async-start | bytes 524288 | tf_op jit(solution)/shard_map/all_to_all | solution.py:439
  42.4 2.4 %collective-permute-start.1 = (bf16[256,1024]{1,0:T(8,128)(2,1)S(1)}, bf16[256,1024]{1,0:T(8,128)(2,1)S(1)}, u32[]{:S(2)}, u32[]{:S(2)}) collective-permute-start(bf16[256,1024]{1,0:T(8,128)(2,1)S(1)} %get-tuple-element.34.refs_0_.own_ref), channel_id=1, source_target_pairs={{0,1},{1,0},{2,3},{3,2},{4,5},{5,4},{6,7},{7,6},{8,9},{9,8},{10,11... | collective-permute-start | bytes 1572872 | tf_op jit(solution)/shard_map/ppermute | solution.py:501
  44.2 5.2 %collective-permute-start.2 = (bf16[256,1024]{1,0:T(8,128)(2,1)S(1)}, bf16[256,1024]{1,0:T(8,128)(2,1)S(1)}, u32[]{:S(2)}, u32[]{:S(2)}) collective-permute-start(bf16[256,1024]{1,0:T(8,128)(2,1)S(1)} %norm.3.refs_1_.own_ref), channel_id=1, source_target_pairs={{0,1},{1,0},{2,3},{3,2},{4,5},{5,4},{6,7},{7,6},{8,9},{9,8},{10,11... | collective-permute-start | bytes 1572872 | tf_op jit(solution)/shard_map/ppermute | solution.py:503
  46.1 12.7 %collective-permute-start.5 = (bf16[256,512]{1,0:T(8,128)(2,1)S(1)}, bf16[256,512]{1,0:T(8,128)(2,1)S(1)}, u32[]{:S(2)}, u32[]{:S(2)}) collective-permute-start(bf16[256,512]{1,0:T(8,128)(2,1)S(1)} %get-tuple-element.41), channel_id=1, source_target_pairs={{0,2},{1,3},{2,4},{3,5},{4,6},{5,7},{6,0},{7,1},{8,10},{9,11},{10,... | collective-permute-start | bytes 786440 | tf_op jit(solution)/shard_map/ppermute | solution.py:505
  47.7 12.5 %collective-permute-start.7 = (bf16[256,512]{1,0:T(8,128)(2,1)S(1)}, bf16[256,512]{1,0:T(8,128)(2,1)S(1)}, u32[]{:S(2)}, u32[]{:S(2)}) collective-permute-start(bf16[256,512]{1,0:T(8,128)(2,1)S(1)} %get-tuple-element.43), channel_id=1, source_target_pairs={{0,6},{1,7},{2,0},{3,1},{4,2},{5,3},{6,4},{7,5},{8,14},{9,15},{10,... | collective-permute-start | bytes 786440 | tf_op jit(solution)/shard_map/ppermute | solution.py:505
  50.7 10.6 %collective-permute-start.6 = (bf16[256,512]{1,0:T(8,128)(2,1)S(1)}, bf16[256,512]{1,0:T(8,128)(2,1)S(1)}, u32[]{:S(2)}, u32[]{:S(2)}) collective-permute-start(bf16[256,512]{1,0:T(8,128)(2,1)S(1)} %get-tuple-element.42), channel_id=1, source_target_pairs={{0,2},{1,3},{2,4},{3,5},{4,6},{5,7},{6,0},{7,1},{8,10},{9,11},{10,... | collective-permute-start | bytes 786440 | tf_op jit(solution)/shard_map/ppermute | solution.py:507
  51.1 11.5 %collective-permute-start.8 = (bf16[256,512]{1,0:T(8,128)(2,1)S(1)}, bf16[256,512]{1,0:T(8,128)(2,1)S(1)}, u32[]{:S(2)}, u32[]{:S(2)}) collective-permute-start(bf16[256,512]{1,0:T(8,128)(2,1)S(1)} %get-tuple-element.44), channel_id=1, source_target_pairs={{0,6},{1,7},{2,0},{3,1},{4,2},{5,3},{6,4},{7,5},{8,14},{9,15},{10,... | collective-permute-start | bytes 786440 | tf_op jit(solution)/shard_map/ppermute | solution.py:507
  58.1 15.6 %collective-permute-start.3 = (bf16[512,512]{1,0:T(8,128)(2,1)S(1)}, bf16[512,512]{1,0:T(8,128)(2,1)S(1)}, u32[]{:S(2)}, u32[]{:S(2)}) collective-permute-start(bf16[512,512]{1,0:T(8,128)(2,1)S(1)} %get-tuple-element.35), channel_id=1, source_target_pairs={{0,6},{1,7},{2,0},{3,1},{4,2},{5,3},{6,4},{7,5},{8,14},{9,15},{10,... | collective-permute-start | bytes 1572872 | tf_op jit(solution)/shard_map/ppermute | solution.py:510
  58.8 16.1 %collective-permute-start.4 = (bf16[512,512]{1,0:T(8,128)(2,1)S(1)}, bf16[512,512]{1,0:T(8,128)(2,1)S(1)}, u32[]{:S(2)}, u32[]{:S(2)}) collective-permute-start(bf16[512,512]{1,0:T(8,128)(2,1)S(1)} %get-tuple-element.36), channel_id=1, source_target_pairs={{0,2},{1,3},{2,4},{3,5},{4,6},{5,7},{6,0},{7,1},{8,10},{9,11},{10,... | collective-permute-start | bytes 1572872 | tf_op jit(solution)/shard_map/ppermute | solution.py:510
  66.7 17.1 %collective-permute-start.9 = (bf16[512,512]{1,0:T(8,128)(2,1)S(1)}, bf16[512,512]{1,0:T(8,128)(2,1)S(1)}, u32[]{:S(2)}, u32[]{:S(2)}) collective-permute-start(bf16[512,512]{1,0:T(8,128)(2,1)S(1)} %get-tuple-element.45), channel_id=1, source_target_pairs={{0,2},{1,3},{2,4},{3,5},{4,6},{5,7},{6,0},{7,1},{8,10},{9,11},{10,... | collective-permute-start | bytes 1572872 | tf_op jit(solution)/shard_map/ppermute | solution.py:512
  68.3 15.4 %collective-permute-start.10 = (bf16[512,512]{1,0:T(8,128)(2,1)S(1)}, bf16[512,512]{1,0:T(8,128)(2,1)S(1)}, u32[]{:S(2)}, u32[]{:S(2)}) collective-permute-start(bf16[512,512]{1,0:T(8,128)(2,1)S(1)} %get-tuple-element.46), channel_id=1, source_target_pairs={{0,6},{1,7},{2,0},{3,1},{4,2},{5,3},{6,4},{7,5},{8,14},{9,15},{10,... | collective-permute-start | bytes 1572872 | tf_op jit(solution)/shard_map/ppermute | solution.py:512

commit v8 on v7

--- a/solution.py
+++ b/solution.py
@@ -13,7 +13,6 @@
 HT = TOK // 2
 BT = 128
 EDGE = 3
-MSG = 1152
 WID = 1024
 HALF = WID // 2
 HEADS = 8
@@ -131,55 +130,70 @@
     bc_row = jnp.concatenate(bc_rows + [jnp.zeros((1, WID - EDGE * 2 * ST), F32)], axis=1)
     rows = jnp.where(row < EDGE, last, jnp.where(row < 2 * EDGE, head, 0.0))
     rows = jnp.where(row == 2 * EDGE, jnp.broadcast_to(bc_row, (8, WID)), rows)
-    row = row_ids(8, HW)
     total = cum[TOK - 1 : TOK, :]
     high = jnp.floor(total * (1.0 / 256.0))
-    low = total - 256.0 * high
-    heads = jnp.where(row < 5, pltpu.roll(cum[0:8, :], 2, 0), 0.0)
-    heads = jnp.where(row == 0, high, jnp.where(row == 1, low, heads))
-    heads = pltpu.roll(heads, HW // 2, 1)
-    pad = jnp.zeros((HW - 8, HW), F32)
+    spare = jnp.zeros((1, HW), F32)
+    heads = [high, total - 256.0 * high] + [cum[k : k + 1, :] for k in range(EDGE)] + [spare]
+    heads = jnp.broadcast_to(jnp.concatenate([spare, spare] + heads, axis=1), (8, WID))
+    rows = jnp.where(row == 7, heads, rows)
     none = jnp.zeros((8, ST), F32)
     b_last = conv_part(jnp.concatenate([bc_last[:, :ST], none], axis=0), cbc_ref, none[0:1], 0, ST)
     b_head = conv_part(jnp.concatenate([none, bc_head[:, :ST]], axis=0), cbc_ref, bbc_ref[:, :ST], 0, ST)
-    b_last = jnp.concatenate([b_last, pad], axis=0).T
-    b_head = jnp.concatenate([b_head, pad], axis=0).T
+    row = row_ids(8, HW)
+    group = lax.broadcasted_iota(jnp.int32, (8, HW), 1) // 8
+
+    def stepped(b):
+        return jnp.where(row == 1, pltpu.roll(b, 8, 1), jnp.where(row == 2, pltpu.roll(b, 16, 1), b))
+
+    def slot(b, j):
+        mine = pltpu.roll(b, (HW - 8 * j) % HW, 1) if j else b
+        mine = jnp.where((row == group) & (row < EDGE), mine, 0.0)
+        return jnp.sum(mine, axis=0, keepdims=True)
+
+    b_last, b_head = stepped(b_last), stepped(b_head)
     for j in range(CTX):
-        at = slice(8 * j, 8 * j + 8)
-        msg_ref[j, :, 0:WID] = jnp.concatenate([state[at, :], rows], axis=0).astype(BF)
-        side = jnp.concatenate([b_last[at, :] + heads, b_head[at, :]], axis=0)
-        msg_ref[j, :, WID:MSG] = side.astype(BF)
+        pair = jnp.broadcast_to(jnp.concatenate([slot(b_last, j), slot(b_head, j)], axis=1), (8, 2 * HW))
+        front = jnp.where(row_ids(8, 2 * HW) == 7, pair, rows[:, : 2 * HW])
+        tail = jnp.concatenate([front, rows[:, 2 * HW :]], axis=1)
+        msg_ref[j] = jnp.concatenate([state[8 * j : 8 * j + 8, :], tail], axis=0).astype(BF)
 
 
 def prefix_body(rate_ref, cx_ref, bx_ref, r_ref, after_ref, q_ref):
-    rate = head_row(rate_ref, DECAY, HW // 2)
+    rate = head_row(rate_ref, DECAY)
     state = jnp.zeros((8, WID), F32)
     before = jnp.zeros((8, WID), F32)
-    side_before = jnp.zeros((8, HW), F32)
     edge_row = row_ids(8, WID) < EDGE
+    row = row_ids(8, HW)
+    b_rows, b_before = [], jnp.zeros((1, HW), F32)
     for c in range(CTX):
-        main = r_ref[c, :, 0:WID].astype(F32)
-        side = r_ref[c, :, WID:MSG].astype(F32)
-        rows = jnp.where(edge_row, before, main[8:16, :])
-        before = main[8:16, :]
+        spare = r_ref[c, 8:16, 0 : 2 * HW].astype(F32)[7:8, :]
+        b_rows.append(b_before + spare[:, HW:])
+        b_before = spare[:, :HW]
+    b_rows = silu(jnp.concatenate(b_rows, axis=0)).astype(BF).astype(F32)
+    b_edge = jnp.concatenate([b_rows, jnp.zeros((HW - CTX, HW), F32)], axis=0).T
+    for c in range(CTX):
+        main = r_ref[c].astype(F32)
+        tail = main[8:16, :]
+        rows = jnp.where(edge_row, before, tail)
+        before = tail
         pre = bx_ref[...] + cx_ref[0:1, :] * rows
         for k in range(1, 4):
             pre = pre + cx_ref[k : k + 1, :] * pltpu.roll(rows, 8 - k, 0)
         edge = silu(pre).astype(BF).astype(F32)
-        heads = side[0:8, :]
-        grow = jnp.exp(rate * pltpu.roll(heads, 6, 0))
-        fade = jnp.exp(-rate * (256.0 * heads[0:1, :] + heads[1:2, :]))
-        b_edge = silu(side_before + side[8:16, :]).astype(BF).astype(F32)
-        side_before = heads
+        heads = [tail[7:8, k * HW : (k + 1) * HW] for k in range(2, 4 + EDGE)]
+        grow = jnp.where(row == 0, heads[2], jnp.where(row == 1, heads[3], heads[4]))
+        grow = jnp.exp(rate * grow)
+        fade = jnp.exp(-rate * (256.0 * heads[0] + heads[1]))
         parts = []
         for h in range(HEADS):
             lo, hi = h * HW, (h + 1) * HW
-            scaled = (edge[:, lo:hi] * spread(grow, HW // 2 + h)).astype(BF).astype(F32)
+            scaled = (edge[:, lo:hi] * spread(grow, h)).astype(BF).astype(F32)
             part = state[:, lo:hi]
             for k in range(EDGE):
-                part = part + spread(b_edge, k) * jnp.broadcast_to(scaled[k : k + 1, :], (8, HW))
+                b_column = spread(b_edge[8 * k : 8 * k + 8, :], c)
+                part = part + b_column * jnp.broadcast_to(scaled[k : k + 1, :], (8, HW))
             q_ref[c, :, lo:hi] = part.astype(BF)
-            parts.append(spread(fade, HW // 2 + h, 8) * (part + main[0:8, lo:hi]))
+            parts.append(spread(fade, h, 8) * (part + main[0:8, lo:hi]))
         state = jnp.concatenate(parts, axis=1)
 
 
@@ -342,9 +356,12 @@
             outs[i // 2][rows, cols] = total.astype(outs[i // 2].dtype)
 
 
-def final_body(m0_ref, m1_ref, a_ref, b_ref, o_ref):
-    o_ref[:, :HALF] = (m0_ref[...] + a_ref[...].astype(F32)).astype(BF)
-    o_ref[:, HALF:] = (m1_ref[...] + b_ref[...].astype(F32)).astype(BF)
+def final_body(side, m_ref, a_ref, *refs):
+    o_hbm, half_ref, sem = refs[-3:]
+    half_ref[...] = (m_ref[...] + a_ref[...].astype(F32)).astype(BF)
+    store = pltpu.make_async_copy(half_ref, o_hbm.at[:, side * HALF : (side + 1) * HALF], sem.at[0])
+    store.start()
+    store.wait()
 
 
 def params(dims=1, room=20):
@@ -400,7 +417,7 @@
         scan_in_body,
         in_specs=[SMEM] + [ANY] * 7,
         out_specs=[VMEM, VMEM],
-        out_shape=[SD((CTX, 16, MSG), BF), SD((8, HW), F32)],
+        out_shape=[SD((CTX, 16, WID), BF), SD((8, HW), F32)],
         scratch_shapes=[
             buf((TOK, WID), BF), buf((TOK, 2 * ST), BF), buf((HEADS, TOK), jnp.int32), buf((4, WID), F32),
             buf((1, WID), F32), buf((4, 2 * ST), F32), buf((1, 2 * ST), F32), buf((TOK, WID), BF), buf((TOK, ST), F32),
@@ -469,7 +486,7 @@
             num_scalar_prefetch=1,
             grid=(1,),
             in_specs=[
-                SMEM, SMEM, pl.BlockSpec((1, 16, MSG), lambda i, ix: (jnp.maximum(ix[0] - 1, 0), 0, 0)),
+                SMEM, SMEM, pl.BlockSpec((1, 16, WID), lambda i, ix: (jnp.maximum(ix[0] - 1, 0), 0, 0)),
                 fixed(16, WID), fixed(16, 2 * ST), fixed(16, WID), fixed(HEADS, HW), fixed(4, WID), fixed(1, WID),
                 fixed(4, 2 * ST), fixed(1, 2 * ST), ANY,
             ],
@@ -511,14 +528,20 @@
     above_l, below_r = run(((1, 0), (3, 1)), ((fl0, fl1), (fr0, fr1)), BF)
     last_l, last_r = lax.ppermute(above_l, "tp", up), lax.ppermute(below_r, "tp", down)
     here_l, here_r = run(((0, 0), (0, 1)), ((from_l,), (from_r,)), F32)
-    return pl.pallas_call(
-        final_body,
-        in_specs=[VMEM] * 4,
-        out_specs=VMEM,
-        out_shape=SD((TOK, WID), BF),
-        compiler_params=params(0),
-        name="final",
-    )(here_l, here_r, last_l, last_r)
+
+    def final(side, here, last, *carry):
+        return pl.pallas_call(
+            functools.partial(final_body, side),
+            in_specs=[VMEM, VMEM] + [ANY] * len(carry),
+            out_specs=ANY,
+            out_shape=SD((TOK, WID), BF),
+            scratch_shapes=[buf((TOK, HALF), BF), pltpu.SemaphoreType.DMA((1,))],
+            input_output_aliases={2: 0} if carry else {},
+            compiler_params=params(0, 4),
+            name="final",
+        )(here, last, *carry)
+
+    return final(1, here_r, last_r, final(0, here_l, last_l))
 
 
 def solution(mesh):

time: 85.5 us -> 85.6 us (level)
    pallas_call x1 -> x2, Pallas kernels: 1.14 us -> 1.78 us  [final(): pl.pallas_call(functools.partial(final_body, side), in_specs=[VMEM, VMEM]...]
  transfers between devices with their start and end apart: 13 -> 13, of which waited for: 7 -> 7; matrix products, arithmetic and copies ran while one was open for 0% -> 0% of each run, Pallas kernels for 40% -> 41%
where the time goes in v8:
time: 85.6 us; the launch traced here: 85 us
  Pallas kernels  37.4 us (44%)
  starting transfers between devices  24.2 us (28%)
  waiting for transfers between devices  23.1 us (27%)
    pallas_call x3, Pallas kernels, project(): pl.pallas_call(functools.partial(project_body, parts, count, targets), ou...  12.4 us
    all_to_all x1, starting transfers between devices, body(): got = lax.all_to_all(msg, 'ctx', 0, 0, tiled=True)  7.97 us
    pallas_call x1, Pallas kernels, body(): pl.pallas_call(local_body, grid=(1,), in_specs=[SMEM, SMEM, whole(TOK, WI...  6.86 us
    all_to_all x1, waiting for transfers between devices, body(): incoming = lax.all_to_all(prefix, 'ctx', 0, 0, tiled=True)  5.83 us
    all_to_all x1, waiting for transfers between devices, body(): got = lax.all_to_all(msg, 'ctx', 0, 0, tiled=True)  5.34 us
    pallas_call x1, Pallas kernels, body(): pl.pallas_call(scan_in_body, in_specs=[SMEM] + [ANY] * 7, out_specs=[VMEM...  5.07 us
    ppermute x1, waiting for transfers between devices, body(): lax.ppermute(above_l, 'tp', up)  4.77 us
    ppermute x1, waiting for transfers between devices, body(): lax.ppermute(below_l, 'tp', down)  3.78 us
  transfers between devices with their start and end apart: 13, of which 7 were waited for; matrix products, arithmetic and copies ran while one was open for 0% of the time, Pallas kernels for 41%

profile of v8, /device:TPU:0, one launch (start us, length us, event | category | flops | bytes accessed | tf_op | source)
XLA Modules:
  0.0 85.0 jit_solution(941337268242830107)
XLA Ops:
  0.0 5.1 %scan_in.1 = (bf16[16,16,1024]{2,1,0:T(8,128)(2,1)}, f32[8,128]{1,0:T(8,128)S(1)}) custom-call(f32[8]{0:T(128)} %rate_ref.7, bf16[512,1024]{1,0:T(8,128)(2,1)} %x_ref.3, bf16[512,256]{1,0:T(8,128)(2,1)} %bc_ref.3, s32[8,512]{1,0:T(8,128)} %bitcast.6, f32[4,1024]{1,0:T(4,128)} %cx_ref.5, f32[1,1024]{1,0:T(1,128)} %bitcast.9, f32[4,256]{1,0:T(4,128)} %cbc_ref.3, ...), custom_call_target="tpu_custom_call" | custom-call | tf_op jit(solution)/shard_map/scan_in/pallas_call | solution.py:416
  5.1 8.0 %all-to-all-start = ((bf16[16,16,1024]{2,1,0:T(8,128)(2,1)}), bf16[16,16,1024]{2,1,0:T(8,128)(2,1)S(1)}, u32[]{:S(2)}, u32[]{:S(2)}) async-start(bf16[16,16,1024]{2,1,0:T(8,128)(2,1)} %get-tuple-element.26), calls=%async_computation | async-start | bytes 1048576 | tf_op jit(solution)/shard_map/all_to_all | solution.py:429
  13.1 6.9 %local.1 = (bf16[512,1024]{1,0:T(8,128)(2,1)}, bf16[512,1024]{1,0:T(8,128)(2,1)}, bf16[512,128]{1,0:T(8,128)(2,1)}) custom-call(f32[8]{0:T(128)} %rate_ref.7, f32[8]{0:T(128)} %skip_ref.3, bf16[512,1024]{1,0:T(8,128)(2,1)} %x_ref.3, bf16[512,1024]{1,0:T(8,128)(2,1)} %z_ref.3, s32[8,512]{1,0:T(8,128)} %bitcast.7, bf16[512,256]{1,0:T(8,128)(2,1)} %bc_ref.3, ...), custom_call_target="tpu_custom_call" | custom-call | tf_op jit(solution)/shard_map/local/pallas_call | solution.py:431
  19.9 5.3 %all-to-all-done.r_ref.got_ref = bf16[16,16,1024]{2,1,0:T(8,128)(2,1)S(1)} async-done(((bf16[16,16,1024]{2,1,0:T(8,128)(2,1)}), bf16[16,16,1024]{2,1,0:T(8,128)(2,1)S(1)}, u32[]{:S(2)}, u32[]{:S(2)}) %all-to-all-start) | async-done | bytes 524320 | tf_op jit(solution)/shard_map/all_to_all | solution.py:429
  25.3 2.2 %prefix.1.after_ref = bf16[16,8,1024]{2,1,0:T(8,128)(2,1)} custom-call(f32[8]{0:T(128)} %rate_ref.7, f32[4,1024]{1,0:T(4,128)} %cx_ref.5, f32[1,1024]{1,0:T(1,128)} %bitcast.11, bf16[16,16,1024]{2,1,0:T(8,128)(2,1)S(1)} %all-to-all-done.r_ref.got_ref, bf16[512,1024]{1,0:T(8,128)(2,1)} %get-tuple-element.28.after_ref.a1_hbm), custom_call_target="tpu_custom_call" | custom-call | tf_op jit(solution)/shard_map/prefix/pallas_call | solution.py:448
  27.5 3.5 %all-to-all-start.1 = ((bf16[16,8,1024]{2,1,0:T(8,128)(2,1)}), bf16[16,8,1024]{2,1,0:T(8,128)(2,1)S(1)}, u32[]{:S(2)}, u32[]{:S(2)}) async-start(bf16[16,8,1024]{2,1,0:T(8,128)(2,1)} %prefix.1.after_ref), calls=%async_computation.1 | async-start | bytes 524288 | tf_op jit(solution)/shard_map/all_to_all | solution.py:456
  31.0 1.6 %fetch.1 = (bf16[1024,1024]{1,0:T(8,128)(2,1)S(1)}, f32[8,128]{1,0:T(8,128)S(1)}) custom-call(s32[1]{0:T(128)} %bitcast.place_ref, bf16[1024,8192]{1,0:T(8,128)(2,1)} %refs_4_.5, bf16[16,8,1024]{2,1,0:T(8,128)(2,1)} %prefix.1.after_ref), custom_call_target="tpu_custom_call" | custom-call | tf_op jit(solution)/shard_map/fetch/pallas_call | solution.py:461
  33.8 5.8 %all-to-all-done.1.q_ref = bf16[16,8,1024]{2,1,0:T(8,128)(2,1)S(1)} async-done(((bf16[16,8,1024]{2,1,0:T(8,128)(2,1)}), bf16[16,8,1024]{2,1,0:T(8,128)(2,1)S(1)}, u32[]{:S(2)}, u32[]{:S(2)}) %all-to-all-start.1) | async-done | bytes 262176 | tf_op jit(solution)/shard_map/all_to_all | solution.py:456
  39.7 2.0 %norm.2 = (bf16[256,1024]{1,0:T(8,128)(2,1)S(1)}, bf16[1024,1024]{1,0:T(8,128)(2,1)S(1)}) custom-call(s32[1]{0:T(128)} %bitcast.place_ref, bf16[16,8,1024]{2,1,0:T(8,128)(2,1)S(1)} %all-to-all-done.1.q_ref, bf16[512,1024]{1,0:T(8,128)(2,1)} %get-tuple-element.28.after_ref.a1_hbm, bf16[512,1024]{1,0:T(8,128)(2,1)} %get-tuple-element.29.a2_hbm, ...), custom_call_target="tpu_custom_call" | custom-call | tf_op jit(solution)/shard_map/norm/pallas_call | solution.py:502
  41.8 1.7 %norm.3.refs_1_.own_ref = bf16[256,1024]{1,0:T(8,128)(2,1)S(1)} custom-call(s32[1]{0:T(128)} %bitcast.place_ref, bf16[16,8,1024]{2,1,0:T(8,128)(2,1)S(1)} %all-to-all-done.1.q_ref, bf16[512,1024]{1,0:T(8,128)(2,1)} %get-tuple-element.28.after_ref.a1_hbm, bf16[512,1024]{1,0:T(8,128)(2,1)} %get-tuple-element.29.a2_hbm, ...), custom_call_target="tpu_custom_call" | custom-call | tf_op jit(solution)/shard_map/norm/pallas_call | solution.py:502
  44.1 1.3 %project_far.2 = (bf16[256,512]{1,0:T(8,128)(2,1)S(1)}, bf16[256,512]{1,0:T(8,128)(2,1)S(1)}) custom-call(bf16[256,1024]{1,0:T(8,128)(2,1)S(1)} %get-tuple-element.34.refs_0_.own_ref, bf16[256,1024]{1,0:T(8,128)(2,1)S(1)} %collective-permute-done.1.refs_2_.sib_ref, bf16[1024,1024]{1,0:T(8,128)(2,1)S(1)} %get-tuple-element.38.w_ref, ...), custom_call_target="tpu_custom_call" | custom-call | tf_op jit(solution)/shard_map/project_far/pallas_call | solution.py:472
  45.4 1.6 %collective-permute-start.5 = (bf16[256,512]{1,0:T(8,128)(2,1)S(1)}, bf16[256,512]{1,0:T(8,128)(2,1)S(1)}, u32[]{:S(2)}, u32[]{:S(2)}) collective-permute-start(bf16[256,512]{1,0:T(8,128)(2,1)S(1)} %get-tuple-element.40), channel_id=1, source_target_pairs={{0,2},{1,3},{2,4},{3,5},{4,6},{5,7},{6,0},{7,1},{8,10},{9,11},{10,... | collective-permute-start | bytes 786440 | tf_op jit(solution)/shard_map/ppermute | solution.py:522
  47.0 1.7 %collective-permute-start.7 = (bf16[256,512]{1,0:T(8,128)(2,1)S(1)}, bf16[256,512]{1,0:T(8,128)(2,1)S(1)}, u32[]{:S(2)}, u32[]{:S(2)}) collective-permute-start(bf16[256,512]{1,0:T(8,128)(2,1)S(1)} %get-tuple-element.42), channel_id=1, source_target_pairs={{0,6},{1,7},{2,0},{3,1},{4,2},{5,3},{6,4},{7,5},{8,14},{9,15},{10,... | collective-permute-start | bytes 786440 | tf_op jit(solution)/shard_map/ppermute | solution.py:522
  48.7 1.3 %project_far.3 = (bf16[256,512]{1,0:T(8,128)(2,1)S(1)}, bf16[256,512]{1,0:T(8,128)(2,1)S(1)}) custom-call(bf16[256,1024]{1,0:T(8,128)(2,1)S(1)} %norm.3.refs_1_.own_ref, bf16[256,1024]{1,0:T(8,128)(2,1)S(1)} %collective-permute-done.2.refs_3_.sib_ref, bf16[1024,1024]{1,0:T(8,128)(2,1)S(1)} %get-tuple-element.38.w_ref, ...), custom_call_target="tpu_custom_call" | custom-call | tf_op jit(solution)/shard_map/project_far/pallas_call | solution.py:472
  50.4 2.9 %collective-permute-start.8 = (bf16[256,512]{1,0:T(8,128)(2,1)S(1)}, bf16[256,512]{1,0:T(8,128)(2,1)S(1)}, u32[]{:S(2)}, u32[]{:S(2)}) collective-permute-start(bf16[256,512]{1,0:T(8,128)(2,1)S(1)} %get-tuple-element.43), channel_id=1, source_target_pairs={{0,6},{1,7},{2,0},{3,1},{4,2},{5,3},{6,4},{7,5},{8,14},{9,15},{10,... | collective-permute-start | bytes 786440 | tf_op jit(solution)/shard_map/ppermute | solution.py:524
  53.3 4.1 %project.3 = (bf16[512,512]{1,0:T(8,128)(2,1)S(1)}, bf16[512,512]{1,0:T(8,128)(2,1)S(1)}) custom-call(s32[1]{0:T(128)} %bitcast.place_ref, bf16[256,1024]{1,0:T(8,128)(2,1)S(1)} %get-tuple-element.34.refs_0_.own_ref, bf16[256,1024]{1,0:T(8,128)(2,1)S(1)} %norm.3.refs_1_.own_ref, bf16[256,1024]{1,0:T(8,128)(2,1)S(1)} %collective-permute-done.1.refs_2_.sib_ref, ...), custom_call_target="tpu_custom_call" | custom-call | tf_op jit(solution)/shard_map/project/pallas_call | solution.py:391
  58.0 1.5 %collective-permute-start.4 = (bf16[512,512]{1,0:T(8,128)(2,1)S(1)}, bf16[512,512]{1,0:T(8,128)(2,1)S(1)}, u32[]{:S(2)}, u32[]{:S(2)}) collective-permute-start(bf16[512,512]{1,0:T(8,128)(2,1)S(1)} %get-tuple-element.36), channel_id=1, source_target_pairs={{0,2},{1,3},{2,4},{3,5},{4,6},{5,7},{6,0},{7,1},{8,10},{9,11},{10,... | collective-permute-start | bytes 1572872 | tf_op jit(solution)/shard_map/ppermute | solution.py:527
  60.5 1.3 %collective-permute-done.8.refs_9_ = bf16[256,512]{1,0:T(8,128)(2,1)S(1)} collective-permute-done((bf16[256,512]{1,0:T(8,128)(2,1)S(1)}, bf16[256,512]{1,0:T(8,128)(2,1)S(1)}, u32[]{:S(2)}, u32[]{:S(2)}) %collective-permute-start.8) | collective-permute-done | bytes 262176 | tf_op jit(solution)/shard_map/ppermute | solution.py:524
  61.8 4.1 %project.5 = (bf16[512,512]{1,0:T(8,128)(2,1)S(1)}, bf16[512,512]{1,0:T(8,128)(2,1)S(1)}) custom-call(s32[1]{0:T(128)} %bitcast.place_ref, bf16[256,1024]{1,0:T(8,128)(2,1)S(1)} %get-tuple-element.34.refs_0_.own_ref, bf16[256,1024]{1,0:T(8,128)(2,1)S(1)} %norm.3.refs_1_.own_ref, bf16[256,1024]{1,0:T(8,128)(2,1)S(1)} %collective-permute-done.1.refs_2_.sib_ref, ...), custom_call_target="tpu_custom_call" | custom-call | tf_op jit(solution)/shard_map/project/pallas_call | solution.py:391
  66.0 1.6 %collective-permute-start.10 = (bf16[512,512]{1,0:T(8,128)(2,1)S(1)}, bf16[512,512]{1,0:T(8,128)(2,1)S(1)}, u32[]{:S(2)}, u32[]{:S(2)}) collective-permute-start(bf16[512,512]{1,0:T(8,128)(2,1)S(1)} %get-tuple-element.46), channel_id=1, source_target_pairs={{0,2},{1,3},{2,4},{3,5},{4,6},{5,7},{6,0},{7,1},{8,10},{9,11},{10,... | collective-permute-start | bytes 1572872 | tf_op jit(solution)/shard_map/ppermute | solution.py:529
  67.6 1.7 %collective-permute-start.9 = (bf16[512,512]{1,0:T(8,128)(2,1)S(1)}, bf16[512,512]{1,0:T(8,128)(2,1)S(1)}, u32[]{:S(2)}, u32[]{:S(2)}) collective-permute-start(bf16[512,512]{1,0:T(8,128)(2,1)S(1)} %get-tuple-element.44), channel_id=1, source_target_pairs={{0,6},{1,7},{2,0},{3,1},{4,2},{5,3},{6,4},{7,5},{8,14},{9,15},{10,... | collective-permute-start | bytes 1572872 | tf_op jit(solution)/shard_map/ppermute | solution.py:529
  69.3 3.8 %collective-permute-done.3.refs_6_ = bf16[512,512]{1,0:T(8,128)(2,1)S(1)} collective-permute-done((bf16[512,512]{1,0:T(8,128)(2,1)S(1)}, bf16[512,512]{1,0:T(8,128)(2,1)S(1)}, u32[]{:S(2)}, u32[]{:S(2)}) %collective-permute-start.3) | collective-permute-done | bytes 524320 | tf_op jit(solution)/shard_map/ppermute | solution.py:527
  74.1 4.1 %project.4 = (f32[512,512]{1,0:T(8,128)S(1)}, f32[512,512]{1,0:T(8,128)S(1)}) custom-call(s32[1]{0:T(128)} %bitcast.place_ref, bf16[256,1024]{1,0:T(8,128)(2,1)S(1)} %get-tuple-element.34.refs_0_.own_ref, bf16[256,1024]{1,0:T(8,128)(2,1)S(1)} %norm.3.refs_1_.own_ref, bf16[256,1024]{1,0:T(8,128)(2,1)S(1)} %collective-permute-done.1.refs_2_.sib_ref, ...), custom_call_target="tpu_custom_call" | custom-call | tf_op jit(solution)/shard_map/project/pallas_call | solution.py:391
  78.3 4.8 %collective-permute-done.10.a_ref = bf16[512,512]{1,0:T(8,128)(2,1)S(1)} collective-permute-done((bf16[512,512]{1,0:T(8,128)(2,1)S(1)}, bf16[512,512]{1,0:T(8,128)(2,1)S(1)}, u32[]{:S(2)}, u32[]{:S(2)}) %collective-permute-start.10) | collective-permute-done | bytes 524320 | tf_op jit(solution)/shard_map/ppermute | solution.py:529
  (16 shorter events, 6.8 us)
Async XLA Ops:
  0.0 39.7 %collective-permute-start = (bf16[1024,8192]{1,0:T(8,128)(2,1)}, bf16[1024,8192]{1,0:T(8,128)(2,1)}, u32[]{:S(2)}, u32[]{:S(2)}) collective-permute-start(bf16[1024,8192]{1,0:T(8,128)(2,1)} %refs_4_.5), channel_id=1, source_target_pairs={{0,1},{1,0},{2,3},{3,2},{4,5},{5,4},{6,7},{7,6},{8,9},{9,8},{10,11... | collective-permute-start | bytes 50331656 | tf_op jit(solution)/shard_map/ppermute | solution.py:413
  5.1 20.2 %all-to-all-start = ((bf16[16,16,1024]{2,1,0:T(8,128)(2,1)}), bf16[16,16,1024]{2,1,0:T(8,128)(2,1)S(1)}, u32[]{:S(2)}, u32[]{:S(2)}) async-start(bf16[16,16,1024]{2,1,0:T(8,128)(2,1)} %get-tuple-element.26), calls=%async_computation | async-start | bytes 1048576 | tf_op jit(solution)/shard_map/all_to_all | solution.py:429
  27.5 12.2 %all-to-all-start.1 = ((bf16[16,8,1024]{2,1,0:T(8,128)(2,1)}), bf16[16,8,1024]{2,1,0:T(8,128)(2,1)S(1)}, u32[]{:S(2)}, u32[]{:S(2)}) async-start(bf16[16,8,1024]{2,1,0:T(8,128)(2,1)} %prefix.1.after_ref), calls=%async_computation.1 | async-start | bytes 524288 | tf_op jit(solution)/shard_map/all_to_all | solution.py:456
  41.7 2.4 %collective-permute-start.1 = (bf16[256,1024]{1,0:T(8,128)(2,1)S(1)}, bf16[256,1024]{1,0:T(8,128)(2,1)S(1)}, u32[]{:S(2)}, u32[]{:S(2)}) collective-permute-start(bf16[256,1024]{1,0:T(8,128)(2,1)S(1)} %get-tuple-element.34.refs_0_.own_ref), channel_id=1, source_target_pairs={{0,1},{1,0},{2,3},{3,2},{4,5},{5,4},{6,7},{7,6},{8,9},{9,8},{10,11... | collective-permute-start | bytes 1572872 | tf_op jit(solution)/shard_map/ppermute | solution.py:518
  43.5 5.2 %collective-permute-start.2 = (bf16[256,1024]{1,0:T(8,128)(2,1)S(1)}, bf16[256,1024]{1,0:T(8,128)(2,1)S(1)}, u32[]{:S(2)}, u32[]{:S(2)}) collective-permute-start(bf16[256,1024]{1,0:T(8,128)(2,1)S(1)} %norm.3.refs_1_.own_ref), channel_id=1, source_target_pairs={{0,1},{1,0},{2,3},{3,2},{4,5},{5,4},{6,7},{7,6},{8,9},{9,8},{10,11... | collective-permute-start | bytes 1572872 | tf_op jit(solution)/shard_map/ppermute | solution.py:520
  45.4 12.7 %collective-permute-start.5 = (bf16[256,512]{1,0:T(8,128)(2,1)S(1)}, bf16[256,512]{1,0:T(8,128)(2,1)S(1)}, u32[]{:S(2)}, u32[]{:S(2)}) collective-permute-start(bf16[256,512]{1,0:T(8,128)(2,1)S(1)} %get-tuple-element.40), channel_id=1, source_target_pairs={{0,2},{1,3},{2,4},{3,5},{4,6},{5,7},{6,0},{7,1},{8,10},{9,11},{10,... | collective-permute-start | bytes 786440 | tf_op jit(solution)/shard_map/ppermute | solution.py:522
  47.0 12.5 %collective-permute-start.7 = (bf16[256,512]{1,0:T(8,128)(2,1)S(1)}, bf16[256,512]{1,0:T(8,128)(2,1)S(1)}, u32[]{:S(2)}, u32[]{:S(2)}) collective-permute-start(bf16[256,512]{1,0:T(8,128)(2,1)S(1)} %get-tuple-element.42), channel_id=1, source_target_pairs={{0,6},{1,7},{2,0},{3,1},{4,2},{5,3},{6,4},{7,5},{8,14},{9,15},{10,... | collective-permute-start | bytes 786440 | tf_op jit(solution)/shard_map/ppermute | solution.py:522
  50.0 10.6 %collective-permute-start.6 = (bf16[256,512]{1,0:T(8,128)(2,1)S(1)}, bf16[256,512]{1,0:T(8,128)(2,1)S(1)}, u32[]{:S(2)}, u32[]{:S(2)}) collective-permute-start(bf16[256,512]{1,0:T(8,128)(2,1)S(1)} %get-tuple-element.41), channel_id=1, source_target_pairs={{0,2},{1,3},{2,4},{3,5},{4,6},{5,7},{6,0},{7,1},{8,10},{9,11},{10,... | collective-permute-start | bytes 786440 | tf_op jit(solution)/shard_map/ppermute | solution.py:524
  50.4 11.5 %collective-permute-start.8 = (bf16[256,512]{1,0:T(8,128)(2,1)S(1)}, bf16[256,512]{1,0:T(8,128)(2,1)S(1)}, u32[]{:S(2)}, u32[]{:S(2)}) collective-permute-start(bf16[256,512]{1,0:T(8,128)(2,1)S(1)} %get-tuple-element.43), channel_id=1, source_target_pairs={{0,6},{1,7},{2,0},{3,1},{4,2},{5,3},{6,4},{7,5},{8,14},{9,15},{10,... | collective-permute-start | bytes 786440 | tf_op jit(solution)/shard_map/ppermute | solution.py:524
  57.4 15.6 %collective-permute-start.3 = (bf16[512,512]{1,0:T(8,128)(2,1)S(1)}, bf16[512,512]{1,0:T(8,128)(2,1)S(1)}, u32[]{:S(2)}, u32[]{:S(2)}) collective-permute-start(bf16[512,512]{1,0:T(8,128)(2,1)S(1)} %get-tuple-element.35), channel_id=1, source_target_pairs={{0,6},{1,7},{2,0},{3,1},{4,2},{5,3},{6,4},{7,5},{8,14},{9,15},{10,... | collective-permute-start | bytes 1572872 | tf_op jit(solution)/shard_map/ppermute | solution.py:527
  58.0 16.1 %collective-permute-start.4 = (bf16[512,512]{1,0:T(8,128)(2,1)S(1)}, bf16[512,512]{1,0:T(8,128)(2,1)S(1)}, u32[]{:S(2)}, u32[]{:S(2)}) collective-permute-start(bf16[512,512]{1,0:T(8,128)(2,1)S(1)} %get-tuple-element.36), channel_id=1, source_target_pairs={{0,2},{1,3},{2,4},{3,5},{4,6},{5,7},{6,0},{7,1},{8,10},{9,11},{10,... | collective-permute-start | bytes 1572872 | tf_op jit(solution)/shard_map/ppermute | solution.py:527
  66.0 17.1 %collective-permute-start.10 = (bf16[512,512]{1,0:T(8,128)(2,1)S(1)}, bf16[512,512]{1,0:T(8,128)(2,1)S(1)}, u32[]{:S(2)}, u32[]{:S(2)}) collective-permute-start(bf16[512,512]{1,0:T(8,128)(2,1)S(1)} %get-tuple-element.46), channel_id=1, source_target_pairs={{0,2},{1,3},{2,4},{3,5},{4,6},{5,7},{6,0},{7,1},{8,10},{9,11},{10,... | collective-permute-start | bytes 1572872 | tf_op jit(solution)/shard_map/ppermute | solution.py:529
  67.6 16.3 %collective-permute-start.9 = (bf16[512,512]{1,0:T(8,128)(2,1)S(1)}, bf16[512,512]{1,0:T(8,128)(2,1)S(1)}, u32[]{:S(2)}, u32[]{:S(2)}) collective-permute-start(bf16[512,512]{1,0:T(8,128)(2,1)S(1)} %get-tuple-element.44), channel_id=1, source_target_pairs={{0,6},{1,7},{2,0},{3,1},{4,2},{5,3},{6,4},{7,5},{8,14},{9,15},{10,... | collective-permute-start | bytes 1572872 | tf_op jit(solution)/shard_map/ppermute | solution.py:529

commit v9 on v8

--- a/solution.py
+++ b/solution.py
@@ -22,7 +22,7 @@
 SEQ = TOK * CTX
 DECAY = 12.288 / SEQ / 63.0
 SCALE = 1.0 / (ST * SEQ) ** 0.5
-ROWS = 64
+ROWS = 32
 SD = jax.ShapeDtypeStruct
 
 

time: 85.6 us -> 85.5 us (level)
  no operation moved by 1% of the time
where the time goes in v9:
time: 85.5 us; the launch traced here: 85 us
  Pallas kernels  37.4 us (44%)
  starting transfers between devices  24.2 us (28%)
  waiting for transfers between devices  23.1 us (27%)
    pallas_call x3, Pallas kernels, project(): pl.pallas_call(functools.partial(project_body, parts, count, targets), ou...  12.4 us
    all_to_all x1, starting transfers between devices, body(): got = lax.all_to_all(msg, 'ctx', 0, 0, tiled=True)  7.97 us
    pallas_call x1, Pallas kernels, body(): pl.pallas_call(local_body, grid=(1,), in_specs=[SMEM, SMEM, whole(TOK, WI...  6.89 us
    all_to_all x1, waiting for transfers between devices, body(): incoming = lax.all_to_all(prefix, 'ctx', 0, 0, tiled=True)  5.83 us
    all_to_all x1, waiting for transfers between devices, body(): got = lax.all_to_all(msg, 'ctx', 0, 0, tiled=True)  5.32 us
    pallas_call x1, Pallas kernels, body(): pl.pallas_call(scan_in_body, in_specs=[SMEM] + [ANY] * 7, out_specs=[VMEM...  5.06 us
    ppermute x1, waiting for transfers between devices, body(): lax.ppermute(above_l, 'tp', up)  4.77 us
    ppermute x1, waiting for transfers between devices, body(): lax.ppermute(below_l, 'tp', down)  3.77 us
  transfers between devices with their start and end apart: 13, of which 7 were waited for; matrix products, arithmetic and copies ran while one was open for 0% of the time, Pallas kernels for 41%

profile of v9, /device:TPU:0, one launch (start us, length us, event | category | flops | bytes accessed | tf_op | source)
XLA Modules:
  0.0 85.0 jit_solution(12376431711510325695)
XLA Ops:
  0.0 5.1 %scan_in.1 = (bf16[16,16,1024]{2,1,0:T(8,128)(2,1)}, f32[8,128]{1,0:T(8,128)S(1)}) custom-call(f32[8]{0:T(128)} %rate_ref.7, bf16[512,1024]{1,0:T(8,128)(2,1)} %x_ref.3, bf16[512,256]{1,0:T(8,128)(2,1)} %bc_ref.3, s32[8,512]{1,0:T(8,128)} %bitcast.6, f32[4,1024]{1,0:T(4,128)} %cx_ref.5, f32[1,1024]{1,0:T(1,128)} %bitcast.9, f32[4,256]{1,0:T(4,128)} %cbc_ref.3, ...), custom_call_target="tpu_custom_call" | custom-call | tf_op jit(solution)/shard_map/scan_in/pallas_call | solution.py:416
  5.1 8.0 %all-to-all-start = ((bf16[16,16,1024]{2,1,0:T(8,128)(2,1)}), bf16[16,16,1024]{2,1,0:T(8,128)(2,1)S(1)}, u32[]{:S(2)}, u32[]{:S(2)}) async-start(bf16[16,16,1024]{2,1,0:T(8,128)(2,1)} %get-tuple-element.26), calls=%async_computation | async-start | bytes 1048576 | tf_op jit(solution)/shard_map/all_to_all | solution.py:429
  13.1 6.9 %local.1 = (bf16[512,1024]{1,0:T(8,128)(2,1)}, bf16[512,1024]{1,0:T(8,128)(2,1)}, bf16[512,128]{1,0:T(8,128)(2,1)}) custom-call(f32[8]{0:T(128)} %rate_ref.7, f32[8]{0:T(128)} %skip_ref.3, bf16[512,1024]{1,0:T(8,128)(2,1)} %x_ref.3, bf16[512,1024]{1,0:T(8,128)(2,1)} %z_ref.3, s32[8,512]{1,0:T(8,128)} %bitcast.7, bf16[512,256]{1,0:T(8,128)(2,1)} %bc_ref.3, ...), custom_call_target="tpu_custom_call" | custom-call | tf_op jit(solution)/shard_map/local/pallas_call | solution.py:431
  19.9 5.3 %all-to-all-done.r_ref.got_ref = bf16[16,16,1024]{2,1,0:T(8,128)(2,1)S(1)} async-done(((bf16[16,16,1024]{2,1,0:T(8,128)(2,1)}), bf16[16,16,1024]{2,1,0:T(8,128)(2,1)S(1)}, u32[]{:S(2)}, u32[]{:S(2)}) %all-to-all-start) | async-done | bytes 524320 | tf_op jit(solution)/shard_map/all_to_all | solution.py:429
  25.3 2.2 %prefix.1.after_ref = bf16[16,8,1024]{2,1,0:T(8,128)(2,1)} custom-call(f32[8]{0:T(128)} %rate_ref.7, f32[4,1024]{1,0:T(4,128)} %cx_ref.5, f32[1,1024]{1,0:T(1,128)} %bitcast.11, bf16[16,16,1024]{2,1,0:T(8,128)(2,1)S(1)} %all-to-all-done.r_ref.got_ref, bf16[512,1024]{1,0:T(8,128)(2,1)} %get-tuple-element.28.after_ref.a1_hbm), custom_call_target="tpu_custom_call" | custom-call | tf_op jit(solution)/shard_map/prefix/pallas_call | solution.py:448
  27.5 3.5 %all-to-all-start.1 = ((bf16[16,8,1024]{2,1,0:T(8,128)(2,1)}), bf16[16,8,1024]{2,1,0:T(8,128)(2,1)S(1)}, u32[]{:S(2)}, u32[]{:S(2)}) async-start(bf16[16,8,1024]{2,1,0:T(8,128)(2,1)} %prefix.1.after_ref), calls=%async_computation.1 | async-start | bytes 524288 | tf_op jit(solution)/shard_map/all_to_all | solution.py:456
  31.0 1.6 %fetch.1 = (bf16[1024,1024]{1,0:T(8,128)(2,1)S(1)}, f32[8,128]{1,0:T(8,128)S(1)}) custom-call(s32[1]{0:T(128)} %bitcast.place_ref, bf16[1024,8192]{1,0:T(8,128)(2,1)} %refs_4_.5, bf16[16,8,1024]{2,1,0:T(8,128)(2,1)} %prefix.1.after_ref), custom_call_target="tpu_custom_call" | custom-call | tf_op jit(solution)/shard_map/fetch/pallas_call | solution.py:461
  33.8 5.8 %all-to-all-done.1.q_ref = bf16[16,8,1024]{2,1,0:T(8,128)(2,1)S(1)} async-done(((bf16[16,8,1024]{2,1,0:T(8,128)(2,1)}), bf16[16,8,1024]{2,1,0:T(8,128)(2,1)S(1)}, u32[]{:S(2)}, u32[]{:S(2)}) %all-to-all-start.1) | async-done | bytes 262176 | tf_op jit(solution)/shard_map/all_to_all | solution.py:456
  39.7 2.0 %norm.2 = (bf16[256,1024]{1,0:T(8,128)(2,1)S(1)}, bf16[1024,1024]{1,0:T(8,128)(2,1)S(1)}) custom-call(s32[1]{0:T(128)} %bitcast.place_ref, bf16[16,8,1024]{2,1,0:T(8,128)(2,1)S(1)} %all-to-all-done.1.q_ref, bf16[512,1024]{1,0:T(8,128)(2,1)} %get-tuple-element.28.after_ref.a1_hbm, bf16[512,1024]{1,0:T(8,128)(2,1)} %get-tuple-element.29.a2_hbm, ...), custom_call_target="tpu_custom_call" | custom-call | tf_op jit(solution)/shard_map/norm/pallas_call | solution.py:502
  41.8 1.7 %norm.3.refs_1_.own_ref = bf16[256,1024]{1,0:T(8,128)(2,1)S(1)} custom-call(s32[1]{0:T(128)} %bitcast.place_ref, bf16[16,8,1024]{2,1,0:T(8,128)(2,1)S(1)} %all-to-all-done.1.q_ref, bf16[512,1024]{1,0:T(8,128)(2,1)} %get-tuple-element.28.after_ref.a1_hbm, bf16[512,1024]{1,0:T(8,128)(2,1)} %get-tuple-element.29.a2_hbm, ...), custom_call_target="tpu_custom_call" | custom-call | tf_op jit(solution)/shard_map/norm/pallas_call | solution.py:502
  44.1 1.3 %project_far.2 = (bf16[256,512]{1,0:T(8,128)(2,1)S(1)}, bf16[256,512]{1,0:T(8,128)(2,1)S(1)}) custom-call(bf16[256,1024]{1,0:T(8,128)(2,1)S(1)} %get-tuple-element.34.refs_0_.own_ref, bf16[256,1024]{1,0:T(8,128)(2,1)S(1)} %collective-permute-done.1.refs_2_.sib_ref, bf16[1024,1024]{1,0:T(8,128)(2,1)S(1)} %get-tuple-element.38.w_ref, ...), custom_call_target="tpu_custom_call" | custom-call | tf_op jit(solution)/shard_map/project_far/pallas_call | solution.py:472
  45.3 1.6 %collective-permute-start.5 = (bf16[256,512]{1,0:T(8,128)(2,1)S(1)}, bf16[256,512]{1,0:T(8,128)(2,1)S(1)}, u32[]{:S(2)}, u32[]{:S(2)}) collective-permute-start(bf16[256,512]{1,0:T(8,128)(2,1)S(1)} %get-tuple-element.40), channel_id=1, source_target_pairs={{0,2},{1,3},{2,4},{3,5},{4,6},{5,7},{6,0},{7,1},{8,10},{9,11},{10,... | collective-permute-start | bytes 786440 | tf_op jit(solution)/shard_map/ppermute | solution.py:522
  47.0 1.7 %collective-permute-start.7 = (bf16[256,512]{1,0:T(8,128)(2,1)S(1)}, bf16[256,512]{1,0:T(8,128)(2,1)S(1)}, u32[]{:S(2)}, u32[]{:S(2)}) collective-permute-start(bf16[256,512]{1,0:T(8,128)(2,1)S(1)} %get-tuple-element.42), channel_id=1, source_target_pairs={{0,6},{1,7},{2,0},{3,1},{4,2},{5,3},{6,4},{7,5},{8,14},{9,15},{10,... | collective-permute-start | bytes 786440 | tf_op jit(solution)/shard_map/ppermute | solution.py:522
  48.7 1.3 %project_far.3 = (bf16[256,512]{1,0:T(8,128)(2,1)S(1)}, bf16[256,512]{1,0:T(8,128)(2,1)S(1)}) custom-call(bf16[256,1024]{1,0:T(8,128)(2,1)S(1)} %norm.3.refs_1_.own_ref, bf16[256,1024]{1,0:T(8,128)(2,1)S(1)} %collective-permute-done.2.refs_3_.sib_ref, bf16[1024,1024]{1,0:T(8,128)(2,1)S(1)} %get-tuple-element.38.w_ref, ...), custom_call_target="tpu_custom_call" | custom-call | tf_op jit(solution)/shard_map/project_far/pallas_call | solution.py:472
  50.4 2.9 %collective-permute-start.8 = (bf16[256,512]{1,0:T(8,128)(2,1)S(1)}, bf16[256,512]{1,0:T(8,128)(2,1)S(1)}, u32[]{:S(2)}, u32[]{:S(2)}) collective-permute-start(bf16[256,512]{1,0:T(8,128)(2,1)S(1)} %get-tuple-element.43), channel_id=1, source_target_pairs={{0,6},{1,7},{2,0},{3,1},{4,2},{5,3},{6,4},{7,5},{8,14},{9,15},{10,... | collective-permute-start | bytes 786440 | tf_op jit(solution)/shard_map/ppermute | solution.py:524
  53.3 4.1 %project.3 = (bf16[512,512]{1,0:T(8,128)(2,1)S(1)}, bf16[512,512]{1,0:T(8,128)(2,1)S(1)}) custom-call(s32[1]{0:T(128)} %bitcast.place_ref, bf16[256,1024]{1,0:T(8,128)(2,1)S(1)} %get-tuple-element.34.refs_0_.own_ref, bf16[256,1024]{1,0:T(8,128)(2,1)S(1)} %norm.3.refs_1_.own_ref, bf16[256,1024]{1,0:T(8,128)(2,1)S(1)} %collective-permute-done.1.refs_2_.sib_ref, ...), custom_call_target="tpu_custom_call" | custom-call | tf_op jit(solution)/shard_map/project/pallas_call | solution.py:391
  58.0 1.5 %collective-permute-start.4 = (bf16[512,512]{1,0:T(8,128)(2,1)S(1)}, bf16[512,512]{1,0:T(8,128)(2,1)S(1)}, u32[]{:S(2)}, u32[]{:S(2)}) collective-permute-start(bf16[512,512]{1,0:T(8,128)(2,1)S(1)} %get-tuple-element.36), channel_id=1, source_target_pairs={{0,2},{1,3},{2,4},{3,5},{4,6},{5,7},{6,0},{7,1},{8,10},{9,11},{10,... | collective-permute-start | bytes 1572872 | tf_op jit(solution)/shard_map/ppermute | solution.py:527
  60.5 1.3 %collective-permute-done.8.refs_9_ = bf16[256,512]{1,0:T(8,128)(2,1)S(1)} collective-permute-done((bf16[256,512]{1,0:T(8,128)(2,1)S(1)}, bf16[256,512]{1,0:T(8,128)(2,1)S(1)}, u32[]{:S(2)}, u32[]{:S(2)}) %collective-permute-start.8) | collective-permute-done | bytes 262176 | tf_op jit(solution)/shard_map/ppermute | solution.py:524
  61.8 4.1 %project.5 = (bf16[512,512]{1,0:T(8,128)(2,1)S(1)}, bf16[512,512]{1,0:T(8,128)(2,1)S(1)}) custom-call(s32[1]{0:T(128)} %bitcast.place_ref, bf16[256,1024]{1,0:T(8,128)(2,1)S(1)} %get-tuple-element.34.refs_0_.own_ref, bf16[256,1024]{1,0:T(8,128)(2,1)S(1)} %norm.3.refs_1_.own_ref, bf16[256,1024]{1,0:T(8,128)(2,1)S(1)} %collective-permute-done.1.refs_2_.sib_ref, ...), custom_call_target="tpu_custom_call" | custom-call | tf_op jit(solution)/shard_map/project/pallas_call | solution.py:391
  66.0 1.6 %collective-permute-start.10 = (bf16[512,512]{1,0:T(8,128)(2,1)S(1)}, bf16[512,512]{1,0:T(8,128)(2,1)S(1)}, u32[]{:S(2)}, u32[]{:S(2)}) collective-permute-start(bf16[512,512]{1,0:T(8,128)(2,1)S(1)} %get-tuple-element.46), channel_id=1, source_target_pairs={{0,2},{1,3},{2,4},{3,5},{4,6},{5,7},{6,0},{7,1},{8,10},{9,11},{10,... | collective-permute-start | bytes 1572872 | tf_op jit(solution)/shard_map/ppermute | solution.py:529
  67.6 1.7 %collective-permute-start.9 = (bf16[512,512]{1,0:T(8,128)(2,1)S(1)}, bf16[512,512]{1,0:T(8,128)(2,1)S(1)}, u32[]{:S(2)}, u32[]{:S(2)}) collective-permute-start(bf16[512,512]{1,0:T(8,128)(2,1)S(1)} %get-tuple-element.44), channel_id=1, source_target_pairs={{0,6},{1,7},{2,0},{3,1},{4,2},{5,3},{6,4},{7,5},{8,14},{9,15},{10,... | collective-permute-start | bytes 1572872 | tf_op jit(solution)/shard_map/ppermute | solution.py:529
  69.3 3.8 %collective-permute-done.3.refs_6_ = bf16[512,512]{1,0:T(8,128)(2,1)S(1)} collective-permute-done((bf16[512,512]{1,0:T(8,128)(2,1)S(1)}, bf16[512,512]{1,0:T(8,128)(2,1)S(1)}, u32[]{:S(2)}, u32[]{:S(2)}) %collective-permute-start.3) | collective-permute-done | bytes 524320 | tf_op jit(solution)/shard_map/ppermute | solution.py:527
  74.1 4.1 %project.4 = (f32[512,512]{1,0:T(8,128)S(1)}, f32[512,512]{1,0:T(8,128)S(1)}) custom-call(s32[1]{0:T(128)} %bitcast.place_ref, bf16[256,1024]{1,0:T(8,128)(2,1)S(1)} %get-tuple-element.34.refs_0_.own_ref, bf16[256,1024]{1,0:T(8,128)(2,1)S(1)} %norm.3.refs_1_.own_ref, bf16[256,1024]{1,0:T(8,128)(2,1)S(1)} %collective-permute-done.1.refs_2_.sib_ref, ...), custom_call_target="tpu_custom_call" | custom-call | tf_op jit(solution)/shard_map/project/pallas_call | solution.py:391
  78.3 4.8 %collective-permute-done.10.a_ref = bf16[512,512]{1,0:T(8,128)(2,1)S(1)} collective-permute-done((bf16[512,512]{1,0:T(8,128)(2,1)S(1)}, bf16[512,512]{1,0:T(8,128)(2,1)S(1)}, u32[]{:S(2)}, u32[]{:S(2)}) %collective-permute-start.10) | collective-permute-done | bytes 524320 | tf_op jit(solution)/shard_map/ppermute | solution.py:529
  (16 shorter events, 6.8 us)
Async XLA Ops:
  0.0 39.7 %collective-permute-start = (bf16[1024,8192]{1,0:T(8,128)(2,1)}, bf16[1024,8192]{1,0:T(8,128)(2,1)}, u32[]{:S(2)}, u32[]{:S(2)}) collective-permute-start(bf16[1024,8192]{1,0:T(8,128)(2,1)} %refs_4_.5), channel_id=1, source_target_pairs={{0,1},{1,0},{2,3},{3,2},{4,5},{5,4},{6,7},{7,6},{8,9},{9,8},{10,11... | collective-permute-start | bytes 50331656 | tf_op jit(solution)/shard_map/ppermute | solution.py:413
  5.1 20.2 %all-to-all-start = ((bf16[16,16,1024]{2,1,0:T(8,128)(2,1)}), bf16[16,16,1024]{2,1,0:T(8,128)(2,1)S(1)}, u32[]{:S(2)}, u32[]{:S(2)}) async-start(bf16[16,16,1024]{2,1,0:T(8,128)(2,1)} %get-tuple-element.26), calls=%async_computation | async-start | bytes 1048576 | tf_op jit(solution)/shard_map/all_to_all | solution.py:429
  27.5 12.2 %all-to-all-start.1 = ((bf16[16,8,1024]{2,1,0:T(8,128)(2,1)}), bf16[16,8,1024]{2,1,0:T(8,128)(2,1)S(1)}, u32[]{:S(2)}, u32[]{:S(2)}) async-start(bf16[16,8,1024]{2,1,0:T(8,128)(2,1)} %prefix.1.after_ref), calls=%async_computation.1 | async-start | bytes 524288 | tf_op jit(solution)/shard_map/all_to_all | solution.py:456
  41.7 2.4 %collective-permute-start.1 = (bf16[256,1024]{1,0:T(8,128)(2,1)S(1)}, bf16[256,1024]{1,0:T(8,128)(2,1)S(1)}, u32[]{:S(2)}, u32[]{:S(2)}) collective-permute-start(bf16[256,1024]{1,0:T(8,128)(2,1)S(1)} %get-tuple-element.34.refs_0_.own_ref), channel_id=1, source_target_pairs={{0,1},{1,0},{2,3},{3,2},{4,5},{5,4},{6,7},{7,6},{8,9},{9,8},{10,11... | collective-permute-start | bytes 1572872 | tf_op jit(solution)/shard_map/ppermute | solution.py:518
  43.5 5.2 %collective-permute-start.2 = (bf16[256,1024]{1,0:T(8,128)(2,1)S(1)}, bf16[256,1024]{1,0:T(8,128)(2,1)S(1)}, u32[]{:S(2)}, u32[]{:S(2)}) collective-permute-start(bf16[256,1024]{1,0:T(8,128)(2,1)S(1)} %norm.3.refs_1_.own_ref), channel_id=1, source_target_pairs={{0,1},{1,0},{2,3},{3,2},{4,5},{5,4},{6,7},{7,6},{8,9},{9,8},{10,11... | collective-permute-start | bytes 1572872 | tf_op jit(solution)/shard_map/ppermute | solution.py:520
  45.3 12.7 %collective-permute-start.5 = (bf16[256,512]{1,0:T(8,128)(2,1)S(1)}, bf16[256,512]{1,0:T(8,128)(2,1)S(1)}, u32[]{:S(2)}, u32[]{:S(2)}) collective-permute-start(bf16[256,512]{1,0:T(8,128)(2,1)S(1)} %get-tuple-element.40), channel_id=1, source_target_pairs={{0,2},{1,3},{2,4},{3,5},{4,6},{5,7},{6,0},{7,1},{8,10},{9,11},{10,... | collective-permute-start | bytes 786440 | tf_op jit(solution)/shard_map/ppermute | solution.py:522
  47.0 12.5 %collective-permute-start.7 = (bf16[256,512]{1,0:T(8,128)(2,1)S(1)}, bf16[256,512]{1,0:T(8,128)(2,1)S(1)}, u32[]{:S(2)}, u32[]{:S(2)}) collective-permute-start(bf16[256,512]{1,0:T(8,128)(2,1)S(1)} %get-tuple-element.42), channel_id=1, source_target_pairs={{0,6},{1,7},{2,0},{3,1},{4,2},{5,3},{6,4},{7,5},{8,14},{9,15},{10,... | collective-permute-start | bytes 786440 | tf_op jit(solution)/shard_map/ppermute | solution.py:522
  50.0 10.6 %collective-permute-start.6 = (bf16[256,512]{1,0:T(8,128)(2,1)S(1)}, bf16[256,512]{1,0:T(8,128)(2,1)S(1)}, u32[]{:S(2)}, u32[]{:S(2)}) collective-permute-start(bf16[256,512]{1,0:T(8,128)(2,1)S(1)} %get-tuple-element.41), channel_id=1, source_target_pairs={{0,2},{1,3},{2,4},{3,5},{4,6},{5,7},{6,0},{7,1},{8,10},{9,11},{10,... | collective-permute-start | bytes 786440 | tf_op jit(solution)/shard_map/ppermute | solution.py:524
  50.4 11.5 %collective-permute-start.8 = (bf16[256,512]{1,0:T(8,128)(2,1)S(1)}, bf16[256,512]{1,0:T(8,128)(2,1)S(1)}, u32[]{:S(2)}, u32[]{:S(2)}) collective-permute-start(bf16[256,512]{1,0:T(8,128)(2,1)S(1)} %get-tuple-element.43), channel_id=1, source_target_pairs={{0,6},{1,7},{2,0},{3,1},{4,2},{5,3},{6,4},{7,5},{8,14},{9,15},{10,... | collective-permute-start | bytes 786440 | tf_op jit(solution)/shard_map/ppermute | solution.py:524
  57.4 15.6 %collective-permute-start.3 = (bf16[512,512]{1,0:T(8,128)(2,1)S(1)}, bf16[512,512]{1,0:T(8,128)(2,1)S(1)}, u32[]{:S(2)}, u32[]{:S(2)}) collective-permute-start(bf16[512,512]{1,0:T(8,128)(2,1)S(1)} %get-tuple-element.35), channel_id=1, source_target_pairs={{0,6},{1,7},{2,0},{3,1},{4,2},{5,3},{6,4},{7,5},{8,14},{9,15},{10,... | collective-permute-start | bytes 1572872 | tf_op jit(solution)/shard_map/ppermute | solution.py:527
  58.0 16.1 %collective-permute-start.4 = (bf16[512,512]{1,0:T(8,128)(2,1)S(1)}, bf16[512,512]{1,0:T(8,128)(2,1)S(1)}, u32[]{:S(2)}, u32[]{:S(2)}) collective-permute-start(bf16[512,512]{1,0:T(8,128)(2,1)S(1)} %get-tuple-element.36), channel_id=1, source_target_pairs={{0,2},{1,3},{2,4},{3,5},{4,6},{5,7},{6,0},{7,1},{8,10},{9,11},{10,... | collective-permute-start | bytes 1572872 | tf_op jit(solution)/shard_map/ppermute | solution.py:527
  66.0 17.1 %collective-permute-start.10 = (bf16[512,512]{1,0:T(8,128)(2,1)S(1)}, bf16[512,512]{1,0:T(8,128)(2,1)S(1)}, u32[]{:S(2)}, u32[]{:S(2)}) collective-permute-start(bf16[512,512]{1,0:T(8,128)(2,1)S(1)} %get-tuple-element.46), channel_id=1, source_target_pairs={{0,2},{1,3},{2,4},{3,5},{4,6},{5,7},{6,0},{7,1},{8,10},{9,11},{10,... | collective-permute-start | bytes 1572872 | tf_op jit(solution)/shard_map/ppermute | solution.py:529
  67.6 16.3 %collective-permute-start.9 = (bf16[512,512]{1,0:T(8,128)(2,1)S(1)}, bf16[512,512]{1,0:T(8,128)(2,1)S(1)}, u32[]{:S(2)}, u32[]{:S(2)}) collective-permute-start(bf16[512,512]{1,0:T(8,128)(2,1)S(1)} %get-tuple-element.44), channel_id=1, source_target_pairs={{0,6},{1,7},{2,0},{3,1},{4,2},{5,3},{6,4},{7,5},{8,14},{9,15},{10,... | collective-permute-start | bytes 1572872 | tf_op jit(solution)/shard_map/ppermute | solution.py:529
